TPU v7x, 256 devices: a whole 4x4x8 slice. The times are simulated.
256 devices in a mesh: frame: 16 (over z_hi, y, core), row: 16 (over x, z_lo).
Axes of the slice: x: 4, y: 4, z: 8 (z_hi: 2, z_lo: 4; z = z_hi * 4 + z_lo), core: 2. Of those that a mesh axis runs over, the one named last changes fastest.
Arguments:
- features: float32 [16, 64, 256, 256], P('frame', 'row'), may hold values from -6 to 6
- conv_weight: float32 [2, 3, 3, 256, 256], replicated, may hold values from -0.125 to 0.125
Outputs:
- activations: float32 [16, 64, 256, 256], P('frame', 'row')
All inputs are finite; a program needn't handle non-finite values.
Results may differ from a plain program's by a relative error of at most 0.0001.
Values sent between devices are 32-bit elements; how exact they have to be, the bound alone decides.
No kernel may reach another device: no remote copies, remote signals or barrier semaphores. Data moves between devices by JAX's collectives and lax.ppermute only.
A program may use at most 64 MiB of HBM per device.

v0:
```python
import jax
import jax.numpy as jnp
from jax import lax
from jax.sharding import PartitionSpec as P

LAYERS = 2


def passed_along(block, axis, distance):
    devices = range(lax.axis_size(axis))
    route = [(i - distance, i) for i in devices if i - distance in devices]
    return lax.ppermute(block, axis, route)


def padded_2(cells, sides, width):
    for axis, dim in sides:
        count = lax.axis_size(axis)
        ends = count - 1
        head = lax.slice_in_dim(cells, 0, width, axis=dim)
        tail = lax.slice_in_dim(cells, cells.shape[dim] - width, cells.shape[dim], axis=dim)
        cells = jnp.concatenate(
            [
                lax.ppermute(tail, axis, [(i, (i + 1) % count) for i in range(ends)]),
                cells,
                lax.ppermute(head, axis, [((i + 1) % count, i) for i in range(ends)]),
            ],
            axis=dim,
        )
    return cells


def convolve_block(padded, kernel):
    frames, rows_pad, cols, chans = padded.shape
    rows = rows_pad - 2
    widened = jnp.pad(padded, ((0, 0), (0, 0), (1, 1), (0, 0)))
    total = jnp.zeros((frames * rows * cols, kernel.shape[3]), jnp.float32)
    for tap_row in range(3):
        for tap_col in range(3):
            window = widened[:, tap_row : tap_row + rows, tap_col : tap_col + cols, :].reshape(
                frames * rows * cols, chans
            )
            total = total + jnp.dot(
                window,
                kernel[tap_row, tap_col],
                preferred_element_type=jnp.float32,
                precision=lax.Precision.HIGHEST,
            )
    return jnp.maximum(total, 0.0).reshape(frames, rows, cols, kernel.shape[3])


def shift_layer(field, kernel):
    fold = field.shape[3] // 8
    incoming_next = passed_along(field[:1, :, :, :fold], "frame", -1)
    incoming_prev = passed_along(field[-1:, :, :, fold : 2 * fold], "frame", 1)
    from_next = jnp.concatenate([field[1:, :, :, :fold], incoming_next], axis=0)
    from_prev = jnp.concatenate([incoming_prev, field[:-1, :, :, fold : 2 * fold]], axis=0)
    shifted = jnp.concatenate([from_next, from_prev, field[:, :, :, 2 * fold :]], axis=3)
    padded = padded_2(shifted, (("row", 1),), 1)
    return convolve_block(padded, kernel)


def local(features, conv_weight):
    field = features
    for layer in range(LAYERS):
        field = shift_layer(field, conv_weight[layer])
    return field


def solution(mesh):
    placed = (P("frame", "row", None, None), P())
    return jax.shard_map(
        local, mesh=mesh, in_specs=placed, out_specs=P("frame", "row", None, None), check_vma=False
    )
```

profile of v0, /device:TPU:224, one launch (start us, length us, event | category | flops | bytes accessed | tf_op | source)
XLA Modules:
  0.0 111.1 jit_solution(2338507898418259538)
XLA Ops:
  0.0 1.5 %fusion.30 = (f32[1,4,256,32]{3,2,1,0:T(8,128)S(1)}, f32[1,4,256,32]{3,2,1,0:T(8,128)S(1)}) fusion(f32[1,4,256,256]{3,2,1,0:T(8,128)} %param.2), kind=kLoop, calls=%fused_computation.76 | loop fusion | bytes 524288 | tf_op jit(solution)/shard_map/slice | solution.py:53
  1.5 5.2 %collective-permute-start = (f32[1,4,256,32]{3,2,1,0:T(8,128)S(1)}, f32[1,4,256,32]{3,2,1,0:T(8,128)S(1)}, u32[]{:S(2)}, u32[]{:S(2)}) collective-permute-start(f32[1,4,256,32]{3,2,1,0:T(8,128)S(1)} %get-tuple-element.29), channel_id=1, source_target_pairs={{16,0},{32,16},{48,32},{64,48},{80,64},{96,80},{112,96},{128,112},... | collective-permute-start | bytes 393224 | tf_op jit(solution)/shard_map/ppermute | solution.py:12
  6.7 0.0 copy-start
  6.7 2.1 %collective-permute-start.1 = (f32[1,4,256,32]{3,2,1,0:T(8,128)S(1)}, f32[1,4,256,32]{3,2,1,0:T(8,128)S(1)}, u32[]{:S(2)}, u32[]{:S(2)}) collective-permute-start(f32[1,4,256,32]{3,2,1,0:T(8,128)S(1)} %get-tuple-element.30), channel_id=1, source_target_pairs={{0,16},{16,32},{32,48},{48,64},{64,80},{80,96},{96,112},{112,128},... | collective-permute-start | bytes 393224 | tf_op jit(solution)/shard_map/ppermute | solution.py:12
  8.8 2.8 %slice_bitcast_fusion = (f32[3,3,256,256]{3,2,1,0:T(8,128)S(1)}, f32[3,3,256,256]{3,2,1,0:T(8,128)S(1)}) fusion(f32[2,3,3,256,256]{4,3,2,1,0:T(8,128)} %param.3), kind=kLoop, calls=%fused_computation.2 | loop fusion | bytes 9437184 | tf_op jit(solution)/shard_map/squeeze | solution.py:65
  11.6 0.0 copy-done
  11.6 0.3 slice.152
  12.0 1.4 %collective-permute-done = f32[1,4,256,32]{3,2,1,0:T(8,128)S(1)} collective-permute-done((f32[1,4,256,32]{3,2,1,0:T(8,128)S(1)}, f32[1,4,256,32]{3,2,1,0:T(8,128)S(1)}, u32[]{:S(2)}, u32[]{:S(2)}) %collective-permute-start) | collective-permute-done | bytes 131104 | tf_op jit(solution)/shard_map/ppermute | solution.py:12
  13.4 11.1 %collective-permute-done.1 = f32[1,4,256,32]{3,2,1,0:T(8,128)S(1)} collective-permute-done((f32[1,4,256,32]{3,2,1,0:T(8,128)S(1)}, f32[1,4,256,32]{3,2,1,0:T(8,128)S(1)}, u32[]{:S(2)}, u32[]{:S(2)}) %collective-permute-start.1) | collective-permute-done | bytes 131104 | tf_op jit(solution)/shard_map/ppermute | solution.py:12
  24.4 0.6 pad_maximum_fusion.12
  25.1 1.9 %collective-permute-start.2 = (f32[1,1,256,256]{3,2,1,0:T(8,128)S(1)}, f32[1,1,256,256]{3,2,1,0:T(8,128)S(1)}, u32[]{:S(2)}, u32[]{:S(2)}) collective-permute-start(f32[1,1,256,256]{3,2,1,0:T(8,128)S(1)} %get-tuple-element.27), channel_id=1, source_target_pairs={{0,1},{1,2},{2,3},{3,4},{4,5},{5,6},{6,7},{7,8},{8,9},{9,10},{10,1... | collective-permute-start | bytes 786440 | tf_op jit(solution)/shard_map/ppermute | solution.py:23
  27.0 8.5 %collective-permute-start.3 = (f32[1,1,256,256]{3,2,1,0:T(8,128)S(1)}, f32[1,1,256,256]{3,2,1,0:T(8,128)S(1)}, u32[]{:S(2)}, u32[]{:S(2)}) collective-permute-start(f32[1,1,256,256]{3,2,1,0:T(8,128)S(1)} %get-tuple-element.28), channel_id=1, source_target_pairs={{1,0},{2,1},{3,2},{4,3},{5,4},{6,5},{7,6},{8,7},{9,8},{10,9},{11,1... | collective-permute-start | bytes 786440 | tf_op jit(solution)/shard_map/ppermute | solution.py:25
  35.5 1.0 fusion.20
  36.5 1.4 %collective-permute-done.2 = f32[1,1,256,256]{3,2,1,0:T(8,128)S(1)} collective-permute-done((f32[1,1,256,256]{3,2,1,0:T(8,128)S(1)}, f32[1,1,256,256]{3,2,1,0:T(8,128)S(1)}, u32[]{:S(2)}, u32[]{:S(2)}) %collective-permute-start.2) | collective-permute-done | bytes 262176 | tf_op jit(solution)/shard_map/ppermute | solution.py:23
  37.9 11.2 %collective-permute-done.3 = f32[1,1,256,256]{3,2,1,0:T(8,128)S(1)} collective-permute-done((f32[1,1,256,256]{3,2,1,0:T(8,128)S(1)}, f32[1,1,256,256]{3,2,1,0:T(8,128)S(1)}, u32[]{:S(2)}, u32[]{:S(2)}) %collective-permute-start.3) | collective-permute-done | bytes 262176 | tf_op jit(solution)/shard_map/ppermute | solution.py:25
  49.1 0.6 select_maximum_fusion.4
  49.8 0.6 fusion.26
  50.4 1.0 fusion.17
  51.4 0.9 pad_maximum_fusion.9
  52.3 1.0 fusion.18
  53.3 1.0 fusion.19
  54.3 1.0 fusion.21
  55.3 1.0 fusion.22
  56.3 1.0 fusion.23
  57.3 1.0 fusion.24
  58.3 1.4 %fusion.8 = f32[1024,256]{1,0:T(8,128)S(1)} fusion(f32[1024,256]{1,0:T(8,128)S(1)} %fusion.17, f32[1024,256]{1,0:T(8,128)S(1)} %fusion.18, f32[1024,256]{1,0:T(8,128)S(1)} %fusion.19, f32[1024,256]{1,0:T(8,128)S(1)} %bitcast.114, f32[1024,256]{1,0:T(8,128)S(1)} %fusion.20, f32[1024,256]{1,0:T(8,128)S(1)} %fusion.21, f32[1024,256]{1,0:T(8,128)S(1)} %fusion.22, ...), kind=kOutput, calls=%fused_computation.22 | convolution fusion | flops 807665664 | bytes 10747904 | tf_op jit(solution)/shard_map/dot_general | solution.py:42
  59.7 0.2 fusion.28
  59.9 1.9 %collective-permute-start.4 = (f32[1,4,256,32]{3,2,1,0:T(8,128)S(1)}, f32[1,4,256,32]{3,2,1,0:T(8,128)S(1)}, u32[]{:S(2)}, u32[]{:S(2)}) collective-permute-start(f32[1,4,256,32]{3,2,1,0:T(8,128)S(1)} %get-tuple-element.25), channel_id=1, source_target_pairs={{16,0},{32,16},{48,32},{64,48},{80,64},{96,80},{112,96},{128,112},... | collective-permute-start | bytes 393224 | tf_op jit(solution)/shard_map/ppermute | solution.py:12
  61.8 2.6 %collective-permute-start.5 = (f32[1,4,256,32]{3,2,1,0:T(8,128)S(1)}, f32[1,4,256,32]{3,2,1,0:T(8,128)S(1)}, u32[]{:S(2)}, u32[]{:S(2)}) collective-permute-start(f32[1,4,256,32]{3,2,1,0:T(8,128)S(1)} %get-tuple-element.26), channel_id=1, source_target_pairs={{0,16},{16,32},{32,48},{48,64},{64,80},{80,96},{96,112},{112,128},... | collective-permute-start | bytes 393224 | tf_op jit(solution)/shard_map/ppermute | solution.py:12
  64.4 0.3 slice.215
  64.8 3.7 %collective-permute-done.4 = f32[1,4,256,32]{3,2,1,0:T(8,128)S(1)} collective-permute-done((f32[1,4,256,32]{3,2,1,0:T(8,128)S(1)}, f32[1,4,256,32]{3,2,1,0:T(8,128)S(1)}, u32[]{:S(2)}, u32[]{:S(2)}) %collective-permute-start.4) | collective-permute-done | bytes 131104 | tf_op jit(solution)/shard_map/ppermute | solution.py:12
  68.5 11.7 %collective-permute-done.5 = f32[1,4,256,32]{3,2,1,0:T(8,128)S(1)} collective-permute-done((f32[1,4,256,32]{3,2,1,0:T(8,128)S(1)}, f32[1,4,256,32]{3,2,1,0:T(8,128)S(1)}, u32[]{:S(2)}, u32[]{:S(2)}) %collective-permute-start.5) | collective-permute-done | bytes 131104 | tf_op jit(solution)/shard_map/ppermute | solution.py:12
  80.3 0.6 pad_maximum_fusion.13
  80.9 4.1 %collective-permute-start.6 = (f32[1,1,256,256]{3,2,1,0:T(8,128)S(1)}, f32[1,1,256,256]{3,2,1,0:T(8,128)S(1)}, u32[]{:S(2)}, u32[]{:S(2)}) collective-permute-start(f32[1,1,256,256]{3,2,1,0:T(8,128)S(1)} %get-tuple-element.23), channel_id=1, source_target_pairs={{0,1},{1,2},{2,3},{3,4},{4,5},{5,6},{6,7},{7,8},{8,9},{9,10},{10,1... | collective-permute-start | bytes 786440 | tf_op jit(solution)/shard_map/ppermute | solution.py:23
  85.0 3.1 %collective-permute-start.7 = (f32[1,1,256,256]{3,2,1,0:T(8,128)S(1)}, f32[1,1,256,256]{3,2,1,0:T(8,128)S(1)}, u32[]{:S(2)}, u32[]{:S(2)}) collective-permute-start(f32[1,1,256,256]{3,2,1,0:T(8,128)S(1)} %get-tuple-element.24), channel_id=1, source_target_pairs={{1,0},{2,1},{3,2},{4,3},{5,4},{6,5},{7,6},{8,7},{9,8},{10,9},{11,1... | collective-permute-start | bytes 786440 | tf_op jit(solution)/shard_map/ppermute | solution.py:25
  88.1 1.0 fusion.12
  89.1 1.4 %collective-permute-done.6 = f32[1,1,256,256]{3,2,1,0:T(8,128)S(1)} collective-permute-done((f32[1,1,256,256]{3,2,1,0:T(8,128)S(1)}, f32[1,1,256,256]{3,2,1,0:T(8,128)S(1)}, u32[]{:S(2)}, u32[]{:S(2)}) %collective-permute-start.6) | collective-permute-done | bytes 262176 | tf_op jit(solution)/shard_map/ppermute | solution.py:23
  90.5 9.0 %collective-permute-done.7 = f32[1,1,256,256]{3,2,1,0:T(8,128)S(1)} collective-permute-done((f32[1,1,256,256]{3,2,1,0:T(8,128)S(1)}, f32[1,1,256,256]{3,2,1,0:T(8,128)S(1)}, u32[]{:S(2)}, u32[]{:S(2)}) %collective-permute-start.7) | collective-permute-done | bytes 262176 | tf_op jit(solution)/shard_map/ppermute | solution.py:25
  99.5 0.9 pad_maximum_fusion.3
  100.4 1.0 fusion.15
  101.4 1.0 fusion.10
  102.5 0.7 select_maximum_fusion
  103.1 0.6 fusion.25
  103.7 1.0 fusion.16
  104.7 1.0 fusion.11
  105.8 1.0 fusion.13
  106.8 1.0 fusion.14
  107.8 1.0 fusion.9
  108.8 2.3 %fusion.4 = f32[1024,256]{1,0:T(8,128)} fusion(f32[1024,256]{1,0:T(8,128)S(1)} %fusion.9, f32[1024,256]{1,0:T(8,128)S(1)} %fusion.10, f32[1024,256]{1,0:T(8,128)S(1)} %fusion.11, f32[1024,256]{1,0:T(8,128)S(1)} %bitcast.115, f32[1024,256]{1,0:T(8,128)S(1)} %fusion.12, f32[1024,256]{1,0:T(8,128)S(1)} %fusion.13, f32[1024,256]{1,0:T(8,128)S(1)} %fusion.14, ...), kind=kOutput, calls=%fused_computation.17 | convolution fusion | flops 807665664 | bytes 10747904 | tf_op jit(solution)/shard_map/dot_general | solution.py:42
  (2 shorter events, 0.1 us)
Async XLA Ops:
  1.5 11.9 %collective-permute-start = (f32[1,4,256,32]{3,2,1,0:T(8,128)S(1)}, f32[1,4,256,32]{3,2,1,0:T(8,128)S(1)}, u32[]{:S(2)}, u32[]{:S(2)}) collective-permute-start(f32[1,4,256,32]{3,2,1,0:T(8,128)S(1)} %get-tuple-element.29), channel_id=1, source_target_pairs={{16,0},{32,16},{48,32},{64,48},{80,64},{96,80},{112,96},{128,112},... | collective-permute-start | bytes 393224 | tf_op jit(solution)/shard_map/ppermute | solution.py:12
  6.7 4.9 %copy-start = (f32[1,4,256,256]{3,2,1,0:T(8,128)S(1)}, f32[1,4,256,256]{3,2,1,0:T(8,128)}, u32[]{:S(2)}) copy-start(f32[1,4,256,256]{3,2,1,0:T(8,128)} %param.2) | copy-start | bytes 3145732
  6.7 17.7 %collective-permute-start.1 = (f32[1,4,256,32]{3,2,1,0:T(8,128)S(1)}, f32[1,4,256,32]{3,2,1,0:T(8,128)S(1)}, u32[]{:S(2)}, u32[]{:S(2)}) collective-permute-start(f32[1,4,256,32]{3,2,1,0:T(8,128)S(1)} %get-tuple-element.30), channel_id=1, source_target_pairs={{0,16},{16,32},{32,48},{48,64},{64,80},{80,96},{96,112},{112,128},... | collective-permute-start | bytes 393224 | tf_op jit(solution)/shard_map/ppermute | solution.py:12
  25.1 12.8 %collective-permute-start.2 = (f32[1,1,256,256]{3,2,1,0:T(8,128)S(1)}, f32[1,1,256,256]{3,2,1,0:T(8,128)S(1)}, u32[]{:S(2)}, u32[]{:S(2)}) collective-permute-start(f32[1,1,256,256]{3,2,1,0:T(8,128)S(1)} %get-tuple-element.27), channel_id=1, source_target_pairs={{0,1},{1,2},{2,3},{3,4},{4,5},{5,6},{6,7},{7,8},{8,9},{9,10},{10,1... | collective-permute-start | bytes 786440 | tf_op jit(solution)/shard_map/ppermute | solution.py:23
  27.0 22.1 %collective-permute-start.3 = (f32[1,1,256,256]{3,2,1,0:T(8,128)S(1)}, f32[1,1,256,256]{3,2,1,0:T(8,128)S(1)}, u32[]{:S(2)}, u32[]{:S(2)}) collective-permute-start(f32[1,1,256,256]{3,2,1,0:T(8,128)S(1)} %get-tuple-element.28), channel_id=1, source_target_pairs={{1,0},{2,1},{3,2},{4,3},{5,4},{6,5},{7,6},{8,7},{9,8},{10,9},{11,1... | collective-permute-start | bytes 786440 | tf_op jit(solution)/shard_map/ppermute | solution.py:25
  59.9 8.6 %collective-permute-start.4 = (f32[1,4,256,32]{3,2,1,0:T(8,128)S(1)}, f32[1,4,256,32]{3,2,1,0:T(8,128)S(1)}, u32[]{:S(2)}, u32[]{:S(2)}) collective-permute-start(f32[1,4,256,32]{3,2,1,0:T(8,128)S(1)} %get-tuple-element.25), channel_id=1, source_target_pairs={{16,0},{32,16},{48,32},{64,48},{80,64},{96,80},{112,96},{128,112},... | collective-permute-start | bytes 393224 | tf_op jit(solution)/shard_map/ppermute | solution.py:12
  61.8 18.4 %collective-permute-start.5 = (f32[1,4,256,32]{3,2,1,0:T(8,128)S(1)}, f32[1,4,256,32]{3,2,1,0:T(8,128)S(1)}, u32[]{:S(2)}, u32[]{:S(2)}) collective-permute-start(f32[1,4,256,32]{3,2,1,0:T(8,128)S(1)} %get-tuple-element.26), channel_id=1, source_target_pairs={{0,16},{16,32},{32,48},{48,64},{64,80},{80,96},{96,112},{112,128},... | collective-permute-start | bytes 393224 | tf_op jit(solution)/shard_map/ppermute | solution.py:12
  80.9 9.6 %collective-permute-start.6 = (f32[1,1,256,256]{3,2,1,0:T(8,128)S(1)}, f32[1,1,256,256]{3,2,1,0:T(8,128)S(1)}, u32[]{:S(2)}, u32[]{:S(2)}) collective-permute-start(f32[1,1,256,256]{3,2,1,0:T(8,128)S(1)} %get-tuple-element.23), channel_id=1, source_target_pairs={{0,1},{1,2},{2,3},{3,4},{4,5},{5,6},{6,7},{7,8},{8,9},{9,10},{10,1... | collective-permute-start | bytes 786440 | tf_op jit(solution)/shard_map/ppermute | solution.py:23
  85.0 14.6 %collective-permute-start.7 = (f32[1,1,256,256]{3,2,1,0:T(8,128)S(1)}, f32[1,1,256,256]{3,2,1,0:T(8,128)S(1)}, u32[]{:S(2)}, u32[]{:S(2)}) collective-permute-start(f32[1,1,256,256]{3,2,1,0:T(8,128)S(1)} %get-tuple-element.24), channel_id=1, source_target_pairs={{1,0},{2,1},{3,2},{4,3},{5,4},{6,5},{7,6},{8,7},{9,8},{10,9},{11,1... | collective-permute-start | bytes 786440 | tf_op jit(solution)/shard_map/ppermute | solution.py:25
where the time goes:
time: 111 us
  waiting for transfers between devices  50.9 us (46%)
  starting transfers between devices  29.4 us (26%)
  matrix products  19.7 us (18%)
  local copies, waits for them, and re-layouts  6.46 us (6%)
  other arithmetic  4.32 us (4%)
    ppermute x4, waiting for transfers between devices, passed_along(): return lax.ppermute(block, axis, route)  27.9 us
    ppermute x2, waiting for transfers between devices, padded_2(): lax.ppermute(head, axis, [((i + 1) % count, i) for i in range(ends)])  20.2 us
    dot_general x18, matrix products, convolve_block(): jnp.dot(window, kernel[tap_row, tap_col], preferred_element_type=jnp.floa...  19.7 us
    ppermute x4, starting transfers between devices, passed_along(): return lax.ppermute(block, axis, route)  11.8 us
    ppermute x2, starting transfers between devices, padded_2(): lax.ppermute(head, axis, [((i + 1) % count, i) for i in range(ends)])  11.6 us
    ppermute x2, starting transfers between devices, padded_2(): lax.ppermute(tail, axis, [(i, (i + 1) % count) for i in range(ends)])  5.98 us
    concatenate x4, other arithmetic, padded_2(): jnp.concatenate([lax.ppermute(tail, axis, [(i, (i + 1) % count) for i in...  3.08 us
    squeeze x1, local copies, waits for them, and re-layouts, local(): field = shift_layer(field, conv_weight[layer])  2.84 us
  transfers between devices with their start and end apart: 8, of which 8 were waited for; matrix products, arithmetic and copies ran while one was open for 5% of the time, Pallas kernels for 0%

commit v1 on v0

v1 whole, which is shorter than its diff:
```python
import jax
import jax.numpy as jnp
from jax import lax
from jax.experimental import pallas as pl
from jax.experimental.pallas import tpu as pltpu
from jax.sharding import PartitionSpec as P

F32 = jnp.float32
BF16 = jnp.bfloat16
VMEM = pl.BlockSpec(memory_space=pltpu.VMEM)
PARAMS = pltpu.CompilerParams(vmem_limit_bytes=48 * 2**20)


def exchange(block, axis, odd):
    count = lax.axis_size(axis)
    pairs = [(i, i + 1) for i in range(odd, count - 1, 2)]
    return lax.ppermute(block, axis, pairs + [(b, a) for a, b in pairs])


def parts(x):
    hi = x.astype(BF16)
    return hi, (x - hi.astype(F32)).astype(BF16)


def dot(a, b):
    return jnp.dot(a, b, preferred_element_type=F32)


def dot3(ah, al, bh, bl):
    return dot(ah, bh) + (dot(al, bh) + dot(ah, bl))


def join_columns(left, mid, right):
    cols = mid.shape[0]
    at = lax.broadcasted_iota(jnp.int32, mid.shape, 0)
    left = jnp.where(at == 0, 0.0, pltpu.roll(left, 1, 0))
    right = jnp.where(at == cols - 1, 0.0, pltpu.roll(right, cols - 1, 0))
    return mid + left + right


def pack(row, first, fold):
    blocks = 128 // fold
    height = row.shape[0] // blocks
    lane = lax.broadcasted_iota(jnp.int32, (height, 128), 1) // fold
    out = jnp.zeros((height, 128), F32)
    for j in range(blocks):
        piece = pltpu.roll(row[j * height : (j + 1) * height, :128], (j * fold - first) % 128, 1)
        out = jnp.where(lane == j, piece, out)
    return out


def shifted_lanes(lanes, following, before, fold):
    blocks = 128 // fold
    height = following.shape[0]
    lane = lax.broadcasted_iota(jnp.int32, (height, 128), 1)
    pieces = []
    for j in range(blocks):
        nxt = pltpu.roll(following, (-j * fold) % 128, 1)
        prv = pltpu.roll(before, (fold - j * fold) % 128, 1)
        own = lanes[j * height : (j + 1) * height]
        pieces.append(jnp.where(lane < fold, nxt, jnp.where(lane < 2 * fold, prv, own)))
    return jnp.concatenate(pieces, axis=0)


def split_weights_kernel(w_ref, hi_ref, lo_ref):
    hi, lo = parts(w_ref[...])
    hi_ref[...] = hi
    lo_ref[...] = lo


def split_weights(weight):
    spec = pl.BlockSpec((1, 1) + weight.shape[2:], lambda l, i: (l, i, 0, 0, 0))
    return pl.pallas_call(
        split_weights_kernel,
        grid=weight.shape[:2],
        in_specs=[spec],
        out_specs=[spec, spec],
        out_shape=[jax.ShapeDtypeStruct(weight.shape, BF16)] * 2,
        name="split_weights",
    )(weight)


def by_parity(axis, even_case, odd_case):
    parity = lax.axis_index(axis) % 2
    pl.when(parity == 0)(even_case)
    pl.when(parity == 1)(odd_case)


def pack_kernel(x_ref, even_ref, odd_ref):
    fold = even_ref.shape[1] * 128 // x_ref.shape[1]

    def write(to_before, to_following):
        for r in range(x_ref.shape[0]):
            row = x_ref[r]
            to_before[r] = pack(row, 0, fold)
            to_following[r] = pack(row, fold, fold)

    by_parity("frame", lambda: write(odd_ref, even_ref), lambda: write(even_ref, odd_ref))


def pack_frames(x, fold):
    rows, cols, chans = x.shape
    packed = jax.ShapeDtypeStruct((rows, cols * fold // 128, 128), F32)
    return pl.pallas_call(
        pack_kernel,
        grid=(1,),
        in_specs=[pl.BlockSpec((rows, cols, 128), lambda i: (0, 0, 0))],
        out_specs=[pl.BlockSpec(packed.shape, lambda i: (0, 0, 0))] * 2,
        out_shape=[packed, packed],
        name="pack_frames",
        compiler_params=PARAMS,
    )(x)


def edge_rows_kernel(x_ref, feven_ref, fodd_ref, reven_ref, rodd_ref):
    rows, cols, chans = x_ref.shape
    fold = feven_ref.shape[1] * 128 // cols

    def write(following, before, first_to, last_to):
        for r, out in ((0, first_to), (rows - 1, last_to)):
            out[:, :128] = shifted_lanes(x_ref[r, :, :128], following[r], before[r], fold)
            out[:, 128:] = x_ref[r, :, 128:]

    def rows_case(first_to, last_to):
        by_parity(
            "frame",
            lambda: write(feven_ref, fodd_ref, first_to, last_to),
            lambda: write(fodd_ref, feven_ref, first_to, last_to),
        )

    by_parity("row", lambda: rows_case(rodd_ref, reven_ref), lambda: rows_case(reven_ref, rodd_ref))


def edge_rows(x, feven, fodd):
    rows, cols, chans = x.shape
    edge = jax.ShapeDtypeStruct((cols, chans), F32)
    return pl.pallas_call(
        edge_rows_kernel,
        in_specs=[VMEM] * 3,
        out_specs=[VMEM] * 2,
        out_shape=[edge, edge],
        name="edge_rows",
        compiler_params=PARAMS,
    )(x, feven, fodd)


def inner_kernel(x_ref, feven_ref, fodd_ref, wh_ref, wl_ref, out_ref, hi, lo, acc):
    rows, cols, chans = x_ref.shape
    fold = feven_ref.shape[1] * 128 // cols

    def write(following, before):
        for r in range(rows):
            lanes = shifted_lanes(x_ref[r, :, :128], following[r], before[r], fold)
            at = slice(r * cols, (r + 1) * cols)
            hi[at, :128], lo[at, :128] = parts(lanes)
            hi[at, 128:], lo[at, 128:] = parts(x_ref[r, :, 128:])

    by_parity("frame", lambda: write(feven_ref, fodd_ref), lambda: write(fodd_ref, feven_ref))
    for dx in range(3):
        for dy in (1, 0, 2):
            source = slice(max(dy - 1, 0) * cols, (rows + min(dy - 1, 0)) * cols)
            target = slice(max(1 - dy, 0) * cols, (rows + min(1 - dy, 0)) * cols)
            part = dot3(hi[source], lo[source], wh_ref[dy, dx], wl_ref[dy, dx])
            if dy == 1:
                acc[dx] = part
            else:
                acc[dx, target] += part
    for r in range(rows):
        at = slice(r * cols, (r + 1) * cols)
        total = join_columns(acc[0, at], acc[1, at], acc[2, at])
        out_ref[r] = total if r in (0, rows - 1) else jnp.maximum(total, 0.0)


def inner_rows(x, feven, fodd, wh, wl):
    rows, cols, chans = x.shape
    outs = wh.shape[-1]
    return pl.pallas_call(
        inner_kernel,
        in_specs=[VMEM] * 5,
        out_specs=VMEM,
        out_shape=jax.ShapeDtypeStruct((rows, cols, outs), F32),
        scratch_shapes=[
            pltpu.VMEM((rows * cols, chans), BF16),
            pltpu.VMEM((rows * cols, chans), BF16),
            pltpu.VMEM((3, rows * cols, outs), F32),
        ],
        name="inner_rows",
        compiler_params=PARAMS,
    )(x, feven, fodd, wh, wl)


def outer_kernel(reven_ref, rodd_ref, wh_ref, wl_ref, partial_ref, out_ref):
    step = pl.program_id(0)
    parity = lax.axis_index("row") % 2

    def finish(halo_ref):
        hi, lo = parts(halo_ref[...])
        taps = [dot3(hi, lo, wh_ref[0, dx], wl_ref[0, dx]) for dx in range(3)]
        out_ref[0] = jnp.maximum(partial_ref[0] + join_columns(*taps), 0.0)

    pl.when(step == parity)(lambda: finish(rodd_ref))
    pl.when(step != parity)(lambda: finish(reven_ref))


def outer_rows(partial, reven, rodd, wh, wl):
    rows, cols, outs = partial.shape
    row = pl.BlockSpec((1, cols, outs), lambda i: (i * (rows - 1), 0, 0))
    tap = pl.BlockSpec((1,) + wh.shape[1:], lambda i: (2 * i, 0, 0, 0))
    return pl.pallas_call(
        outer_kernel,
        grid=(2,),
        in_specs=[VMEM, VMEM, tap, tap, row],
        out_specs=row,
        out_shape=jax.ShapeDtypeStruct(partial.shape, F32),
        input_output_aliases={4: 0},
        name="outer_rows",
        compiler_params=PARAMS,
    )(reven, rodd, wh, wl, partial)


def local(features, conv_weight):
    frames, rows, cols, chans = features.shape
    field = features.reshape(rows, cols, chans)
    wh, wl = split_weights(conv_weight)
    for layer in range(conv_weight.shape[0]):
        peven, podd = pack_frames(field, chans // 8)
        feven, fodd = exchange(peven, "frame", 0), exchange(podd, "frame", 1)
        seven, sodd = edge_rows(field, feven, fodd)
        reven, rodd = exchange(seven, "row", 0), exchange(sodd, "row", 1)
        partial = inner_rows(field, feven, fodd, wh[layer], wl[layer])
        field = outer_rows(partial, reven, rodd, wh[layer], wl[layer])
    return field.reshape(features.shape)


def solution(mesh):
    placed = (P("frame", "row", None, None), P())
    return jax.shard_map(
        local, mesh=mesh, in_specs=placed, out_specs=P("frame", "row", None, None), check_vma=False
    )
```

time: 111 us -> 60.3 us (0.54)
  the two profiles are of different devices: /device:TPU:224 before, /device:TPU:27 now
where the time goes in v1:
time: 60.3 us; the launch traced here: 59.2 us
  starting transfers between devices  27.3 us (45%)
  Pallas kernels  18.8 us (31%)
  waiting for transfers between devices  8.87 us (15%)
  local copies, waits for them, and re-layouts  4.06 us (7%)
    ppermute x8, starting transfers between devices, exchange(): return lax.ppermute(block, axis, pairs + [(b, a) for a, b in pairs])  27.3 us
    ppermute x8, waiting for transfers between devices, exchange(): return lax.ppermute(block, axis, pairs + [(b, a) for a, b in pairs])  8.87 us
    pallas_call x2, Pallas kernels, inner_rows(): pl.pallas_call(inner_kernel, in_specs=[VMEM] * 5, out_specs=VMEM, out_sha...  8.14 us
    pallas_call x1, Pallas kernels, split_weights(): pl.pallas_call(split_weights_kernel, grid=weight.shape[:2], in_specs=[spe...  6.05 us
    pallas_call x2, Pallas kernels, outer_rows(): pl.pallas_call(outer_kernel, grid=(2,), in_specs=[VMEM, VMEM, tap, tap, r...  3.68 us
    squeeze x1, local copies, waits for them, and re-layouts, local(): field = outer_rows(partial, reven, rodd, wh[layer], wl[layer])  2.84 us
    unnamed x4, local copies, waits for them, and re-layouts  1.23 us
  transfers between devices with their start and end apart: 8, of which 3 were waited for; matrix products, arithmetic and copies ran while one was open for 5% of the time, Pallas kernels for 24%

profile of v1, /device:TPU:27, one launch (start us, length us, event | category | flops | bytes accessed | tf_op | source)
XLA Modules:
  0.0 59.2 jit_solution(5297254314611126347)
XLA Ops:
  0.0 0.0 copy-start
  0.0 1.2 %copy-done = f32[1,4,256,256]{3,2,1,0:T(8,128)S(1)} copy-done((f32[1,4,256,256]{3,2,1,0:T(8,128)S(1)}, f32[1,4,256,256]{3,2,1,0:T(8,128)}, u32[]{:S(2)}) %copy-start) | copy-done | bytes 1048600
  1.2 0.3 pack_frames.2
  1.5 0.8 %collective-permute-start = (f32[4,64,128]{2,1,0:T(8,128)S(1)}, f32[4,64,128]{2,1,0:T(8,128)S(1)}, u32[]{:S(2)}, u32[]{:S(2)}) collective-permute-start(f32[4,64,128]{2,1,0:T(8,128)S(1)} %get-tuple-element.15), channel_id=1, source_target_pairs={{0,16},{32,48},{64,80},{96,112},{128,144},{160,176},{192,208},{224... | collective-permute-start | bytes 393224 | tf_op jit(solution)/shard_map/ppermute | solution.py:17
  2.3 0.0 copy-start.1
  2.3 8.5 %collective-permute-start.1 = (f32[4,64,128]{2,1,0:T(8,128)S(1)}, f32[4,64,128]{2,1,0:T(8,128)S(1)}, u32[]{:S(2)}, u32[]{:S(2)}) collective-permute-start(f32[4,64,128]{2,1,0:T(8,128)S(1)} %get-tuple-element.16), channel_id=1, source_target_pairs={{16,32},{48,64},{80,96},{112,128},{144,160},{176,192},{208,224},{3... | collective-permute-start | bytes 393224 | tf_op jit(solution)/shard_map/ppermute | solution.py:17
  10.8 6.1 %split_weights.1 = (bf16[2,3,3,256,256]{4,3,2,1,0:T(8,128)(2,1)}, bf16[2,3,3,256,256]{4,3,2,1,0:T(8,128)(2,1)}) custom-call(f32[2,3,3,256,256]{4,3,2,1,0:T(8,128)} %w_ref.1), custom_call_target="tpu_custom_call" | custom-call | tf_op jit(solution)/shard_map/split_weights/pallas_call | solution.py:73
  16.9 0.0 collective-permute-done.feven_ref
  16.9 0.0 collective-permute-done.1.fodd_ref
  16.9 0.0 copy-done.1
  16.9 0.2 edge_rows.2
  17.1 0.8 %collective-permute-start.2 = (f32[256,256]{1,0:T(8,128)S(1)}, f32[256,256]{1,0:T(8,128)S(1)}, u32[]{:S(2)}, u32[]{:S(2)}) collective-permute-start(f32[256,256]{1,0:T(8,128)S(1)} %get-tuple-element.17), channel_id=1, source_target_pairs={{0,1},{2,3},{4,5},{6,7},{8,9},{10,11},{12,13},{14,15},{1,0},{3,2},... | collective-permute-start | bytes 786440 | tf_op jit(solution)/shard_map/ppermute | solution.py:17
  17.9 3.7 %collective-permute-start.3 = (f32[256,256]{1,0:T(8,128)S(1)}, f32[256,256]{1,0:T(8,128)S(1)}, u32[]{:S(2)}, u32[]{:S(2)}) collective-permute-start(f32[256,256]{1,0:T(8,128)S(1)} %get-tuple-element.18), channel_id=1, source_target_pairs={{1,2},{3,4},{5,6},{7,8},{9,10},{11,12},{13,14},{2,1},{4,3},{6,5},{... | collective-permute-start | bytes 786440 | tf_op jit(solution)/shard_map/ppermute | solution.py:17
  21.6 2.8 %slice_bitcast_fusion = (bf16[3,3,256,256]{3,2,1,0:T(8,128)(2,1)S(1)}, bf16[3,3,256,256]{3,2,1,0:T(8,128)(2,1)S(1)}, bf16[3,3,256,256]{3,2,1,0:T(8,128)(2,1)S(1)}, bf16[3,3,256,256]{3,2,1,0:T(8,128)(2,1)S(1)}) fusion(bf16[2,3,3,256,256]{4,3,2,1,0:T(8,128)(2,1)} %get-tuple-element.20, bf16[2,3,3,256,256]{4,3,2,1,0:T(8,128)(2,1)} %get-tuple-element.19), kind=kLoop, calls=%fused_computation | loop fusion | bytes 9437184 | tf_op jit(solution)/shard_map/squeeze | solution.py:231
  24.5 3.6 %inner_rows.2.partial_ref = f32[4,256,256]{2,1,0:T(8,128)S(1)} custom-call(f32[4,256,256]{2,1,0:T(8,128)S(1)} %bitcast.12, f32[4,64,128]{2,1,0:T(8,128)S(1)} %collective-permute-done.feven_ref, f32[4,64,128]{2,1,0:T(8,128)S(1)} %collective-permute-done.1.fodd_ref, bf16[3,3,256,256]{3,2,1,0:T(8,128)(2,1)S(1)} %get-tuple-element.29.wh_ref, ...), custom_call_target="tpu_custom_call" | custom-call | tf_op jit(solution)/shard_map/inner_rows/pallas_call | solution.py:177
  28.1 0.0 collective-permute-done.2.reven_ref
  28.1 1.1 %collective-permute-done.3.rodd_ref = f32[256,256]{1,0:T(8,128)S(1)} collective-permute-done((f32[256,256]{1,0:T(8,128)S(1)}, f32[256,256]{1,0:T(8,128)S(1)}, u32[]{:S(2)}, u32[]{:S(2)}) %collective-permute-start.3) | collective-permute-done | bytes 262176 | tf_op jit(solution)/shard_map/ppermute | solution.py:17
  29.2 1.0 %outer_rows.2.x_ref = f32[4,256,256]{2,1,0:T(8,128)S(1)} custom-call(f32[256,256]{1,0:T(8,128)S(1)} %collective-permute-done.2.reven_ref, f32[256,256]{1,0:T(8,128)S(1)} %collective-permute-done.3.rodd_ref, bf16[3,3,256,256]{3,2,1,0:T(8,128)(2,1)S(1)} %get-tuple-element.29.wh_ref, ...), custom_call_target="tpu_custom_call", output_to_operand_aliasing={{}: (4, {})} | custom-call | tf_op jit(solution)/shard_map/outer_rows/pallas_call | solution.py:209
  30.2 0.3 pack_frames.3
  30.5 0.1 collective-permute-start.4
  30.6 8.0 %collective-permute-start.5 = (f32[4,64,128]{2,1,0:T(8,128)S(1)}, f32[4,64,128]{2,1,0:T(8,128)S(1)}, u32[]{:S(2)}, u32[]{:S(2)}) collective-permute-start(f32[4,64,128]{2,1,0:T(8,128)S(1)} %get-tuple-element.22), channel_id=1, source_target_pairs={{16,32},{48,64},{80,96},{112,128},{144,160},{176,192},{208,224},{3... | collective-permute-start | bytes 393224 | tf_op jit(solution)/shard_map/ppermute | solution.py:17
  38.7 0.0 collective-permute-done.4.feven_ref
  38.7 4.3 %collective-permute-done.5.fodd_ref = f32[4,64,128]{2,1,0:T(8,128)S(1)} collective-permute-done((f32[4,64,128]{2,1,0:T(8,128)S(1)}, f32[4,64,128]{2,1,0:T(8,128)S(1)}, u32[]{:S(2)}, u32[]{:S(2)}) %collective-permute-start.5) | collective-permute-done | bytes 131104 | tf_op jit(solution)/shard_map/ppermute | solution.py:17
  43.0 0.2 edge_rows.3
  43.1 3.5 %collective-permute-start.6 = (f32[256,256]{1,0:T(8,128)S(1)}, f32[256,256]{1,0:T(8,128)S(1)}, u32[]{:S(2)}, u32[]{:S(2)}) collective-permute-start(f32[256,256]{1,0:T(8,128)S(1)} %get-tuple-element.23), channel_id=1, source_target_pairs={{0,1},{2,3},{4,5},{6,7},{8,9},{10,11},{12,13},{14,15},{1,0},{3,2},... | collective-permute-start | bytes 786440 | tf_op jit(solution)/shard_map/ppermute | solution.py:17
  46.7 1.9 %collective-permute-start.7 = (f32[256,256]{1,0:T(8,128)S(1)}, f32[256,256]{1,0:T(8,128)S(1)}, u32[]{:S(2)}, u32[]{:S(2)}) collective-permute-start(f32[256,256]{1,0:T(8,128)S(1)} %get-tuple-element.24), channel_id=1, source_target_pairs={{1,2},{3,4},{5,6},{7,8},{9,10},{11,12},{13,14},{2,1},{4,3},{6,5},{... | collective-permute-start | bytes 786440 | tf_op jit(solution)/shard_map/ppermute | solution.py:17
  48.6 4.6 %inner_rows.3.partial_ref = f32[4,256,256]{2,1,0:T(8,128)} custom-call(f32[4,256,256]{2,1,0:T(8,128)S(1)} %outer_rows.2.x_ref, f32[4,64,128]{2,1,0:T(8,128)S(1)} %collective-permute-done.4.feven_ref, f32[4,64,128]{2,1,0:T(8,128)S(1)} %collective-permute-done.5.fodd_ref, bf16[3,3,256,256]{3,2,1,0:T(8,128)(2,1)S(1)} %get-tuple-element.30.wh_ref, ...), custom_call_target="tpu_custom_call" | custom-call | tf_op jit(solution)/shard_map/inner_rows/pallas_call | solution.py:177
  53.1 0.0 collective-permute-done.6.reven_ref
  53.1 3.4 %collective-permute-done.7.rodd_ref = f32[256,256]{1,0:T(8,128)S(1)} collective-permute-done((f32[256,256]{1,0:T(8,128)S(1)}, f32[256,256]{1,0:T(8,128)S(1)}, u32[]{:S(2)}, u32[]{:S(2)}) %collective-permute-start.7) | collective-permute-done | bytes 262176 | tf_op jit(solution)/shard_map/ppermute | solution.py:17
  56.6 2.7 %outer_rows.3 = f32[4,256,256]{2,1,0:T(8,128)} custom-call(f32[256,256]{1,0:T(8,128)S(1)} %collective-permute-done.6.reven_ref, f32[256,256]{1,0:T(8,128)S(1)} %collective-permute-done.7.rodd_ref, bf16[3,3,256,256]{3,2,1,0:T(8,128)(2,1)S(1)} %get-tuple-element.30.wh_ref, ...), custom_call_target="tpu_custom_call", output_to_operand_aliasing={{}: (4, {})} | custom-call | tf_op jit(solution)/shard_map/outer_rows/pallas_call | solution.py:209
Async XLA Ops:
  0.0 1.2 %copy-start = (f32[1,4,256,256]{3,2,1,0:T(8,128)S(1)}, f32[1,4,256,256]{3,2,1,0:T(8,128)}, u32[]{:S(2)}) copy-start(f32[1,4,256,256]{3,2,1,0:T(8,128)} %param.2) | copy-start | bytes 3145732
  1.5 15.4 %collective-permute-start = (f32[4,64,128]{2,1,0:T(8,128)S(1)}, f32[4,64,128]{2,1,0:T(8,128)S(1)}, u32[]{:S(2)}, u32[]{:S(2)}) collective-permute-start(f32[4,64,128]{2,1,0:T(8,128)S(1)} %get-tuple-element.15), channel_id=1, source_target_pairs={{0,16},{32,48},{64,80},{96,112},{128,144},{160,176},{192,208},{224... | collective-permute-start | bytes 393224 | tf_op jit(solution)/shard_map/ppermute | solution.py:17
  2.3 14.6 %copy-start.1 = (f32[1,4,256,256]{3,2,1,0:T(8,128)S(1)}, f32[1,4,256,256]{3,2,1,0:T(8,128)}, u32[]{:S(2)}) copy-start(f32[1,4,256,256]{3,2,1,0:T(8,128)} %param.2) | copy-start | bytes 3145732
  2.3 14.6 %collective-permute-start.1 = (f32[4,64,128]{2,1,0:T(8,128)S(1)}, f32[4,64,128]{2,1,0:T(8,128)S(1)}, u32[]{:S(2)}, u32[]{:S(2)}) collective-permute-start(f32[4,64,128]{2,1,0:T(8,128)S(1)} %get-tuple-element.16), channel_id=1, source_target_pairs={{16,32},{48,64},{80,96},{112,128},{144,160},{176,192},{208,224},{3... | collective-permute-start | bytes 393224 | tf_op jit(solution)/shard_map/ppermute | solution.py:17
  17.1 11.0 %collective-permute-start.2 = (f32[256,256]{1,0:T(8,128)S(1)}, f32[256,256]{1,0:T(8,128)S(1)}, u32[]{:S(2)}, u32[]{:S(2)}) collective-permute-start(f32[256,256]{1,0:T(8,128)S(1)} %get-tuple-element.17), channel_id=1, source_target_pairs={{0,1},{2,3},{4,5},{6,7},{8,9},{10,11},{12,13},{14,15},{1,0},{3,2},... | collective-permute-start | bytes 786440 | tf_op jit(solution)/shard_map/ppermute | solution.py:17
  17.9 11.3 %collective-permute-start.3 = (f32[256,256]{1,0:T(8,128)S(1)}, f32[256,256]{1,0:T(8,128)S(1)}, u32[]{:S(2)}, u32[]{:S(2)}) collective-permute-start(f32[256,256]{1,0:T(8,128)S(1)} %get-tuple-element.18), channel_id=1, source_target_pairs={{1,2},{3,4},{5,6},{7,8},{9,10},{11,12},{13,14},{2,1},{4,3},{6,5},{... | collective-permute-start | bytes 786440 | tf_op jit(solution)/shard_map/ppermute | solution.py:17
  30.5 8.1 %collective-permute-start.4 = (f32[4,64,128]{2,1,0:T(8,128)S(1)}, f32[4,64,128]{2,1,0:T(8,128)S(1)}, u32[]{:S(2)}, u32[]{:S(2)}) collective-permute-start(f32[4,64,128]{2,1,0:T(8,128)S(1)} %get-tuple-element.21), channel_id=1, source_target_pairs={{0,16},{32,48},{64,80},{96,112},{128,144},{160,176},{192,208},{224... | collective-permute-start | bytes 393224 | tf_op jit(solution)/shard_map/ppermute | solution.py:17
  30.6 12.3 %collective-permute-start.5 = (f32[4,64,128]{2,1,0:T(8,128)S(1)}, f32[4,64,128]{2,1,0:T(8,128)S(1)}, u32[]{:S(2)}, u32[]{:S(2)}) collective-permute-start(f32[4,64,128]{2,1,0:T(8,128)S(1)} %get-tuple-element.22), channel_id=1, source_target_pairs={{16,32},{48,64},{80,96},{112,128},{144,160},{176,192},{208,224},{3... | collective-permute-start | bytes 393224 | tf_op jit(solution)/shard_map/ppermute | solution.py:17
  43.1 10.0 %collective-permute-start.6 = (f32[256,256]{1,0:T(8,128)S(1)}, f32[256,256]{1,0:T(8,128)S(1)}, u32[]{:S(2)}, u32[]{:S(2)}) collective-permute-start(f32[256,256]{1,0:T(8,128)S(1)} %get-tuple-element.23), channel_id=1, source_target_pairs={{0,1},{2,3},{4,5},{6,7},{8,9},{10,11},{12,13},{14,15},{1,0},{3,2},... | collective-permute-start | bytes 786440 | tf_op jit(solution)/shard_map/ppermute | solution.py:17
  46.7 9.9 %collective-permute-start.7 = (f32[256,256]{1,0:T(8,128)S(1)}, f32[256,256]{1,0:T(8,128)S(1)}, u32[]{:S(2)}, u32[]{:S(2)}) collective-permute-start(f32[256,256]{1,0:T(8,128)S(1)} %get-tuple-element.24), channel_id=1, source_target_pairs={{1,2},{3,4},{5,6},{7,8},{9,10},{11,12},{13,14},{2,1},{4,3},{6,5},{... | collective-permute-start | bytes 786440 | tf_op jit(solution)/shard_map/ppermute | solution.py:17

commit v2 on v0

v2 whole, which is shorter than its diff:
```python
import functools

import jax
import jax.numpy as jnp
from jax import lax
from jax.experimental import pallas as pl
from jax.experimental.pallas import tpu as pltpu
from jax.sharding import PartitionSpec as P

F32 = jnp.float32
BF16 = jnp.bfloat16
VMEM = pl.BlockSpec(memory_space=pltpu.VMEM)
PARAMS = pltpu.CompilerParams(vmem_limit_bytes=40 * 2**20)
LANES = 128


def exchange(block, axis, odd):
    count = lax.axis_size(axis)
    pairs = [(i, i + 1) for i in range(odd, count - 1, 2)]
    return lax.ppermute(block, axis, pairs + [(b, a) for a, b in pairs])


def by_parity(axis, even_case, odd_case):
    parity = lax.axis_index(axis) % 2
    pl.when(parity == 0)(even_case)
    pl.when(parity == 1)(odd_case)


def parts(x):
    hi = x.astype(BF16)
    return hi, (x - hi.astype(F32)).astype(BF16)


def dot(a, b):
    return jnp.dot(a, b, preferred_element_type=F32)


def dot3(ah, al, bh, bl):
    return dot(ah, bh) + (dot(al, bh) + dot(ah, bl))


def lane_of(height):
    return lax.broadcasted_iota(jnp.int32, (height, LANES), 1)


def turn(x, lanes):
    return pltpu.roll(x, lanes % LANES, 1) if lanes % LANES else x


def shift_columns(x, dx):
    cols = x.shape[0]
    at = lax.broadcasted_iota(jnp.int32, x.shape, 0)
    if dx == 0:
        return jnp.where(at == 0, 0.0, pltpu.roll(x, 1, 0))
    if dx == 2:
        return jnp.where(at == cols - 1, 0.0, pltpu.roll(x, cols - 1, 0))
    return x


def pack(row, first, width):
    blocks = LANES // width
    height = row.shape[0] // blocks
    block = lane_of(height) // width
    out = turn(row[:height], -first)
    for j in range(1, blocks):
        out = jnp.where(block == j, turn(row[j * height : (j + 1) * height], j * width - first), out)
    return out


def shifted_lanes(own, following, before, fold):
    blocks = LANES // fold
    height = following.shape[0]
    lane = lane_of(height)
    pieces = []
    for j in range(blocks):
        nxt = turn(following, -j * fold)
        prv = turn(before, fold - j * fold)
        pieces.append(
            jnp.where(lane < fold, nxt, jnp.where(lane < 2 * fold, prv, own[j * height : (j + 1) * height]))
        )
    return jnp.concatenate(pieces, axis=0)


def shifted_packed(following, before, fold):
    halves = LANES // (2 * fold)
    block = lane_of(following.shape[0]) // fold
    pieces = []
    for i in range(halves):
        out = turn(following, -i * fold)
        for k in range(halves):
            j = k * halves + i
            out = jnp.where(block == 2 * k, turn(following, (2 * k - j) * fold), out)
            out = jnp.where(block == 2 * k + 1, turn(before, (2 * k + 1 - j) * fold), out)
        pieces.append(out)
    return jnp.concatenate(pieces, axis=0)


def send_kernel(fold, x_ref, fodd_ref, feven_ref, rodd_ref, reven_ref):
    rows, cols, chans = x_ref.shape

    def frames(to_before, to_following):
        for r in range(rows):
            lanes = x_ref[r, :, :LANES]
            to_before[r] = pack(lanes, 0, fold)
            to_following[r] = pack(lanes, fold, fold)

    def edges(first_to, last_to):
        for r, out in ((0, first_to), (rows - 1, last_to)):
            out[:cols] = x_ref[r, :, LANES:]
            out[cols:] = pack(x_ref[r, :, :LANES], 2 * fold, LANES - 2 * fold)

    by_parity("frame", lambda: frames(fodd_ref, feven_ref), lambda: frames(feven_ref, fodd_ref))
    by_parity("row", lambda: edges(rodd_ref, reven_ref), lambda: edges(reven_ref, rodd_ref))


def send(x):
    rows, cols, chans = x.shape
    fold = chans // 8
    frames = jax.ShapeDtypeStruct((rows, cols * fold // LANES, LANES), F32)
    edge = jax.ShapeDtypeStruct((cols * (chans - 2 * fold) // LANES, LANES), F32)
    return pl.pallas_call(
        functools.partial(send_kernel, fold),
        in_specs=[VMEM],
        out_specs=[VMEM] * 4,
        out_shape=[frames, frames, edge, edge],
        name="send",
        compiler_params=PARAMS,
    )(x)


def forward_kernel(fold, fodd_ref, feven_ref, sodd_ref, seven_ref):
    rows = fodd_ref.shape[0]

    def write(following, before, first_to, last_to):
        for r, out in ((0, first_to), (rows - 1, last_to)):
            out[...] = shifted_packed(following[r], before[r], fold)

    def rows_case(first_to, last_to):
        by_parity(
            "frame",
            lambda: write(feven_ref, fodd_ref, first_to, last_to),
            lambda: write(fodd_ref, feven_ref, first_to, last_to),
        )

    by_parity("row", lambda: rows_case(sodd_ref, seven_ref), lambda: rows_case(seven_ref, sodd_ref))


def forward(fodd, feven, cols, fold):
    edge = jax.ShapeDtypeStruct((cols * 2 * fold // LANES, LANES), F32)
    return pl.pallas_call(
        functools.partial(forward_kernel, fold),
        in_specs=[VMEM] * 2,
        out_specs=[VMEM] * 2,
        out_shape=[edge, edge],
        name="forward",
        compiler_params=PARAMS,
    )(fodd, feven)


def inner_kernel(fold, x_ref, fodd_ref, feven_ref, w_ref, out_ref, partial_ref, wh_ref, wl_ref, hi, lo):
    rows, cols, chans = x_ref.shape
    dx = pl.program_id(0)

    def write(following, before):
        for r in range(rows):
            lanes = shifted_lanes(x_ref[r, :, :LANES], following[r], before[r], fold)
            at = slice(r * cols, (r + 1) * cols)
            hi[at, :LANES], lo[at, :LANES] = parts(lanes)
            hi[at, LANES:], lo[at, LANES:] = parts(x_ref[r, :, LANES:])

    @pl.when(dx == 0)
    def _():
        by_parity("frame", lambda: write(feven_ref, fodd_ref), lambda: write(fodd_ref, feven_ref))

    weights = [parts(w_ref[0, dy, 0]) for dy in range(3)]
    for i, dy in enumerate((0, 2)):
        wh_ref[i, 0], wl_ref[i, 0] = weights[dy]

    def products(dy, first, last):
        at = slice(first * cols, last * cols)
        return dot3(hi[at], lo[at], *weights[dy])

    top = products(1, 0, 1) + products(2, 1, 2)
    middle = products(0, 0, rows - 2) + products(1, 1, rows - 1) + products(2, 2, rows)
    bottom = products(0, rows - 2, rows - 1) + products(1, rows - 1, rows)
    for k in range(3):

        @pl.when(dx == k)
        def _(k=k):
            for i, total in enumerate((top, bottom)):
                total = shift_columns(total, k)
                partial_ref[i] = total if k == 0 else partial_ref[i] + total
            for r in range(1, rows - 1):
                total = shift_columns(middle[(r - 1) * cols : r * cols], k)
                total = total if k == 0 else out_ref[r - 1] + total
                out_ref[r - 1] = jnp.maximum(total, 0.0) if k == 2 else total


def inner_rows(x, fodd, feven, weight, layer):
    rows, cols, chans = x.shape
    outs = weight.shape[-1]
    whole = lambda shape: pl.BlockSpec(shape, lambda dx: (0,) * len(shape))
    taps = pl.BlockSpec((2, 1, chans, outs), lambda dx: (0, dx, 0, 0))
    split = jax.ShapeDtypeStruct((2, 3, chans, outs), BF16)
    return pl.pallas_call(
        functools.partial(inner_kernel, chans // 8),
        grid=(3,),
        in_specs=[VMEM, VMEM, VMEM, pl.BlockSpec((1, 3, 1, chans, outs), lambda dx: (layer, 0, dx, 0, 0))],
        out_specs=[whole((rows - 2, cols, outs)), whole((2, cols, outs)), taps, taps],
        out_shape=[
            jax.ShapeDtypeStruct((rows - 2, cols, outs), F32),
            jax.ShapeDtypeStruct((2, cols, outs), F32),
            split,
            split,
        ],
        scratch_shapes=[pltpu.VMEM((rows * cols, chans), BF16), pltpu.VMEM((rows * cols, chans), BF16)],
        name="inner_rows",
        compiler_params=PARAMS,
    )(x, fodd, feven, weight)


def outer_kernel(fold, rodd_ref, reven_ref, sodd_ref, seven_ref, wh_ref, wl_ref, partial_ref, inner_ref, out_ref):
    rows, cols, outs = out_ref.shape
    width = 2 * fold
    out_ref[1 : rows - 1] = inner_ref[...]

    def finish(i, kept_ref, moved_ref):
        halves = LANES // width
        height = cols // halves
        lane = lane_of(height)
        low = []
        for k in range(halves):
            moved = turn(moved_ref[...], -k * width)
            kept = turn(kept_ref[cols:], width - k * width)
            low.append(jnp.where(lane < width, moved, kept))
        halo = jnp.concatenate([jnp.concatenate(low, axis=0), kept_ref[:cols]], axis=1)
        hi, lo = parts(halo)
        total = partial_ref[i]
        for dx in range(3):
            total = total + shift_columns(dot3(hi, lo, wh_ref[i, dx], wl_ref[i, dx]), dx)
        out_ref[i * (rows - 1)] = jnp.maximum(total, 0.0)

    def both(above, below):
        finish(0, *above)
        finish(1, *below)

    odd, even = (rodd_ref, sodd_ref), (reven_ref, seven_ref)
    by_parity("row", lambda: both(odd, even), lambda: both(even, odd))


def outer_rows(rodd, reven, sodd, seven, wh, wl, partial, inner):
    rows, cols, outs = inner.shape
    return pl.pallas_call(
        functools.partial(outer_kernel, wh.shape[2] // 8),
        in_specs=[VMEM] * 8,
        out_specs=VMEM,
        out_shape=jax.ShapeDtypeStruct((rows + 2, cols, outs), F32),
        name="outer_rows",
        compiler_params=PARAMS,
    )(rodd, reven, sodd, seven, wh, wl, partial, inner)


def local(features, conv_weight):
    frames, rows, cols, chans = features.shape
    field = features.reshape(rows, cols, chans)
    for layer in range(conv_weight.shape[0]):
        fodd, feven, rodd, reven = send(field)
        fodd, feven = exchange(fodd, "frame", 1), exchange(feven, "frame", 0)
        rodd, reven = exchange(rodd, "row", 1), exchange(reven, "row", 0)
        sodd, seven = forward(fodd, feven, cols, chans // 8)
        sodd, seven = exchange(sodd, "row", 1), exchange(seven, "row", 0)
        inner, partial, wh, wl = inner_rows(field, fodd, feven, conv_weight, layer)
        field = outer_rows(rodd, reven, sodd, seven, wh, wl, partial, inner)
    return field.reshape(features.shape)


def solution(mesh):
    placed = (P("frame", "row", None, None), P())
    return jax.shard_map(
        local, mesh=mesh, in_specs=placed, out_specs=P("frame", "row", None, None), check_vma=False
    )
```

time: 111 us -> 58.1 us (0.52)
  the two profiles are of different devices: /device:TPU:224 before, /device:TPU:26 now
where the time goes in v2:
time: 58.1 us; the launch traced here: 57.8 us
  starting transfers between devices  36.7 us (63%)
  Pallas kernels  12.9 us (22%)
  local copies, waits for them, and re-layouts  4.79 us (8%)
  waiting for transfers between devices  3.2 us (6%)
    ppermute x12, starting transfers between devices, exchange(): return lax.ppermute(block, axis, pairs + [(b, a) for a, b in pairs])  36.7 us
    pallas_call x2, Pallas kernels, inner_rows(): pl.pallas_call(functools.partial(inner_kernel, chans // 8), grid=(3,), in...  9.2 us
    unnamed x8, local copies, waits for them, and re-layouts  4.79 us
    ppermute x12, waiting for transfers between devices, exchange(): return lax.ppermute(block, axis, pairs + [(b, a) for a, b in pairs])  3.2 us
    pallas_call x2, Pallas kernels, outer_rows(): pl.pallas_call(functools.partial(outer_kernel, wh.shape[2] // 8), in_spec...  2.71 us
  transfers between devices with their start and end apart: 12, of which 1 were waited for; matrix products, arithmetic and copies ran while one was open for 0% of the time, Pallas kernels for 16%

profile of v2, /device:TPU:26, one launch (start us, length us, event | category | flops | bytes accessed | tf_op | source)
XLA Modules:
  0.0 57.8 jit_solution(3049222495830087591)
XLA Ops:
  0.0 0.0 copy-start.2
  0.0 1.2 %copy-done.2 = f32[1,4,256,256]{3,2,1,0:T(8,128)S(1)} copy-done((f32[1,4,256,256]{3,2,1,0:T(8,128)S(1)}, f32[1,4,256,256]{3,2,1,0:T(8,128)}, u32[]{:S(2)}) %copy-start.2) | copy-done | bytes 1048600
  1.2 0.4 send.2
  1.6 2.1 %collective-permute-start.2 = (f32[4,64,128]{2,1,0:T(8,128)S(1)}, f32[4,64,128]{2,1,0:T(8,128)S(1)}, u32[]{:S(2)}, u32[]{:S(2)}) collective-permute-start(f32[4,64,128]{2,1,0:T(8,128)S(1)} %get-tuple-element.27), channel_id=1, source_target_pairs={{16,32},{48,64},{80,96},{112,128},{144,160},{176,192},{208,224},{3... | collective-permute-start | bytes 393224 | tf_op jit(solution)/shard_map/ppermute | solution.py:20
  3.7 6.9 %collective-permute-start.3 = (f32[4,64,128]{2,1,0:T(8,128)S(1)}, f32[4,64,128]{2,1,0:T(8,128)S(1)}, u32[]{:S(2)}, u32[]{:S(2)}) collective-permute-start(f32[4,64,128]{2,1,0:T(8,128)S(1)} %get-tuple-element.28), channel_id=1, source_target_pairs={{0,16},{32,48},{64,80},{96,112},{128,144},{160,176},{192,208},{224... | collective-permute-start | bytes 393224 | tf_op jit(solution)/shard_map/ppermute | solution.py:20
  10.6 3.8 %collective-permute-start = (f32[384,128]{1,0:T(8,128)S(1)}, f32[384,128]{1,0:T(8,128)S(1)}, u32[]{:S(2)}, u32[]{:S(2)}) collective-permute-start(f32[384,128]{1,0:T(8,128)S(1)} %get-tuple-element.25), channel_id=1, source_target_pairs={{1,2},{3,4},{5,6},{7,8},{9,10},{11,12},{13,14},{2,1},{4,3},{6,5},{... | collective-permute-start | bytes 589832 | tf_op jit(solution)/shard_map/ppermute | solution.py:20
  14.4 0.2 collective-permute-start.1
  14.6 0.0 collective-permute-done.2.fodd_ref
  14.6 0.0 collective-permute-done.3.feven_ref
  14.6 0.1 forward.2
  14.7 4.6 %collective-permute-start.4 = (f32[128,128]{1,0:T(8,128)S(1)}, f32[128,128]{1,0:T(8,128)S(1)}, u32[]{:S(2)}, u32[]{:S(2)}) collective-permute-start(f32[128,128]{1,0:T(8,128)S(1)} %get-tuple-element.29), channel_id=1, source_target_pairs={{1,2},{3,4},{5,6},{7,8},{9,10},{11,12},{13,14},{2,1},{4,3},{6,5},{... | collective-permute-start | bytes 196616 | tf_op jit(solution)/shard_map/ppermute | solution.py:20
  19.4 1.2 %collective-permute-start.5 = (f32[128,128]{1,0:T(8,128)S(1)}, f32[128,128]{1,0:T(8,128)S(1)}, u32[]{:S(2)}, u32[]{:S(2)}) collective-permute-start(f32[128,128]{1,0:T(8,128)S(1)} %get-tuple-element.30), channel_id=1, source_target_pairs={{0,1},{2,3},{4,5},{6,7},{8,9},{10,11},{12,13},{14,15},{1,0},{3,2},... | collective-permute-start | bytes 196616 | tf_op jit(solution)/shard_map/ppermute | solution.py:20
  20.6 0.0 copy-start
  20.6 2.3 %copy-done = f32[2,3,3,256,256]{4,3,2,1,0:T(8,128)S(1)} copy-done((f32[2,3,3,256,256]{4,3,2,1,0:T(8,128)S(1)}, f32[2,3,3,256,256]{4,3,2,1,0:T(8,128)}, u32[]{:S(2)}) %copy-start) | copy-done | bytes 4718616
  22.9 0.0 copy-start.3
  22.9 1.2 %copy-done.3 = f32[1,4,256,256]{3,2,1,0:T(8,128)S(1)} copy-done((f32[1,4,256,256]{3,2,1,0:T(8,128)S(1)}, f32[1,4,256,256]{3,2,1,0:T(8,128)}, u32[]{:S(2)}) %copy-start.3) | copy-done | bytes 1048600
  24.1 0.0 copy-start.1
  24.1 4.6 %inner_rows.2 = (f32[2,256,256]{2,1,0:T(8,128)S(1)}, f32[2,256,256]{2,1,0:T(8,128)S(1)}, bf16[2,3,256,256]{3,2,1,0:T(8,128)(2,1)S(1)}, bf16[2,3,256,256]{3,2,1,0:T(8,128)(2,1)S(1)}) custom-call(f32[4,256,256]{2,1,0:T(8,128)S(1)} %bitcast.3, f32[4,64,128]{2,1,0:T(8,128)S(1)} %collective-permute-done.2.fodd_ref, ...), custom_call_target="tpu_custom_call" | custom-call | tf_op jit(solution)/shard_map/inner_rows/pallas_call | solution.py:205
  28.7 0.0 collective-permute-done.4.sodd_ref
  28.8 0.0 collective-permute-done.5.seven_ref
  28.8 0.0 collective-permute-done.rodd_ref
  28.8 0.0 collective-permute-done.1.reven_ref
  28.8 0.9 %outer_rows.2.x_ref = f32[4,256,256]{2,1,0:T(8,128)S(1)} custom-call(f32[384,128]{1,0:T(8,128)S(1)} %collective-permute-done.rodd_ref, f32[384,128]{1,0:T(8,128)S(1)} %collective-permute-done.1.reven_ref, f32[128,128]{1,0:T(8,128)S(1)} %collective-permute-done.4.sodd_ref, f32[128,128]{1,0:T(8,128)S(1)} %collective-permute-done.5.seven_ref, ...), custom_call_target="tpu_custom_call" | custom-call | tf_op jit(solution)/shard_map/outer_rows/pallas_call | solution.py:253
  29.7 0.4 send.3
  30.1 1.9 %collective-permute-start.8 = (f32[4,64,128]{2,1,0:T(8,128)S(1)}, f32[4,64,128]{2,1,0:T(8,128)S(1)}, u32[]{:S(2)}, u32[]{:S(2)}) collective-permute-start(f32[4,64,128]{2,1,0:T(8,128)S(1)} %get-tuple-element.37), channel_id=1, source_target_pairs={{16,32},{48,64},{80,96},{112,128},{144,160},{176,192},{208,224},{3... | collective-permute-start | bytes 393224 | tf_op jit(solution)/shard_map/ppermute | solution.py:20
  32.0 6.1 %collective-permute-start.9 = (f32[4,64,128]{2,1,0:T(8,128)S(1)}, f32[4,64,128]{2,1,0:T(8,128)S(1)}, u32[]{:S(2)}, u32[]{:S(2)}) collective-permute-start(f32[4,64,128]{2,1,0:T(8,128)S(1)} %get-tuple-element.38), channel_id=1, source_target_pairs={{0,16},{32,48},{64,80},{96,112},{128,144},{160,176},{192,208},{224... | collective-permute-start | bytes 393224 | tf_op jit(solution)/shard_map/ppermute | solution.py:20
  38.1 3.8 %collective-permute-start.6 = (f32[384,128]{1,0:T(8,128)S(1)}, f32[384,128]{1,0:T(8,128)S(1)}, u32[]{:S(2)}, u32[]{:S(2)}) collective-permute-start(f32[384,128]{1,0:T(8,128)S(1)} %get-tuple-element.35), channel_id=1, source_target_pairs={{1,2},{3,4},{5,6},{7,8},{9,10},{11,12},{13,14},{2,1},{4,3},{6,5},{... | collective-permute-start | bytes 589832 | tf_op jit(solution)/shard_map/ppermute | solution.py:20
  41.9 0.6 collective-permute-start.7
  42.5 0.0 collective-permute-done.8.fodd_ref
  42.5 0.0 collective-permute-done.9.feven_ref
  42.5 0.1 forward.3
  42.6 4.4 %collective-permute-start.10 = (f32[128,128]{1,0:T(8,128)S(1)}, f32[128,128]{1,0:T(8,128)S(1)}, u32[]{:S(2)}, u32[]{:S(2)}) collective-permute-start(f32[128,128]{1,0:T(8,128)S(1)} %get-tuple-element.39), channel_id=1, source_target_pairs={{1,2},{3,4},{5,6},{7,8},{9,10},{11,12},{13,14},{2,1},{4,3},{6,5},{... | collective-permute-start | bytes 196616 | tf_op jit(solution)/shard_map/ppermute | solution.py:20
  47.0 1.2 %collective-permute-start.11 = (f32[128,128]{1,0:T(8,128)S(1)}, f32[128,128]{1,0:T(8,128)S(1)}, u32[]{:S(2)}, u32[]{:S(2)}) collective-permute-start(f32[128,128]{1,0:T(8,128)S(1)} %get-tuple-element.40), channel_id=1, source_target_pairs={{0,1},{2,3},{4,5},{6,7},{8,9},{10,11},{12,13},{14,15},{1,0},{3,2},... | collective-permute-start | bytes 196616 | tf_op jit(solution)/shard_map/ppermute | solution.py:20
  48.1 0.0 copy-done.1
  48.1 4.6 %inner_rows.3 = (f32[2,256,256]{2,1,0:T(8,128)S(1)}, f32[2,256,256]{2,1,0:T(8,128)S(1)}, bf16[2,3,256,256]{3,2,1,0:T(8,128)(2,1)S(1)}, bf16[2,3,256,256]{3,2,1,0:T(8,128)(2,1)S(1)}) custom-call(f32[4,256,256]{2,1,0:T(8,128)S(1)} %outer_rows.2.x_ref, f32[4,64,128]{2,1,0:T(8,128)S(1)} %collective-permute-done.8.fodd_ref, ...), custom_call_target="tpu_custom_call" | custom-call | tf_op jit(solution)/shard_map/inner_rows/pallas_call | solution.py:205
  52.8 3.2 %collective-permute-done.10.sodd_ref = f32[128,128]{1,0:T(8,128)S(1)} collective-permute-done((f32[128,128]{1,0:T(8,128)S(1)}, f32[128,128]{1,0:T(8,128)S(1)}, u32[]{:S(2)}, u32[]{:S(2)}) %collective-permute-start.10) | collective-permute-done | bytes 65568 | tf_op jit(solution)/shard_map/ppermute | solution.py:20
  55.9 0.0 collective-permute-done.11.seven_ref
  55.9 0.0 collective-permute-done.6.rodd_ref
  55.9 0.0 collective-permute-done.7.reven_ref
  55.9 1.8 %outer_rows.3 = f32[4,256,256]{2,1,0:T(8,128)} custom-call(f32[384,128]{1,0:T(8,128)S(1)} %collective-permute-done.6.rodd_ref, f32[384,128]{1,0:T(8,128)S(1)} %collective-permute-done.7.reven_ref, f32[128,128]{1,0:T(8,128)S(1)} %collective-permute-done.10.sodd_ref, f32[128,128]{1,0:T(8,128)S(1)} %collective-permute-done.11.seven_ref, ...), custom_call_target="tpu_custom_call" | custom-call | tf_op jit(solution)/shard_map/outer_rows/pallas_call | solution.py:253
Async XLA Ops:
  0.0 1.2 %copy-start.2 = (f32[1,4,256,256]{3,2,1,0:T(8,128)S(1)}, f32[1,4,256,256]{3,2,1,0:T(8,128)}, u32[]{:S(2)}) copy-start(f32[1,4,256,256]{3,2,1,0:T(8,128)} %param.2) | copy-start | bytes 3145732
  1.6 13.0 %collective-permute-start.2 = (f32[4,64,128]{2,1,0:T(8,128)S(1)}, f32[4,64,128]{2,1,0:T(8,128)S(1)}, u32[]{:S(2)}, u32[]{:S(2)}) collective-permute-start(f32[4,64,128]{2,1,0:T(8,128)S(1)} %get-tuple-element.27), channel_id=1, source_target_pairs={{16,32},{48,64},{80,96},{112,128},{144,160},{176,192},{208,224},{3... | collective-permute-start | bytes 393224 | tf_op jit(solution)/shard_map/ppermute | solution.py:20
  3.7 10.9 %collective-permute-start.3 = (f32[4,64,128]{2,1,0:T(8,128)S(1)}, f32[4,64,128]{2,1,0:T(8,128)S(1)}, u32[]{:S(2)}, u32[]{:S(2)}) collective-permute-start(f32[4,64,128]{2,1,0:T(8,128)S(1)} %get-tuple-element.28), channel_id=1, source_target_pairs={{0,16},{32,48},{64,80},{96,112},{128,144},{160,176},{192,208},{224... | collective-permute-start | bytes 393224 | tf_op jit(solution)/shard_map/ppermute | solution.py:20
  10.6 18.2 %collective-permute-start = (f32[384,128]{1,0:T(8,128)S(1)}, f32[384,128]{1,0:T(8,128)S(1)}, u32[]{:S(2)}, u32[]{:S(2)}) collective-permute-start(f32[384,128]{1,0:T(8,128)S(1)} %get-tuple-element.25), channel_id=1, source_target_pairs={{1,2},{3,4},{5,6},{7,8},{9,10},{11,12},{13,14},{2,1},{4,3},{6,5},{... | collective-permute-start | bytes 589832 | tf_op jit(solution)/shard_map/ppermute | solution.py:20
  14.4 14.4 %collective-permute-start.1 = (f32[384,128]{1,0:T(8,128)S(1)}, f32[384,128]{1,0:T(8,128)S(1)}, u32[]{:S(2)}, u32[]{:S(2)}) collective-permute-start(f32[384,128]{1,0:T(8,128)S(1)} %get-tuple-element.26), channel_id=1, source_target_pairs={{0,1},{2,3},{4,5},{6,7},{8,9},{10,11},{12,13},{14,15},{1,0},{3,2},... | collective-permute-start | bytes 589832 | tf_op jit(solution)/shard_map/ppermute | solution.py:20
  14.7 14.0 %collective-permute-start.4 = (f32[128,128]{1,0:T(8,128)S(1)}, f32[128,128]{1,0:T(8,128)S(1)}, u32[]{:S(2)}, u32[]{:S(2)}) collective-permute-start(f32[128,128]{1,0:T(8,128)S(1)} %get-tuple-element.29), channel_id=1, source_target_pairs={{1,2},{3,4},{5,6},{7,8},{9,10},{11,12},{13,14},{2,1},{4,3},{6,5},{... | collective-permute-start | bytes 196616 | tf_op jit(solution)/shard_map/ppermute | solution.py:20
  19.4 9.4 %collective-permute-start.5 = (f32[128,128]{1,0:T(8,128)S(1)}, f32[128,128]{1,0:T(8,128)S(1)}, u32[]{:S(2)}, u32[]{:S(2)}) collective-permute-start(f32[128,128]{1,0:T(8,128)S(1)} %get-tuple-element.30), channel_id=1, source_target_pairs={{0,1},{2,3},{4,5},{6,7},{8,9},{10,11},{12,13},{14,15},{1,0},{3,2},... | collective-permute-start | bytes 196616 | tf_op jit(solution)/shard_map/ppermute | solution.py:20
  20.6 2.3 %copy-start = (f32[2,3,3,256,256]{4,3,2,1,0:T(8,128)S(1)}, f32[2,3,3,256,256]{4,3,2,1,0:T(8,128)}, u32[]{:S(2)}) copy-start(f32[2,3,3,256,256]{4,3,2,1,0:T(8,128)} %w_ref.3) | copy-start | bytes 14155780
  22.9 1.2 %copy-start.3 = (f32[1,4,256,256]{3,2,1,0:T(8,128)S(1)}, f32[1,4,256,256]{3,2,1,0:T(8,128)}, u32[]{:S(2)}) copy-start(f32[1,4,256,256]{3,2,1,0:T(8,128)} %param.2) | copy-start | bytes 3145732
  24.1 24.0 %copy-start.1 = (f32[2,3,3,256,256]{4,3,2,1,0:T(8,128)S(1)}, f32[2,3,3,256,256]{4,3,2,1,0:T(8,128)}, u32[]{:S(2)}) copy-start(f32[2,3,3,256,256]{4,3,2,1,0:T(8,128)} %w_ref.3) | copy-start | bytes 14155780
  30.1 12.4 %collective-permute-start.8 = (f32[4,64,128]{2,1,0:T(8,128)S(1)}, f32[4,64,128]{2,1,0:T(8,128)S(1)}, u32[]{:S(2)}, u32[]{:S(2)}) collective-permute-start(f32[4,64,128]{2,1,0:T(8,128)S(1)} %get-tuple-element.37), channel_id=1, source_target_pairs={{16,32},{48,64},{80,96},{112,128},{144,160},{176,192},{208,224},{3... | collective-permute-start | bytes 393224 | tf_op jit(solution)/shard_map/ppermute | solution.py:20
  32.0 10.5 %collective-permute-start.9 = (f32[4,64,128]{2,1,0:T(8,128)S(1)}, f32[4,64,128]{2,1,0:T(8,128)S(1)}, u32[]{:S(2)}, u32[]{:S(2)}) collective-permute-start(f32[4,64,128]{2,1,0:T(8,128)S(1)} %get-tuple-element.38), channel_id=1, source_target_pairs={{0,16},{32,48},{64,80},{96,112},{128,144},{160,176},{192,208},{224... | collective-permute-start | bytes 393224 | tf_op jit(solution)/shard_map/ppermute | solution.py:20
  38.1 17.8 %collective-permute-start.6 = (f32[384,128]{1,0:T(8,128)S(1)}, f32[384,128]{1,0:T(8,128)S(1)}, u32[]{:S(2)}, u32[]{:S(2)}) collective-permute-start(f32[384,128]{1,0:T(8,128)S(1)} %get-tuple-element.35), channel_id=1, source_target_pairs={{1,2},{3,4},{5,6},{7,8},{9,10},{11,12},{13,14},{2,1},{4,3},{6,5},{... | collective-permute-start | bytes 589832 | tf_op jit(solution)/shard_map/ppermute | solution.py:20
  41.9 14.0 %collective-permute-start.7 = (f32[384,128]{1,0:T(8,128)S(1)}, f32[384,128]{1,0:T(8,128)S(1)}, u32[]{:S(2)}, u32[]{:S(2)}) collective-permute-start(f32[384,128]{1,0:T(8,128)S(1)} %get-tuple-element.36), channel_id=1, source_target_pairs={{0,1},{2,3},{4,5},{6,7},{8,9},{10,11},{12,13},{14,15},{1,0},{3,2},... | collective-permute-start | bytes 589832 | tf_op jit(solution)/shard_map/ppermute | solution.py:20
  42.6 13.3 %collective-permute-start.10 = (f32[128,128]{1,0:T(8,128)S(1)}, f32[128,128]{1,0:T(8,128)S(1)}, u32[]{:S(2)}, u32[]{:S(2)}) collective-permute-start(f32[128,128]{1,0:T(8,128)S(1)} %get-tuple-element.39), channel_id=1, source_target_pairs={{1,2},{3,4},{5,6},{7,8},{9,10},{11,12},{13,14},{2,1},{4,3},{6,5},{... | collective-permute-start | bytes 196616 | tf_op jit(solution)/shard_map/ppermute | solution.py:20
  47.0 9.0 %collective-permute-start.11 = (f32[128,128]{1,0:T(8,128)S(1)}, f32[128,128]{1,0:T(8,128)S(1)}, u32[]{:S(2)}, u32[]{:S(2)}) collective-permute-start(f32[128,128]{1,0:T(8,128)S(1)} %get-tuple-element.40), channel_id=1, source_target_pairs={{0,1},{2,3},{4,5},{6,7},{8,9},{10,11},{12,13},{14,15},{1,0},{3,2},... | collective-permute-start | bytes 196616 | tf_op jit(solution)/shard_map/ppermute | solution.py:20

commit v3 on v2

--- a/solution.py
+++ b/solution.py
@@ -128,7 +128,7 @@
     )(x)
 
 
-def forward_kernel(fold, fodd_ref, feven_ref, sodd_ref, seven_ref):
+def forward_kernel(fold, fodd_ref, feven_ref, ready_ref, sodd_ref, seven_ref):
     rows = fodd_ref.shape[0]
 
     def write(following, before, first_to, last_to):
@@ -145,81 +145,122 @@
     by_parity("row", lambda: rows_case(sodd_ref, seven_ref), lambda: rows_case(seven_ref, sodd_ref))
 
 
-def forward(fodd, feven, cols, fold):
+def forward(fodd, feven, ready, cols, fold):
     edge = jax.ShapeDtypeStruct((cols * 2 * fold // LANES, LANES), F32)
     return pl.pallas_call(
         functools.partial(forward_kernel, fold),
-        in_specs=[VMEM] * 2,
+        in_specs=[VMEM] * 3,
         out_specs=[VMEM] * 2,
         out_shape=[edge, edge],
         name="forward",
         compiler_params=PARAMS,
-    )(fodd, feven)
-
-
-def inner_kernel(fold, x_ref, fodd_ref, feven_ref, w_ref, out_ref, partial_ref, wh_ref, wl_ref, hi, lo):
+    )(fodd, feven, ready)
+
+
+def prepare_kernel(w_ref, *refs):
+    layers = w_ref.shape[0]
+    for l in range(layers):
+        hi_ref, lo_ref = refs[2 * l], refs[2 * l + 1]
+        for dx in range(3):
+            first, mid, last = w_ref[l, 0, dx], w_ref[l, 1, dx], w_ref[l, 2, dx]
+            ends = 0.5 * (first + last)
+            half = 0.5 * mid
+            for m, value in enumerate((first, ends + half, ends - half, last)):
+                hi_ref[m, dx], lo_ref[m, dx] = parts(value)
+    refs[2 * layers][...] = jnp.zeros_like(refs[2 * layers])
+
+
+def prepare(weight):
+    layers, _, _, chans, outs = weight.shape
+    split = jax.ShapeDtypeStruct((4, 3, chans, outs), BF16)
+    *split, ready = pl.pallas_call(
+        prepare_kernel,
+        in_specs=[VMEM],
+        out_specs=[VMEM] * (2 * layers + 1),
+        out_shape=[split] * (2 * layers) + [jax.ShapeDtypeStruct((8, LANES), F32)],
+        name="prepare",
+        compiler_params=PARAMS,
+    )(weight)
+    return split, ready
+
+
+def inner_kernel(fold, x_ref, fodd_ref, feven_ref, wh_ref, wl_ref, out_ref, partial_ref, beside_ref, shifted, hi, lo):
     rows, cols, chans = x_ref.shape
-    dx = pl.program_id(0)
+    pairs = rows // 2
 
     def write(following, before):
         for r in range(rows):
-            lanes = shifted_lanes(x_ref[r, :, :LANES], following[r], before[r], fold)
-            at = slice(r * cols, (r + 1) * cols)
-            hi[at, :LANES], lo[at, :LANES] = parts(lanes)
-            hi[at, LANES:], lo[at, LANES:] = parts(x_ref[r, :, LANES:])
-
-    @pl.when(dx == 0)
-    def _():
-        by_parity("frame", lambda: write(feven_ref, fodd_ref), lambda: write(fodd_ref, feven_ref))
-
-    weights = [parts(w_ref[0, dy, 0]) for dy in range(3)]
-    for i, dy in enumerate((0, 2)):
-        wh_ref[i, 0], wl_ref[i, 0] = weights[dy]
-
-    def products(dy, first, last):
-        at = slice(first * cols, last * cols)
-        return dot3(hi[at], lo[at], *weights[dy])
-
-    top = products(1, 0, 1) + products(2, 1, 2)
-    middle = products(0, 0, rows - 2) + products(1, 1, rows - 1) + products(2, 2, rows)
-    bottom = products(0, rows - 2, rows - 1) + products(1, rows - 1, rows)
-    for k in range(3):
-
-        @pl.when(dx == k)
-        def _(k=k):
-            for i, total in enumerate((top, bottom)):
-                total = shift_columns(total, k)
-                partial_ref[i] = total if k == 0 else partial_ref[i] + total
-            for r in range(1, rows - 1):
-                total = shift_columns(middle[(r - 1) * cols : r * cols], k)
-                total = total if k == 0 else out_ref[r - 1] + total
-                out_ref[r - 1] = jnp.maximum(total, 0.0) if k == 2 else total
-
-
-def inner_rows(x, fodd, feven, weight, layer):
+            shifted[r, :, :LANES] = shifted_lanes(x_ref[r, :, :LANES], following[r], before[r], fold)
+            shifted[r, :, LANES:] = x_ref[r, :, LANES:]
+
+    by_parity("frame", lambda: write(feven_ref, fodd_ref), lambda: write(fodd_ref, feven_ref))
+    beside_ref[0] = shifted[1]
+    beside_ref[1] = shifted[rows - 2]
+
+    def fill(at, value):
+        place = slice(at * cols, (at + 1) * cols)
+        hi[place], lo[place] = parts(value)
+
+    for p in range(pairs):
+        fill(p, shifted[2 * p] + shifted[2 * p + 1])
+        fill(pairs + p, shifted[2 * p + 1] - shifted[2 * p])
+    for p in range(pairs - 1):
+        fill(2 * pairs + p, shifted[2 * p + 1] - shifted[2 * p + 3])
+        fill(3 * pairs - 1 + p, shifted[2 * p] - shifted[2 * p + 2])
+
+    def products(m, dx, first, count):
+        at = slice(first * cols, (first + count) * cols)
+        return dot3(hi[at], lo[at], wh_ref[m, dx], wl_ref[m, dx])
+
+    totals = [None] * rows
+    for dx in (1, 0, 2):
+        plus = products(1, dx, 0, pairs)
+        minus = products(2, dx, pairs, pairs)
+        above = products(0, dx, 2 * pairs, pairs - 1)
+        below = products(3, dx, 3 * pairs - 1, pairs - 1)
+        for p in range(pairs):
+            at = slice(p * cols, (p + 1) * cols)
+            one = plus[at] + minus[at]
+            if p > 0:
+                one = one + above[(p - 1) * cols : p * cols]
+            two = plus[at] - minus[at]
+            if p < pairs - 1:
+                two = two - below[p * cols : (p + 1) * cols]
+            for r, value in ((2 * p, one), (2 * p + 1, two)):
+                value = shift_columns(value, dx)
+                totals[r] = value if totals[r] is None else totals[r] + value
+    partial_ref[0] = totals[0]
+    partial_ref[1] = totals[rows - 1]
+    for r in range(1, rows - 1):
+        out_ref[r - 1] = jnp.maximum(totals[r], 0.0)
+
+
+def inner_rows(x, fodd, feven, wh, wl):
     rows, cols, chans = x.shape
-    outs = weight.shape[-1]
-    whole = lambda shape: pl.BlockSpec(shape, lambda dx: (0,) * len(shape))
-    taps = pl.BlockSpec((2, 1, chans, outs), lambda dx: (0, dx, 0, 0))
-    split = jax.ShapeDtypeStruct((2, 3, chans, outs), BF16)
+    outs = wh.shape[-1]
+    products = 4 * (rows // 2) - 2
     return pl.pallas_call(
         functools.partial(inner_kernel, chans // 8),
-        grid=(3,),
-        in_specs=[VMEM, VMEM, VMEM, pl.BlockSpec((1, 3, 1, chans, outs), lambda dx: (layer, 0, dx, 0, 0))],
-        out_specs=[whole((rows - 2, cols, outs)), whole((2, cols, outs)), taps, taps],
+        in_specs=[VMEM] * 5,
+        out_specs=[VMEM] * 3,
         out_shape=[
             jax.ShapeDtypeStruct((rows - 2, cols, outs), F32),
             jax.ShapeDtypeStruct((2, cols, outs), F32),
-            split,
-            split,
+            jax.ShapeDtypeStruct((2, cols, chans), F32),
         ],
-        scratch_shapes=[pltpu.VMEM((rows * cols, chans), BF16), pltpu.VMEM((rows * cols, chans), BF16)],
+        scratch_shapes=[
+            pltpu.VMEM((rows, cols, chans), F32),
+            pltpu.VMEM((products * cols, chans), BF16),
+            pltpu.VMEM((products * cols, chans), BF16),
+        ],
         name="inner_rows",
         compiler_params=PARAMS,
-    )(x, fodd, feven, weight)
-
-
-def outer_kernel(fold, rodd_ref, reven_ref, sodd_ref, seven_ref, wh_ref, wl_ref, partial_ref, inner_ref, out_ref):
+    )(x, fodd, feven, wh, wl)
+
+
+def outer_kernel(
+    fold, rodd_ref, reven_ref, sodd_ref, seven_ref, wh_ref, wl_ref, partial_ref, beside_ref, inner_ref, out_ref
+):
     rows, cols, outs = out_ref.shape
     width = 2 * fold
     out_ref[1 : rows - 1] = inner_ref[...]
@@ -234,10 +275,10 @@
             kept = turn(kept_ref[cols:], width - k * width)
             low.append(jnp.where(lane < width, moved, kept))
         halo = jnp.concatenate([jnp.concatenate(low, axis=0), kept_ref[:cols]], axis=1)
-        hi, lo = parts(halo)
+        hi, lo = parts(halo - beside_ref[i])
         total = partial_ref[i]
         for dx in range(3):
-            total = total + shift_columns(dot3(hi, lo, wh_ref[i, dx], wl_ref[i, dx]), dx)
+            total = total + shift_columns(dot3(hi, lo, wh_ref[3 * i, dx], wl_ref[3 * i, dx]), dx)
         out_ref[i * (rows - 1)] = jnp.maximum(total, 0.0)
 
     def both(above, below):
@@ -248,29 +289,31 @@
     by_parity("row", lambda: both(odd, even), lambda: both(even, odd))
 
 
-def outer_rows(rodd, reven, sodd, seven, wh, wl, partial, inner):
+def outer_rows(rodd, reven, sodd, seven, wh, wl, partial, beside, inner):
     rows, cols, outs = inner.shape
     return pl.pallas_call(
         functools.partial(outer_kernel, wh.shape[2] // 8),
-        in_specs=[VMEM] * 8,
+        in_specs=[VMEM] * 9,
         out_specs=VMEM,
         out_shape=jax.ShapeDtypeStruct((rows + 2, cols, outs), F32),
         name="outer_rows",
         compiler_params=PARAMS,
-    )(rodd, reven, sodd, seven, wh, wl, partial, inner)
+    )(rodd, reven, sodd, seven, wh, wl, partial, beside, inner)
 
 
 def local(features, conv_weight):
     frames, rows, cols, chans = features.shape
     field = features.reshape(rows, cols, chans)
+    split, ready = prepare(conv_weight)
     for layer in range(conv_weight.shape[0]):
+        wh, wl = split[2 * layer], split[2 * layer + 1]
         fodd, feven, rodd, reven = send(field)
         fodd, feven = exchange(fodd, "frame", 1), exchange(feven, "frame", 0)
         rodd, reven = exchange(rodd, "row", 1), exchange(reven, "row", 0)
-        sodd, seven = forward(fodd, feven, cols, chans // 8)
+        sodd, seven = forward(fodd, feven, ready, cols, chans // 8)
         sodd, seven = exchange(sodd, "row", 1), exchange(seven, "row", 0)
-        inner, partial, wh, wl = inner_rows(field, fodd, feven, conv_weight, layer)
-        field = outer_rows(rodd, reven, sodd, seven, wh, wl, partial, inner)
+        inner, partial, beside = inner_rows(field, fodd, feven, wh, wl)
+        field = outer_rows(rodd, reven, sodd, seven, wh, wl, partial, beside, inner)
     return field.reshape(features.shape)
 
 

time: 58.1 us -> 54.8 us (0.943)
  the two profiles are of different devices: /device:TPU:26 before, /device:TPU:27 now
where the time goes in v3:
time: 54.8 us; the launch traced here: 54.1 us
  starting transfers between devices  34.3 us (63%)
  Pallas kernels  10.1 us (18%)
  waiting for transfers between devices  6 us (11%)
  local copies, waits for them, and re-layouts  3.56 us (6%)
    ppermute x12, starting transfers between devices, exchange(): return lax.ppermute(block, axis, pairs + [(b, a) for a, b in pairs])  34.3 us
    ppermute x12, waiting for transfers between devices, exchange(): return lax.ppermute(block, axis, pairs + [(b, a) for a, b in pairs])  6 us
    pallas_call x2, Pallas kernels, inner_rows(): pl.pallas_call(functools.partial(inner_kernel, chans // 8), in_specs=[VME...  5.08 us
    unnamed x6, local copies, waits for them, and re-layouts  3.56 us
    pallas_call x2, Pallas kernels, outer_rows(): pl.pallas_call(functools.partial(outer_kernel, wh.shape[2] // 8), in_spec...  2.75 us
    pallas_call x1, Pallas kernels, prepare(): pl.pallas_call(prepare_kernel, in_specs=[VMEM], out_specs=[VMEM] * (2 * l...  1.29 us
  transfers between devices with their start and end apart: 12, of which 4 were waited for; matrix products, arithmetic and copies ran while one was open for 0% of the time, Pallas kernels for 12%

profile of v3, /device:TPU:27, one launch (start us, length us, event | category | flops | bytes accessed | tf_op | source)
XLA Modules:
  0.0 54.1 jit_solution(11197972359700207501)
XLA Ops:
  0.0 0.0 copy-start.1
  0.0 1.2 %copy-done.1 = f32[1,4,256,256]{3,2,1,0:T(8,128)S(1)} copy-done((f32[1,4,256,256]{3,2,1,0:T(8,128)S(1)}, f32[1,4,256,256]{3,2,1,0:T(8,128)}, u32[]{:S(2)}) %copy-start.1) | copy-done | bytes 1048600
  1.2 0.4 send.2
  1.6 9.0 %collective-permute-start.2 = (f32[4,64,128]{2,1,0:T(8,128)S(1)}, f32[4,64,128]{2,1,0:T(8,128)S(1)}, u32[]{:S(2)}, u32[]{:S(2)}) collective-permute-start(f32[4,64,128]{2,1,0:T(8,128)S(1)} %get-tuple-element.30), channel_id=1, source_target_pairs={{16,32},{48,64},{80,96},{112,128},{144,160},{176,192},{208,224},{3... | collective-permute-start | bytes 393224 | tf_op jit(solution)/shard_map/ppermute | solution.py:20
  10.7 0.1 collective-permute-start.3
  10.8 3.5 %collective-permute-start = (f32[384,128]{1,0:T(8,128)S(1)}, f32[384,128]{1,0:T(8,128)S(1)}, u32[]{:S(2)}, u32[]{:S(2)}) collective-permute-start(f32[384,128]{1,0:T(8,128)S(1)} %get-tuple-element.28), channel_id=1, source_target_pairs={{1,2},{3,4},{5,6},{7,8},{9,10},{11,12},{13,14},{2,1},{4,3},{6,5},{... | collective-permute-start | bytes 589832 | tf_op jit(solution)/shard_map/ppermute | solution.py:20
  14.3 0.1 collective-permute-start.1
  14.4 0.0 copy-start
  14.4 2.3 %copy-done = f32[2,3,3,256,256]{4,3,2,1,0:T(8,128)S(1)} copy-done((f32[2,3,3,256,256]{4,3,2,1,0:T(8,128)S(1)}, f32[2,3,3,256,256]{4,3,2,1,0:T(8,128)}, u32[]{:S(2)}) %copy-start) | copy-done | bytes 4718616
  16.7 0.0 copy-start.2
  16.7 1.3 %prepare.1 = (bf16[4,3,256,256]{3,2,1,0:T(8,128)(2,1)S(1)}, bf16[4,3,256,256]{3,2,1,0:T(8,128)(2,1)S(1)}, bf16[4,3,256,256]{3,2,1,0:T(8,128)(2,1)S(1)}, bf16[4,3,256,256]{3,2,1,0:T(8,128)(2,1)S(1)}, f32[8,128]{1,0:T(8,128)S(1)}) custom-call(f32[2,3,3,256,256]{4,3,2,1,0:T(8,128)S(1)} %copy-done), custom_call_target="tpu_custom_call" | custom-call | tf_op jit(solution)/shard_map/prepare/pallas_call | solution.py:176
  18.0 0.0 collective-permute-done.2.fodd_ref
  18.0 0.0 collective-permute-done.3.feven_ref
  18.1 0.1 forward.2
  18.2 4.5 %collective-permute-start.4 = (f32[128,128]{1,0:T(8,128)S(1)}, f32[128,128]{1,0:T(8,128)S(1)}, u32[]{:S(2)}, u32[]{:S(2)}) collective-permute-start(f32[128,128]{1,0:T(8,128)S(1)} %get-tuple-element.33), channel_id=1, source_target_pairs={{1,2},{3,4},{5,6},{7,8},{9,10},{11,12},{13,14},{2,1},{4,3},{6,5},{... | collective-permute-start | bytes 196616 | tf_op jit(solution)/shard_map/ppermute | solution.py:20
  22.6 0.7 %collective-permute-start.5 = (f32[128,128]{1,0:T(8,128)S(1)}, f32[128,128]{1,0:T(8,128)S(1)}, u32[]{:S(2)}, u32[]{:S(2)}) collective-permute-start(f32[128,128]{1,0:T(8,128)S(1)} %get-tuple-element.34), channel_id=1, source_target_pairs={{0,1},{2,3},{4,5},{6,7},{8,9},{10,11},{12,13},{14,15},{1,0},{3,2},... | collective-permute-start | bytes 196616 | tf_op jit(solution)/shard_map/ppermute | solution.py:20
  23.3 0.0 copy-done.2
  23.3 2.5 %inner_rows.2 = (f32[2,256,256]{2,1,0:T(8,128)S(1)}, f32[2,256,256]{2,1,0:T(8,128)S(1)}, f32[2,256,256]{2,1,0:T(8,128)S(1)}) custom-call(f32[4,256,256]{2,1,0:T(8,128)S(1)} %bitcast.3, f32[4,64,128]{2,1,0:T(8,128)S(1)} %collective-permute-done.2.fodd_ref, f32[4,64,128]{2,1,0:T(8,128)S(1)} %collective-permute-done.3.feven_ref, ...), custom_call_target="tpu_custom_call" | custom-call | tf_op jit(solution)/shard_map/inner_rows/pallas_call | solution.py:242
  25.8 0.9 %collective-permute-done.4.sodd_ref = f32[128,128]{1,0:T(8,128)S(1)} collective-permute-done((f32[128,128]{1,0:T(8,128)S(1)}, f32[128,128]{1,0:T(8,128)S(1)}, u32[]{:S(2)}, u32[]{:S(2)}) %collective-permute-start.4) | collective-permute-done | bytes 65568 | tf_op jit(solution)/shard_map/ppermute | solution.py:20
  26.7 0.0 collective-permute-done.5.seven_ref
  26.7 0.0 collective-permute-done.rodd_ref
  26.7 0.0 collective-permute-done.1.reven_ref
  26.7 0.9 %outer_rows.2.x_ref = f32[4,256,256]{2,1,0:T(8,128)S(1)} custom-call(f32[384,128]{1,0:T(8,128)S(1)} %collective-permute-done.rodd_ref, f32[384,128]{1,0:T(8,128)S(1)} %collective-permute-done.1.reven_ref, f32[128,128]{1,0:T(8,128)S(1)} %collective-permute-done.4.sodd_ref, f32[128,128]{1,0:T(8,128)S(1)} %collective-permute-done.5.seven_ref, ...), custom_call_target="tpu_custom_call" | custom-call | tf_op jit(solution)/shard_map/outer_rows/pallas_call | solution.py:294
  27.6 0.4 send.3
  28.0 6.5 %collective-permute-start.8 = (f32[4,64,128]{2,1,0:T(8,128)S(1)}, f32[4,64,128]{2,1,0:T(8,128)S(1)}, u32[]{:S(2)}, u32[]{:S(2)}) collective-permute-start(f32[4,64,128]{2,1,0:T(8,128)S(1)} %get-tuple-element.42), channel_id=1, source_target_pairs={{16,32},{48,64},{80,96},{112,128},{144,160},{176,192},{208,224},{3... | collective-permute-start | bytes 393224 | tf_op jit(solution)/shard_map/ppermute | solution.py:20
  34.5 0.1 collective-permute-start.9
  34.6 4.3 %collective-permute-start.6 = (f32[384,128]{1,0:T(8,128)S(1)}, f32[384,128]{1,0:T(8,128)S(1)}, u32[]{:S(2)}, u32[]{:S(2)}) collective-permute-start(f32[384,128]{1,0:T(8,128)S(1)} %get-tuple-element.40), channel_id=1, source_target_pairs={{1,2},{3,4},{5,6},{7,8},{9,10},{11,12},{13,14},{2,1},{4,3},{6,5},{... | collective-permute-start | bytes 589832 | tf_op jit(solution)/shard_map/ppermute | solution.py:20
  38.9 0.1 collective-permute-start.7
  39.0 1.4 %collective-permute-done.8.fodd_ref = f32[4,64,128]{2,1,0:T(8,128)S(1)} collective-permute-done((f32[4,64,128]{2,1,0:T(8,128)S(1)}, f32[4,64,128]{2,1,0:T(8,128)S(1)}, u32[]{:S(2)}, u32[]{:S(2)}) %collective-permute-start.8) | collective-permute-done | bytes 131104 | tf_op jit(solution)/shard_map/ppermute | solution.py:20
  40.4 0.0 collective-permute-done.9.feven_ref
  40.4 0.1 forward.3
  40.6 3.7 %collective-permute-start.10 = (f32[128,128]{1,0:T(8,128)S(1)}, f32[128,128]{1,0:T(8,128)S(1)}, u32[]{:S(2)}, u32[]{:S(2)}) collective-permute-start(f32[128,128]{1,0:T(8,128)S(1)} %get-tuple-element.44), channel_id=1, source_target_pairs={{1,2},{3,4},{5,6},{7,8},{9,10},{11,12},{13,14},{2,1},{4,3},{6,5},{... | collective-permute-start | bytes 196616 | tf_op jit(solution)/shard_map/ppermute | solution.py:20
  44.3 1.7 %collective-permute-start.11 = (f32[128,128]{1,0:T(8,128)S(1)}, f32[128,128]{1,0:T(8,128)S(1)}, u32[]{:S(2)}, u32[]{:S(2)}) collective-permute-start(f32[128,128]{1,0:T(8,128)S(1)} %get-tuple-element.45), channel_id=1, source_target_pairs={{0,1},{2,3},{4,5},{6,7},{8,9},{10,11},{12,13},{14,15},{1,0},{3,2},... | collective-permute-start | bytes 196616 | tf_op jit(solution)/shard_map/ppermute | solution.py:20
  46.0 2.6 %inner_rows.3 = (f32[2,256,256]{2,1,0:T(8,128)S(1)}, f32[2,256,256]{2,1,0:T(8,128)S(1)}, f32[2,256,256]{2,1,0:T(8,128)S(1)}) custom-call(f32[4,256,256]{2,1,0:T(8,128)S(1)} %outer_rows.2.x_ref, f32[4,64,128]{2,1,0:T(8,128)S(1)} %collective-permute-done.8.fodd_ref, f32[4,64,128]{2,1,0:T(8,128)S(1)} %collective-permute-done.9.feven_ref, ...), custom_call_target="tpu_custom_call" | custom-call | tf_op jit(solution)/shard_map/inner_rows/pallas_call | solution.py:242
  48.6 2.0 %collective-permute-done.10.sodd_ref = f32[128,128]{1,0:T(8,128)S(1)} collective-permute-done((f32[128,128]{1,0:T(8,128)S(1)}, f32[128,128]{1,0:T(8,128)S(1)}, u32[]{:S(2)}, u32[]{:S(2)}) %collective-permute-start.10) | collective-permute-done | bytes 65568 | tf_op jit(solution)/shard_map/ppermute | solution.py:20
  50.6 1.7 %collective-permute-done.11.seven_ref = f32[128,128]{1,0:T(8,128)S(1)} collective-permute-done((f32[128,128]{1,0:T(8,128)S(1)}, f32[128,128]{1,0:T(8,128)S(1)}, u32[]{:S(2)}, u32[]{:S(2)}) %collective-permute-start.11) | collective-permute-done | bytes 65568 | tf_op jit(solution)/shard_map/ppermute | solution.py:20
  52.3 0.0 collective-permute-done.6.rodd_ref
  52.3 0.0 collective-permute-done.7.reven_ref
  52.3 1.8 %outer_rows.3 = f32[4,256,256]{2,1,0:T(8,128)} custom-call(f32[384,128]{1,0:T(8,128)S(1)} %collective-permute-done.6.rodd_ref, f32[384,128]{1,0:T(8,128)S(1)} %collective-permute-done.7.reven_ref, f32[128,128]{1,0:T(8,128)S(1)} %collective-permute-done.10.sodd_ref, f32[128,128]{1,0:T(8,128)S(1)} %collective-permute-done.11.seven_ref, ...), custom_call_target="tpu_custom_call" | custom-call | tf_op jit(solution)/shard_map/outer_rows/pallas_call | solution.py:294
Async XLA Ops:
  0.0 1.2 %copy-start.1 = (f32[1,4,256,256]{3,2,1,0:T(8,128)S(1)}, f32[1,4,256,256]{3,2,1,0:T(8,128)}, u32[]{:S(2)}) copy-start(f32[1,4,256,256]{3,2,1,0:T(8,128)} %param.2) | copy-start | bytes 3145732
  1.6 16.4 %collective-permute-start.2 = (f32[4,64,128]{2,1,0:T(8,128)S(1)}, f32[4,64,128]{2,1,0:T(8,128)S(1)}, u32[]{:S(2)}, u32[]{:S(2)}) collective-permute-start(f32[4,64,128]{2,1,0:T(8,128)S(1)} %get-tuple-element.30), channel_id=1, source_target_pairs={{16,32},{48,64},{80,96},{112,128},{144,160},{176,192},{208,224},{3... | collective-permute-start | bytes 393224 | tf_op jit(solution)/shard_map/ppermute | solution.py:20
  10.7 7.4 %collective-permute-start.3 = (f32[4,64,128]{2,1,0:T(8,128)S(1)}, f32[4,64,128]{2,1,0:T(8,128)S(1)}, u32[]{:S(2)}, u32[]{:S(2)}) collective-permute-start(f32[4,64,128]{2,1,0:T(8,128)S(1)} %get-tuple-element.31), channel_id=1, source_target_pairs={{0,16},{32,48},{64,80},{96,112},{128,144},{160,176},{192,208},{224... | collective-permute-start | bytes 393224 | tf_op jit(solution)/shard_map/ppermute | solution.py:20
  10.8 16.0 %collective-permute-start = (f32[384,128]{1,0:T(8,128)S(1)}, f32[384,128]{1,0:T(8,128)S(1)}, u32[]{:S(2)}, u32[]{:S(2)}) collective-permute-start(f32[384,128]{1,0:T(8,128)S(1)} %get-tuple-element.28), channel_id=1, source_target_pairs={{1,2},{3,4},{5,6},{7,8},{9,10},{11,12},{13,14},{2,1},{4,3},{6,5},{... | collective-permute-start | bytes 589832 | tf_op jit(solution)/shard_map/ppermute | solution.py:20
  14.3 12.4 %collective-permute-start.1 = (f32[384,128]{1,0:T(8,128)S(1)}, f32[384,128]{1,0:T(8,128)S(1)}, u32[]{:S(2)}, u32[]{:S(2)}) collective-permute-start(f32[384,128]{1,0:T(8,128)S(1)} %get-tuple-element.29), channel_id=1, source_target_pairs={{0,1},{2,3},{4,5},{6,7},{8,9},{10,11},{12,13},{14,15},{1,0},{3,2},... | collective-permute-start | bytes 589832 | tf_op jit(solution)/shard_map/ppermute | solution.py:20
  14.4 2.3 %copy-start = (f32[2,3,3,256,256]{4,3,2,1,0:T(8,128)S(1)}, f32[2,3,3,256,256]{4,3,2,1,0:T(8,128)}, u32[]{:S(2)}) copy-start(f32[2,3,3,256,256]{4,3,2,1,0:T(8,128)} %w_ref.1) | copy-start | bytes 14155780
  16.7 6.6 %copy-start.2 = (f32[1,4,256,256]{3,2,1,0:T(8,128)S(1)}, f32[1,4,256,256]{3,2,1,0:T(8,128)}, u32[]{:S(2)}) copy-start(f32[1,4,256,256]{3,2,1,0:T(8,128)} %param.2) | copy-start | bytes 3145732
  18.2 8.5 %collective-permute-start.4 = (f32[128,128]{1,0:T(8,128)S(1)}, f32[128,128]{1,0:T(8,128)S(1)}, u32[]{:S(2)}, u32[]{:S(2)}) collective-permute-start(f32[128,128]{1,0:T(8,128)S(1)} %get-tuple-element.33), channel_id=1, source_target_pairs={{1,2},{3,4},{5,6},{7,8},{9,10},{11,12},{13,14},{2,1},{4,3},{6,5},{... | collective-permute-start | bytes 196616 | tf_op jit(solution)/shard_map/ppermute | solution.py:20
  22.6 4.1 %collective-permute-start.5 = (f32[128,128]{1,0:T(8,128)S(1)}, f32[128,128]{1,0:T(8,128)S(1)}, u32[]{:S(2)}, u32[]{:S(2)}) collective-permute-start(f32[128,128]{1,0:T(8,128)S(1)} %get-tuple-element.34), channel_id=1, source_target_pairs={{0,1},{2,3},{4,5},{6,7},{8,9},{10,11},{12,13},{14,15},{1,0},{3,2},... | collective-permute-start | bytes 196616 | tf_op jit(solution)/shard_map/ppermute | solution.py:20
  28.0 12.4 %collective-permute-start.8 = (f32[4,64,128]{2,1,0:T(8,128)S(1)}, f32[4,64,128]{2,1,0:T(8,128)S(1)}, u32[]{:S(2)}, u32[]{:S(2)}) collective-permute-start(f32[4,64,128]{2,1,0:T(8,128)S(1)} %get-tuple-element.42), channel_id=1, source_target_pairs={{16,32},{48,64},{80,96},{112,128},{144,160},{176,192},{208,224},{3... | collective-permute-start | bytes 393224 | tf_op jit(solution)/shard_map/ppermute | solution.py:20
  34.5 5.9 %collective-permute-start.9 = (f32[4,64,128]{2,1,0:T(8,128)S(1)}, f32[4,64,128]{2,1,0:T(8,128)S(1)}, u32[]{:S(2)}, u32[]{:S(2)}) collective-permute-start(f32[4,64,128]{2,1,0:T(8,128)S(1)} %get-tuple-element.43), channel_id=1, source_target_pairs={{0,16},{32,48},{64,80},{96,112},{128,144},{160,176},{192,208},{224... | collective-permute-start | bytes 393224 | tf_op jit(solution)/shard_map/ppermute | solution.py:20
  34.6 17.6 %collective-permute-start.6 = (f32[384,128]{1,0:T(8,128)S(1)}, f32[384,128]{1,0:T(8,128)S(1)}, u32[]{:S(2)}, u32[]{:S(2)}) collective-permute-start(f32[384,128]{1,0:T(8,128)S(1)} %get-tuple-element.40), channel_id=1, source_target_pairs={{1,2},{3,4},{5,6},{7,8},{9,10},{11,12},{13,14},{2,1},{4,3},{6,5},{... | collective-permute-start | bytes 589832 | tf_op jit(solution)/shard_map/ppermute | solution.py:20
  38.9 13.4 %collective-permute-start.7 = (f32[384,128]{1,0:T(8,128)S(1)}, f32[384,128]{1,0:T(8,128)S(1)}, u32[]{:S(2)}, u32[]{:S(2)}) collective-permute-start(f32[384,128]{1,0:T(8,128)S(1)} %get-tuple-element.41), channel_id=1, source_target_pairs={{0,1},{2,3},{4,5},{6,7},{8,9},{10,11},{12,13},{14,15},{1,0},{3,2},... | collective-permute-start | bytes 589832 | tf_op jit(solution)/shard_map/ppermute | solution.py:20
  40.6 10.0 %collective-permute-start.10 = (f32[128,128]{1,0:T(8,128)S(1)}, f32[128,128]{1,0:T(8,128)S(1)}, u32[]{:S(2)}, u32[]{:S(2)}) collective-permute-start(f32[128,128]{1,0:T(8,128)S(1)} %get-tuple-element.44), channel_id=1, source_target_pairs={{1,2},{3,4},{5,6},{7,8},{9,10},{11,12},{13,14},{2,1},{4,3},{6,5},{... | collective-permute-start | bytes 196616 | tf_op jit(solution)/shard_map/ppermute | solution.py:20
  44.3 8.0 %collective-permute-start.11 = (f32[128,128]{1,0:T(8,128)S(1)}, f32[128,128]{1,0:T(8,128)S(1)}, u32[]{:S(2)}, u32[]{:S(2)}) collective-permute-start(f32[128,128]{1,0:T(8,128)S(1)} %get-tuple-element.45), channel_id=1, source_target_pairs={{0,1},{2,3},{4,5},{6,7},{8,9},{10,11},{12,13},{14,15},{1,0},{3,2},... | collective-permute-start | bytes 196616 | tf_op jit(solution)/shard_map/ppermute | solution.py:20

commit v4 on v3

--- a/solution.py
+++ b/solution.py
@@ -95,40 +95,56 @@
     return jnp.concatenate(pieces, axis=0)
 
 
-def send_kernel(fold, x_ref, fodd_ref, feven_ref, rodd_ref, reven_ref):
-    rows, cols, chans = x_ref.shape
-
-    def frames(to_before, to_following):
-        for r in range(rows):
+def frames_kernel(fold, x_ref, even_ref, odd_ref):
+    def write(to_before, to_following):
+        for r in range(x_ref.shape[0]):
             lanes = x_ref[r, :, :LANES]
             to_before[r] = pack(lanes, 0, fold)
             to_following[r] = pack(lanes, fold, fold)
 
-    def edges(first_to, last_to):
+    by_parity("frame", lambda: write(odd_ref, even_ref), lambda: write(even_ref, odd_ref))
+
+
+def frames_to_send(x):
+    rows, cols, chans = x.shape
+    fold = chans // 8
+    frames = jax.ShapeDtypeStruct((rows, cols * fold // LANES, LANES), F32)
+    return pl.pallas_call(
+        functools.partial(frames_kernel, fold),
+        in_specs=[VMEM],
+        out_specs=[VMEM] * 2,
+        out_shape=[frames, frames],
+        name="frames_to_send",
+        compiler_params=PARAMS,
+    )(x)
+
+
+def rows_kernel(fold, x_ref, even_ref, odd_ref):
+    rows, cols, chans = x_ref.shape
+
+    def write(first_to, last_to):
         for r, out in ((0, first_to), (rows - 1, last_to)):
             out[:cols] = x_ref[r, :, LANES:]
             out[cols:] = pack(x_ref[r, :, :LANES], 2 * fold, LANES - 2 * fold)
 
-    by_parity("frame", lambda: frames(fodd_ref, feven_ref), lambda: frames(feven_ref, fodd_ref))
-    by_parity("row", lambda: edges(rodd_ref, reven_ref), lambda: edges(reven_ref, rodd_ref))
-
-
-def send(x):
+    by_parity("row", lambda: write(odd_ref, even_ref), lambda: write(even_ref, odd_ref))
+
+
+def rows_to_send(x):
     rows, cols, chans = x.shape
     fold = chans // 8
-    frames = jax.ShapeDtypeStruct((rows, cols * fold // LANES, LANES), F32)
     edge = jax.ShapeDtypeStruct((cols * (chans - 2 * fold) // LANES, LANES), F32)
     return pl.pallas_call(
-        functools.partial(send_kernel, fold),
+        functools.partial(rows_kernel, fold),
         in_specs=[VMEM],
-        out_specs=[VMEM] * 4,
-        out_shape=[frames, frames, edge, edge],
-        name="send",
+        out_specs=[VMEM] * 2,
+        out_shape=[edge, edge],
+        name="rows_to_send",
         compiler_params=PARAMS,
     )(x)
 
 
-def forward_kernel(fold, fodd_ref, feven_ref, ready_ref, sodd_ref, seven_ref):
+def forward_kernel(fold, feven_ref, fodd_ref, ready_ref, sodd_ref, seven_ref):
     rows = fodd_ref.shape[0]
 
     def write(following, before, first_to, last_to):
@@ -154,20 +170,24 @@
         out_shape=[edge, edge],
         name="forward",
         compiler_params=PARAMS,
-    )(fodd, feven, ready)
+    )(feven, fodd, ready)
 
 
 def prepare_kernel(w_ref, *refs):
     layers = w_ref.shape[0]
-    for l in range(layers):
-        hi_ref, lo_ref = refs[2 * l], refs[2 * l + 1]
-        for dx in range(3):
-            first, mid, last = w_ref[l, 0, dx], w_ref[l, 1, dx], w_ref[l, 2, dx]
-            ends = 0.5 * (first + last)
-            half = 0.5 * mid
-            for m, value in enumerate((first, ends + half, ends - half, last)):
-                hi_ref[m, dx], lo_ref[m, dx] = parts(value)
-    refs[2 * layers][...] = jnp.zeros_like(refs[2 * layers])
+    outs, (stage, sems) = refs[: 2 * layers + 1], refs[2 * layers + 1 :]
+    order = [(l, dx) for l in range(layers) for dx in range(3)]
+    copies = [pltpu.make_async_copy(w_ref.at[l, :, dx], stage.at[l, dx], sems.at[l, dx]) for l, dx in order]
+    for copy in copies:
+        copy.start()
+    for (l, dx), copy in zip(order, copies):
+        copy.wait()
+        first, mid, last = stage[l, dx, 0], stage[l, dx, 1], stage[l, dx, 2]
+        ends = 0.5 * (first + last)
+        half = 0.5 * mid
+        for m, value in enumerate((first, ends + half, ends - half, last)):
+            outs[2 * l][m, dx], outs[2 * l + 1][m, dx] = parts(value)
+    outs[2 * layers][...] = jnp.zeros_like(outs[2 * layers])
 
 
 def prepare(weight):
@@ -175,16 +195,20 @@
     split = jax.ShapeDtypeStruct((4, 3, chans, outs), BF16)
     *split, ready = pl.pallas_call(
         prepare_kernel,
-        in_specs=[VMEM],
+        in_specs=[pl.BlockSpec(memory_space=pltpu.HBM)],
         out_specs=[VMEM] * (2 * layers + 1),
         out_shape=[split] * (2 * layers) + [jax.ShapeDtypeStruct((8, LANES), F32)],
+        scratch_shapes=[
+            pltpu.VMEM((layers, 3, 3, chans, outs), F32),
+            pltpu.SemaphoreType.DMA((layers, 3)),
+        ],
         name="prepare",
-        compiler_params=PARAMS,
+        compiler_params=pltpu.CompilerParams(vmem_limit_bytes=46 * 2**20),
     )(weight)
     return split, ready
 
 
-def inner_kernel(fold, x_ref, fodd_ref, feven_ref, wh_ref, wl_ref, out_ref, partial_ref, beside_ref, shifted, hi, lo):
+def inner_kernel(fold, x_ref, feven_ref, fodd_ref, wh_ref, wl_ref, out_ref, partial_ref, beside_ref, shifted, hi, lo):
     rows, cols, chans = x_ref.shape
     pairs = rows // 2
 
@@ -255,15 +279,22 @@
         ],
         name="inner_rows",
         compiler_params=PARAMS,
-    )(x, fodd, feven, wh, wl)
+    )(x, feven, fodd, wh, wl)
 
 
 def outer_kernel(
-    fold, rodd_ref, reven_ref, sodd_ref, seven_ref, wh_ref, wl_ref, partial_ref, beside_ref, inner_ref, out_ref
+    fold, reven_ref, rodd_ref, sodd_ref, seven_ref, wh_ref, wl_ref, partial_ref, beside_ref, inner_ref, out_ref, *scratch
 ):
     rows, cols, outs = out_ref.shape
     width = 2 * fold
-    out_ref[1 : rows - 1] = inner_ref[...]
+    edges = (0, rows - 1)
+    if scratch:
+        stage, sems = scratch
+        copies = [pltpu.make_async_copy(stage.at[i], out_ref.at[r], sems.at[i]) for i, r in enumerate(edges)]
+        copies.append(pltpu.make_async_copy(inner_ref, out_ref.at[1 : rows - 1], sems.at[2]))
+        copies[2].start()
+    else:
+        out_ref[1 : rows - 1] = inner_ref[...]
 
     def finish(i, kept_ref, moved_ref):
         halves = LANES // width
@@ -279,7 +310,12 @@
         total = partial_ref[i]
         for dx in range(3):
             total = total + shift_columns(dot3(hi, lo, wh_ref[3 * i, dx], wl_ref[3 * i, dx]), dx)
-        out_ref[i * (rows - 1)] = jnp.maximum(total, 0.0)
+        total = jnp.maximum(total, 0.0)
+        if scratch:
+            stage[i] = total
+            copies[i].start()
+        else:
+            out_ref[edges[i]] = total
 
     def both(above, below):
         finish(0, *above)
@@ -287,33 +323,40 @@
 
     odd, even = (rodd_ref, sodd_ref), (reven_ref, seven_ref)
     by_parity("row", lambda: both(odd, even), lambda: both(even, odd))
-
-
-def outer_rows(rodd, reven, sodd, seven, wh, wl, partial, beside, inner):
+    if scratch:
+        for copy in copies:
+            copy.wait()
+
+
+def outer_rows(reven, rodd, sodd, seven, wh, wl, partial, beside, inner, resident):
     rows, cols, outs = inner.shape
+    stage = [pltpu.VMEM((2, cols, outs), F32), pltpu.SemaphoreType.DMA((3,))]
     return pl.pallas_call(
         functools.partial(outer_kernel, wh.shape[2] // 8),
         in_specs=[VMEM] * 9,
-        out_specs=VMEM,
+        out_specs=VMEM if resident else pl.BlockSpec(memory_space=pltpu.HBM),
         out_shape=jax.ShapeDtypeStruct((rows + 2, cols, outs), F32),
+        scratch_shapes=[] if resident else stage,
         name="outer_rows",
         compiler_params=PARAMS,
-    )(rodd, reven, sodd, seven, wh, wl, partial, beside, inner)
+    )(reven, rodd, sodd, seven, wh, wl, partial, beside, inner)
 
 
 def local(features, conv_weight):
     frames, rows, cols, chans = features.shape
+    layers = conv_weight.shape[0]
     field = features.reshape(rows, cols, chans)
     split, ready = prepare(conv_weight)
-    for layer in range(conv_weight.shape[0]):
+    for layer in range(layers):
         wh, wl = split[2 * layer], split[2 * layer + 1]
-        fodd, feven, rodd, reven = send(field)
-        fodd, feven = exchange(fodd, "frame", 1), exchange(feven, "frame", 0)
-        rodd, reven = exchange(rodd, "row", 1), exchange(reven, "row", 0)
+        feven, fodd = frames_to_send(field)
+        feven, fodd = exchange(feven, "frame", 0), exchange(fodd, "frame", 1)
+        reven, rodd = rows_to_send(field)
+        reven, rodd = exchange(reven, "row", 0), exchange(rodd, "row", 1)
         sodd, seven = forward(fodd, feven, ready, cols, chans // 8)
         sodd, seven = exchange(sodd, "row", 1), exchange(seven, "row", 0)
         inner, partial, beside = inner_rows(field, fodd, feven, wh, wl)
-        field = outer_rows(rodd, reven, sodd, seven, wh, wl, partial, beside, inner)
+        field = outer_rows(reven, rodd, sodd, seven, wh, wl, partial, beside, inner, layer < layers - 1)
     return field.reshape(features.shape)
 
 

time: 54.8 us -> 51.4 us (0.938)
  starting transfers between devices: 34.3 us -> 31.1 us
  local copies, waits for them, and re-layouts: 3.56 us -> 1.23 us
  waiting for transfers between devices: 6 us -> 7.26 us
  Pallas kernels: 10.1 us -> 11.2 us
    ppermute x12, starting transfers between devices: 34.3 us -> 31.1 us  [exchange(): return lax.ppermute(block, axis, pairs + [(b, a) for a, b in pairs])]
    unnamed x6 -> x4, local copies, waits for them, and re-layouts: 3.56 us -> 1.23 us
    pallas_call x3 -> x5, Pallas kernels: 2.06 us -> 3.36 us  [the longest x1 2.58 us: prepare(): pl.pallas_call(prepare_kernel, in_specs=[pl.BlockSpec(memory_space=pltpu....]
    ppermute x12, waiting for transfers between devices: 6 us -> 7.26 us  [exchange(): return lax.ppermute(block, axis, pairs + [(b, a) for a, b in pairs])]
  transfers between devices with their start and end apart: 12 -> 12, of which waited for: 4 -> 4; matrix products, arithmetic and copies ran while one was open for 0% -> 0% of each run, Pallas kernels for 12% -> 16%
where the time goes in v4:
time: 51.4 us; the launch traced here: 51.1 us
  starting transfers between devices  31.1 us (61%)
  Pallas kernels  11.2 us (22%)
  waiting for transfers between devices  7.26 us (14%)
  local copies, waits for them, and re-layouts  1.23 us (2%)
    ppermute x12, starting transfers between devices, exchange(): return lax.ppermute(block, axis, pairs + [(b, a) for a, b in pairs])  31.1 us
    ppermute x12, waiting for transfers between devices, exchange(): return lax.ppermute(block, axis, pairs + [(b, a) for a, b in pairs])  7.26 us
    pallas_call x2, Pallas kernels, inner_rows(): pl.pallas_call(functools.partial(inner_kernel, chans // 8), in_specs=[VME...  5.12 us
    pallas_call x1, Pallas kernels, prepare(): pl.pallas_call(prepare_kernel, in_specs=[pl.BlockSpec(memory_space=pltpu....  2.58 us
    pallas_call x2, Pallas kernels, outer_rows(): pl.pallas_call(functools.partial(outer_kernel, wh.shape[2] // 8), in_spec...  2.45 us
    unnamed x4, local copies, waits for them, and re-layouts  1.23 us
  transfers between devices with their start and end apart: 12, of which 4 were waited for; matrix products, arithmetic and copies ran while one was open for 0% of the time, Pallas kernels for 16%

profile of v4, /device:TPU:27, one launch (start us, length us, event | category | flops | bytes accessed | tf_op | source)
XLA Modules:
  0.0 51.1 jit_solution(16458392065683536482)
XLA Ops:
  0.0 0.0 copy-start
  0.0 1.2 %copy-done = f32[1,4,256,256]{3,2,1,0:T(8,128)S(1)} copy-done((f32[1,4,256,256]{3,2,1,0:T(8,128)S(1)}, f32[1,4,256,256]{3,2,1,0:T(8,128)}, u32[]{:S(2)}) %copy-start) | copy-done | bytes 1048600
  1.2 0.3 frames_to_send.2
  1.5 0.8 %collective-permute-start.2 = (f32[4,64,128]{2,1,0:T(8,128)S(1)}, f32[4,64,128]{2,1,0:T(8,128)S(1)}, u32[]{:S(2)}, u32[]{:S(2)}) collective-permute-start(f32[4,64,128]{2,1,0:T(8,128)S(1)} %get-tuple-element.30), channel_id=1, source_target_pairs={{0,16},{32,48},{64,80},{96,112},{128,144},{160,176},{192,208},{224... | collective-permute-start | bytes 393224 | tf_op jit(solution)/shard_map/ppermute | solution.py:20
  2.3 8.4 %collective-permute-start.3 = (f32[4,64,128]{2,1,0:T(8,128)S(1)}, f32[4,64,128]{2,1,0:T(8,128)S(1)}, u32[]{:S(2)}, u32[]{:S(2)}) collective-permute-start(f32[4,64,128]{2,1,0:T(8,128)S(1)} %get-tuple-element.31), channel_id=1, source_target_pairs={{16,32},{48,64},{80,96},{112,128},{144,160},{176,192},{208,224},{3... | collective-permute-start | bytes 393224 | tf_op jit(solution)/shard_map/ppermute | solution.py:20
  10.7 0.1 rows_to_send.2
  10.8 0.8 %collective-permute-start = (f32[384,128]{1,0:T(8,128)S(1)}, f32[384,128]{1,0:T(8,128)S(1)}, u32[]{:S(2)}, u32[]{:S(2)}) collective-permute-start(f32[384,128]{1,0:T(8,128)S(1)} %get-tuple-element.28), channel_id=1, source_target_pairs={{0,1},{2,3},{4,5},{6,7},{8,9},{10,11},{12,13},{14,15},{1,0},{3,2},... | collective-permute-start | bytes 589832 | tf_op jit(solution)/shard_map/ppermute | solution.py:20
  11.6 0.0 copy-start.1
  11.6 3.6 %collective-permute-start.1 = (f32[384,128]{1,0:T(8,128)S(1)}, f32[384,128]{1,0:T(8,128)S(1)}, u32[]{:S(2)}, u32[]{:S(2)}) collective-permute-start(f32[384,128]{1,0:T(8,128)S(1)} %get-tuple-element.29), channel_id=1, source_target_pairs={{1,2},{3,4},{5,6},{7,8},{9,10},{11,12},{13,14},{2,1},{4,3},{6,5},{... | collective-permute-start | bytes 589832 | tf_op jit(solution)/shard_map/ppermute | solution.py:20
  15.2 2.6 %prepare.1 = (bf16[4,3,256,256]{3,2,1,0:T(8,128)(2,1)S(1)}, bf16[4,3,256,256]{3,2,1,0:T(8,128)(2,1)S(1)}, bf16[4,3,256,256]{3,2,1,0:T(8,128)(2,1)S(1)}, bf16[4,3,256,256]{3,2,1,0:T(8,128)(2,1)S(1)}, f32[8,128]{1,0:T(8,128)S(1)}) custom-call(f32[2,3,3,256,256]{4,3,2,1,0:T(8,128)} %w_ref.1), custom_call_target="tpu_custom_call" | custom-call | tf_op jit(solution)/shard_map/prepare/pallas_call | solution.py:196
  17.8 0.0 collective-permute-done.2.feven_ref
  17.8 0.0 collective-permute-done.3.fodd_ref
  17.9 0.1 forward.2
  18.0 4.5 %collective-permute-start.4 = (f32[128,128]{1,0:T(8,128)S(1)}, f32[128,128]{1,0:T(8,128)S(1)}, u32[]{:S(2)}, u32[]{:S(2)}) collective-permute-start(f32[128,128]{1,0:T(8,128)S(1)} %get-tuple-element.33), channel_id=1, source_target_pairs={{1,2},{3,4},{5,6},{7,8},{9,10},{11,12},{13,14},{2,1},{4,3},{6,5},{... | collective-permute-start | bytes 196616 | tf_op jit(solution)/shard_map/ppermute | solution.py:20
  22.5 0.1 collective-permute-start.5
  22.6 0.0 copy-done.1
  22.6 2.5 %inner_rows.2 = (f32[2,256,256]{2,1,0:T(8,128)S(1)}, f32[2,256,256]{2,1,0:T(8,128)S(1)}, f32[2,256,256]{2,1,0:T(8,128)S(1)}) custom-call(f32[4,256,256]{2,1,0:T(8,128)S(1)} %bitcast.4, f32[4,64,128]{2,1,0:T(8,128)S(1)} %collective-permute-done.2.feven_ref, f32[4,64,128]{2,1,0:T(8,128)S(1)} %collective-permute-done.3.fodd_ref, ...), custom_call_target="tpu_custom_call" | custom-call | tf_op jit(solution)/shard_map/inner_rows/pallas_call | solution.py:266
  25.1 0.7 %collective-permute-done.4.sodd_ref = f32[128,128]{1,0:T(8,128)S(1)} collective-permute-done((f32[128,128]{1,0:T(8,128)S(1)}, f32[128,128]{1,0:T(8,128)S(1)}, u32[]{:S(2)}, u32[]{:S(2)}) %collective-permute-start.4) | collective-permute-done | bytes 65568 | tf_op jit(solution)/shard_map/ppermute | solution.py:20
  25.8 0.6 %collective-permute-done.5.seven_ref = f32[128,128]{1,0:T(8,128)S(1)} collective-permute-done((f32[128,128]{1,0:T(8,128)S(1)}, f32[128,128]{1,0:T(8,128)S(1)}, u32[]{:S(2)}, u32[]{:S(2)}) %collective-permute-start.5) | collective-permute-done | bytes 65568 | tf_op jit(solution)/shard_map/ppermute | solution.py:20
  26.4 0.0 collective-permute-done.reven_ref
  26.4 0.0 collective-permute-done.1.rodd_ref
  26.4 0.9 %outer_rows.2.x_ref = f32[4,256,256]{2,1,0:T(8,128)S(1)} custom-call(f32[384,128]{1,0:T(8,128)S(1)} %collective-permute-done.reven_ref, f32[384,128]{1,0:T(8,128)S(1)} %collective-permute-done.1.rodd_ref, f32[128,128]{1,0:T(8,128)S(1)} %collective-permute-done.4.sodd_ref, f32[128,128]{1,0:T(8,128)S(1)} %collective-permute-done.5.seven_ref, ...), custom_call_target="tpu_custom_call" | custom-call | tf_op jit(solution)/shard_map/outer_rows/pallas_call | solution.py:334
  27.3 0.3 frames_to_send.3
  27.6 0.1 collective-permute-start.8
  27.7 6.7 %collective-permute-start.9 = (f32[4,64,128]{2,1,0:T(8,128)S(1)}, f32[4,64,128]{2,1,0:T(8,128)S(1)}, u32[]{:S(2)}, u32[]{:S(2)}) collective-permute-start(f32[4,64,128]{2,1,0:T(8,128)S(1)} %get-tuple-element.43), channel_id=1, source_target_pairs={{16,32},{48,64},{80,96},{112,128},{144,160},{176,192},{208,224},{3... | collective-permute-start | bytes 393224 | tf_op jit(solution)/shard_map/ppermute | solution.py:20
  34.4 0.1 rows_to_send.3
  34.5 1.1 %collective-permute-start.6 = (f32[384,128]{1,0:T(8,128)S(1)}, f32[384,128]{1,0:T(8,128)S(1)}, u32[]{:S(2)}, u32[]{:S(2)}) collective-permute-start(f32[384,128]{1,0:T(8,128)S(1)} %get-tuple-element.40), channel_id=1, source_target_pairs={{0,1},{2,3},{4,5},{6,7},{8,9},{10,11},{12,13},{14,15},{1,0},{3,2},... | collective-permute-start | bytes 589832 | tf_op jit(solution)/shard_map/ppermute | solution.py:20
  35.6 2.4 %collective-permute-start.7 = (f32[384,128]{1,0:T(8,128)S(1)}, f32[384,128]{1,0:T(8,128)S(1)}, u32[]{:S(2)}, u32[]{:S(2)}) collective-permute-start(f32[384,128]{1,0:T(8,128)S(1)} %get-tuple-element.41), channel_id=1, source_target_pairs={{1,2},{3,4},{5,6},{7,8},{9,10},{11,12},{13,14},{2,1},{4,3},{6,5},{... | collective-permute-start | bytes 589832 | tf_op jit(solution)/shard_map/ppermute | solution.py:20
  38.0 0.0 collective-permute-done.8.feven_ref
  38.0 3.5 %collective-permute-done.9.fodd_ref = f32[4,64,128]{2,1,0:T(8,128)S(1)} collective-permute-done((f32[4,64,128]{2,1,0:T(8,128)S(1)}, f32[4,64,128]{2,1,0:T(8,128)S(1)}, u32[]{:S(2)}, u32[]{:S(2)}) %collective-permute-start.9) | collective-permute-done | bytes 131104 | tf_op jit(solution)/shard_map/ppermute | solution.py:20
  41.5 0.1 forward.3
  41.6 2.5 %collective-permute-start.10 = (f32[128,128]{1,0:T(8,128)S(1)}, f32[128,128]{1,0:T(8,128)S(1)}, u32[]{:S(2)}, u32[]{:S(2)}) collective-permute-start(f32[128,128]{1,0:T(8,128)S(1)} %get-tuple-element.44), channel_id=1, source_target_pairs={{1,2},{3,4},{5,6},{7,8},{9,10},{11,12},{13,14},{2,1},{4,3},{6,5},{... | collective-permute-start | bytes 196616 | tf_op jit(solution)/shard_map/ppermute | solution.py:20
  44.2 0.1 collective-permute-start.11
  44.3 2.6 %inner_rows.3 = (f32[2,256,256]{2,1,0:T(8,128)S(1)}, f32[2,256,256]{2,1,0:T(8,128)S(1)}, f32[2,256,256]{2,1,0:T(8,128)S(1)}) custom-call(f32[4,256,256]{2,1,0:T(8,128)S(1)} %outer_rows.2.x_ref, f32[4,64,128]{2,1,0:T(8,128)S(1)} %collective-permute-done.8.feven_ref, f32[4,64,128]{2,1,0:T(8,128)S(1)} %collective-permute-done.9.fodd_ref, ...), custom_call_target="tpu_custom_call" | custom-call | tf_op jit(solution)/shard_map/inner_rows/pallas_call | solution.py:266
  46.9 2.4 %collective-permute-done.10.sodd_ref = f32[128,128]{1,0:T(8,128)S(1)} collective-permute-done((f32[128,128]{1,0:T(8,128)S(1)}, f32[128,128]{1,0:T(8,128)S(1)}, u32[]{:S(2)}, u32[]{:S(2)}) %collective-permute-start.10) | collective-permute-done | bytes 65568 | tf_op jit(solution)/shard_map/ppermute | solution.py:20
  49.4 0.0 collective-permute-done.11.seven_ref
  49.4 0.0 collective-permute-done.6.reven_ref
  49.4 0.0 collective-permute-done.7.rodd_ref
  49.4 1.6 %outer_rows.3 = f32[4,256,256]{2,1,0:T(8,128)} custom-call(f32[384,128]{1,0:T(8,128)S(1)} %collective-permute-done.6.reven_ref, f32[384,128]{1,0:T(8,128)S(1)} %collective-permute-done.7.rodd_ref, f32[128,128]{1,0:T(8,128)S(1)} %collective-permute-done.10.sodd_ref, f32[128,128]{1,0:T(8,128)S(1)} %collective-permute-done.11.seven_ref, ...), custom_call_target="tpu_custom_call" | custom-call | tf_op jit(solution)/shard_map/outer_rows/pallas_call | solution.py:334
Async XLA Ops:
  0.0 1.2 %copy-start = (f32[1,4,256,256]{3,2,1,0:T(8,128)S(1)}, f32[1,4,256,256]{3,2,1,0:T(8,128)}, u32[]{:S(2)}) copy-start(f32[1,4,256,256]{3,2,1,0:T(8,128)} %param.2) | copy-start | bytes 3145732
  1.5 16.3 %collective-permute-start.2 = (f32[4,64,128]{2,1,0:T(8,128)S(1)}, f32[4,64,128]{2,1,0:T(8,128)S(1)}, u32[]{:S(2)}, u32[]{:S(2)}) collective-permute-start(f32[4,64,128]{2,1,0:T(8,128)S(1)} %get-tuple-element.30), channel_id=1, source_target_pairs={{0,16},{32,48},{64,80},{96,112},{128,144},{160,176},{192,208},{224... | collective-permute-start | bytes 393224 | tf_op jit(solution)/shard_map/ppermute | solution.py:20
  2.3 15.6 %collective-permute-start.3 = (f32[4,64,128]{2,1,0:T(8,128)S(1)}, f32[4,64,128]{2,1,0:T(8,128)S(1)}, u32[]{:S(2)}, u32[]{:S(2)}) collective-permute-start(f32[4,64,128]{2,1,0:T(8,128)S(1)} %get-tuple-element.31), channel_id=1, source_target_pairs={{16,32},{48,64},{80,96},{112,128},{144,160},{176,192},{208,224},{3... | collective-permute-start | bytes 393224 | tf_op jit(solution)/shard_map/ppermute | solution.py:20
  10.8 15.6 %collective-permute-start = (f32[384,128]{1,0:T(8,128)S(1)}, f32[384,128]{1,0:T(8,128)S(1)}, u32[]{:S(2)}, u32[]{:S(2)}) collective-permute-start(f32[384,128]{1,0:T(8,128)S(1)} %get-tuple-element.28), channel_id=1, source_target_pairs={{0,1},{2,3},{4,5},{6,7},{8,9},{10,11},{12,13},{14,15},{1,0},{3,2},... | collective-permute-start | bytes 589832 | tf_op jit(solution)/shard_map/ppermute | solution.py:20
  11.6 11.0 %copy-start.1 = (f32[1,4,256,256]{3,2,1,0:T(8,128)S(1)}, f32[1,4,256,256]{3,2,1,0:T(8,128)}, u32[]{:S(2)}) copy-start(f32[1,4,256,256]{3,2,1,0:T(8,128)} %param.2) | copy-start | bytes 3145732
  11.6 14.8 %collective-permute-start.1 = (f32[384,128]{1,0:T(8,128)S(1)}, f32[384,128]{1,0:T(8,128)S(1)}, u32[]{:S(2)}, u32[]{:S(2)}) collective-permute-start(f32[384,128]{1,0:T(8,128)S(1)} %get-tuple-element.29), channel_id=1, source_target_pairs={{1,2},{3,4},{5,6},{7,8},{9,10},{11,12},{13,14},{2,1},{4,3},{6,5},{... | collective-permute-start | bytes 589832 | tf_op jit(solution)/shard_map/ppermute | solution.py:20
  18.0 7.8 %collective-permute-start.4 = (f32[128,128]{1,0:T(8,128)S(1)}, f32[128,128]{1,0:T(8,128)S(1)}, u32[]{:S(2)}, u32[]{:S(2)}) collective-permute-start(f32[128,128]{1,0:T(8,128)S(1)} %get-tuple-element.33), channel_id=1, source_target_pairs={{1,2},{3,4},{5,6},{7,8},{9,10},{11,12},{13,14},{2,1},{4,3},{6,5},{... | collective-permute-start | bytes 196616 | tf_op jit(solution)/shard_map/ppermute | solution.py:20
  22.5 3.9 %collective-permute-start.5 = (f32[128,128]{1,0:T(8,128)S(1)}, f32[128,128]{1,0:T(8,128)S(1)}, u32[]{:S(2)}, u32[]{:S(2)}) collective-permute-start(f32[128,128]{1,0:T(8,128)S(1)} %get-tuple-element.34), channel_id=1, source_target_pairs={{0,1},{2,3},{4,5},{6,7},{8,9},{10,11},{12,13},{14,15},{1,0},{3,2},... | collective-permute-start | bytes 196616 | tf_op jit(solution)/shard_map/ppermute | solution.py:20
  27.6 10.4 %collective-permute-start.8 = (f32[4,64,128]{2,1,0:T(8,128)S(1)}, f32[4,64,128]{2,1,0:T(8,128)S(1)}, u32[]{:S(2)}, u32[]{:S(2)}) collective-permute-start(f32[4,64,128]{2,1,0:T(8,128)S(1)} %get-tuple-element.42), channel_id=1, source_target_pairs={{0,16},{32,48},{64,80},{96,112},{128,144},{160,176},{192,208},{224... | collective-permute-start | bytes 393224 | tf_op jit(solution)/shard_map/ppermute | solution.py:20
  27.7 13.9 %collective-permute-start.9 = (f32[4,64,128]{2,1,0:T(8,128)S(1)}, f32[4,64,128]{2,1,0:T(8,128)S(1)}, u32[]{:S(2)}, u32[]{:S(2)}) collective-permute-start(f32[4,64,128]{2,1,0:T(8,128)S(1)} %get-tuple-element.43), channel_id=1, source_target_pairs={{16,32},{48,64},{80,96},{112,128},{144,160},{176,192},{208,224},{3... | collective-permute-start | bytes 393224 | tf_op jit(solution)/shard_map/ppermute | solution.py:20
  34.5 14.8 %collective-permute-start.6 = (f32[384,128]{1,0:T(8,128)S(1)}, f32[384,128]{1,0:T(8,128)S(1)}, u32[]{:S(2)}, u32[]{:S(2)}) collective-permute-start(f32[384,128]{1,0:T(8,128)S(1)} %get-tuple-element.40), channel_id=1, source_target_pairs={{0,1},{2,3},{4,5},{6,7},{8,9},{10,11},{12,13},{14,15},{1,0},{3,2},... | collective-permute-start | bytes 589832 | tf_op jit(solution)/shard_map/ppermute | solution.py:20
  35.6 13.7 %collective-permute-start.7 = (f32[384,128]{1,0:T(8,128)S(1)}, f32[384,128]{1,0:T(8,128)S(1)}, u32[]{:S(2)}, u32[]{:S(2)}) collective-permute-start(f32[384,128]{1,0:T(8,128)S(1)} %get-tuple-element.41), channel_id=1, source_target_pairs={{1,2},{3,4},{5,6},{7,8},{9,10},{11,12},{13,14},{2,1},{4,3},{6,5},{... | collective-permute-start | bytes 589832 | tf_op jit(solution)/shard_map/ppermute | solution.py:20
  41.6 7.7 %collective-permute-start.10 = (f32[128,128]{1,0:T(8,128)S(1)}, f32[128,128]{1,0:T(8,128)S(1)}, u32[]{:S(2)}, u32[]{:S(2)}) collective-permute-start(f32[128,128]{1,0:T(8,128)S(1)} %get-tuple-element.44), channel_id=1, source_target_pairs={{1,2},{3,4},{5,6},{7,8},{9,10},{11,12},{13,14},{2,1},{4,3},{6,5},{... | collective-permute-start | bytes 196616 | tf_op jit(solution)/shard_map/ppermute | solution.py:20
  44.2 5.2 %collective-permute-start.11 = (f32[128,128]{1,0:T(8,128)S(1)}, f32[128,128]{1,0:T(8,128)S(1)}, u32[]{:S(2)}, u32[]{:S(2)}) collective-permute-start(f32[128,128]{1,0:T(8,128)S(1)} %get-tuple-element.45), channel_id=1, source_target_pairs={{0,1},{2,3},{4,5},{6,7},{8,9},{10,11},{12,13},{14,15},{1,0},{3,2},... | collective-permute-start | bytes 196616 | tf_op jit(solution)/shard_map/ppermute | solution.py:20

commit v5 on v4

--- a/solution.py
+++ b/solution.py
@@ -105,9 +105,8 @@
     by_parity("frame", lambda: write(odd_ref, even_ref), lambda: write(even_ref, odd_ref))
 
 
-def frames_to_send(x):
-    rows, cols, chans = x.shape
-    fold = chans // 8
+def frames_to_send(x, fold):
+    rows, cols, _ = x.shape
     frames = jax.ShapeDtypeStruct((rows, cols * fold // LANES, LANES), F32)
     return pl.pallas_call(
         functools.partial(frames_kernel, fold),
@@ -173,39 +172,32 @@
     )(feven, fodd, ready)
 
 
-def prepare_kernel(w_ref, *refs):
-    layers = w_ref.shape[0]
-    outs, (stage, sems) = refs[: 2 * layers + 1], refs[2 * layers + 1 :]
-    order = [(l, dx) for l in range(layers) for dx in range(3)]
-    copies = [pltpu.make_async_copy(w_ref.at[l, :, dx], stage.at[l, dx], sems.at[l, dx]) for l, dx in order]
+def prepare_kernel(layer, w_ref, after_ref, hi_ref, lo_ref, ready_ref, stage, sems):
+    copies = [pltpu.make_async_copy(w_ref.at[layer, :, dx], stage.at[dx], sems.at[dx]) for dx in range(3)]
     for copy in copies:
         copy.start()
-    for (l, dx), copy in zip(order, copies):
+    for dx, copy in enumerate(copies):
         copy.wait()
-        first, mid, last = stage[l, dx, 0], stage[l, dx, 1], stage[l, dx, 2]
+        first, mid, last = stage[dx, 0], stage[dx, 1], stage[dx, 2]
         ends = 0.5 * (first + last)
         half = 0.5 * mid
         for m, value in enumerate((first, ends + half, ends - half, last)):
-            outs[2 * l][m, dx], outs[2 * l + 1][m, dx] = parts(value)
-    outs[2 * layers][...] = jnp.zeros_like(outs[2 * layers])
-
-
-def prepare(weight):
-    layers, _, _, chans, outs = weight.shape
+            hi_ref[m, dx], lo_ref[m, dx] = parts(value)
+    ready_ref[...] = jnp.zeros_like(ready_ref)
+
+
+def prepare(weight, layer, after):
+    _, _, _, chans, outs = weight.shape
     split = jax.ShapeDtypeStruct((4, 3, chans, outs), BF16)
-    *split, ready = pl.pallas_call(
-        prepare_kernel,
-        in_specs=[pl.BlockSpec(memory_space=pltpu.HBM)],
-        out_specs=[VMEM] * (2 * layers + 1),
-        out_shape=[split] * (2 * layers) + [jax.ShapeDtypeStruct((8, LANES), F32)],
-        scratch_shapes=[
-            pltpu.VMEM((layers, 3, 3, chans, outs), F32),
-            pltpu.SemaphoreType.DMA((layers, 3)),
-        ],
+    return pl.pallas_call(
+        functools.partial(prepare_kernel, layer),
+        in_specs=[pl.BlockSpec(memory_space=pltpu.HBM), VMEM],
+        out_specs=[VMEM] * 3,
+        out_shape=[split, split, jax.ShapeDtypeStruct((8, LANES), F32)],
+        scratch_shapes=[pltpu.VMEM((3, 3, chans, outs), F32), pltpu.SemaphoreType.DMA((3,))],
         name="prepare",
-        compiler_params=pltpu.CompilerParams(vmem_limit_bytes=46 * 2**20),
-    )(weight)
-    return split, ready
+        compiler_params=pltpu.CompilerParams(vmem_limit_bytes=49 * 2**20),
+    )(weight, after)
 
 
 def inner_kernel(fold, x_ref, feven_ref, fodd_ref, wh_ref, wl_ref, out_ref, partial_ref, beside_ref, shifted, hi, lo):
@@ -346,11 +338,10 @@
     frames, rows, cols, chans = features.shape
     layers = conv_weight.shape[0]
     field = features.reshape(rows, cols, chans)
-    split, ready = prepare(conv_weight)
     for layer in range(layers):
-        wh, wl = split[2 * layer], split[2 * layer + 1]
-        feven, fodd = frames_to_send(field)
+        feven, fodd = frames_to_send(field if layer else lax.slice_in_dim(field, 0, LANES, axis=2), chans // 8)
         feven, fodd = exchange(feven, "frame", 0), exchange(fodd, "frame", 1)
+        wh, wl, ready = prepare(conv_weight, layer, feven)
         reven, rodd = rows_to_send(field)
         reven, rodd = exchange(reven, "row", 0), exchange(rodd, "row", 1)
         sodd, seven = forward(fodd, feven, ready, cols, chans // 8)

time: 51.4 us -> 51.2 us (level)
  waiting for transfers between devices: 7.26 us -> 2.6 us
  starting transfers between devices: 31.1 us -> 34.6 us
  Pallas kernels: 11.2 us -> 12.2 us
    ppermute x12, waiting for transfers between devices: 7.26 us -> 2.6 us  [exchange(): return lax.ppermute(block, axis, pairs + [(b, a) for a, b in pairs])]
    ppermute x12, starting transfers between devices: 31.1 us -> 34.6 us  [exchange(): return lax.ppermute(block, axis, pairs + [(b, a) for a, b in pairs])]
    unnamed x4 -> x2, local copies, waits for them, and re-layouts: 1.23 us -> 0.01 us
    slice x0 -> x1, local copies, waits for them, and re-layouts: none -> 1.16 us  [local(): lax.slice_in_dim(field, 0, LANES, axis=2)]
    pallas_call x1 -> x2, Pallas kernels: 2.58 us -> 3.68 us  [prepare(): pl.pallas_call(functools.partial(prepare_kernel, layer), in_specs=[pl.Blo...]
  transfers between devices with their start and end apart: 12 -> 12, of which waited for: 4 -> 4; matrix products, arithmetic and copies ran while one was open for 0% -> 0% of each run, Pallas kernels for 16% -> 18%
where the time goes in v5:
time: 51.2 us; the launch traced here: 50.9 us
  starting transfers between devices  34.6 us (68%)
  Pallas kernels  12.2 us (24%)
  waiting for transfers between devices  2.6 us (5%)
  local copies, waits for them, and re-layouts  1.17 us (2%)
    ppermute x12, starting transfers between devices, exchange(): return lax.ppermute(block, axis, pairs + [(b, a) for a, b in pairs])  34.6 us
    pallas_call x2, Pallas kernels, inner_rows(): pl.pallas_call(functools.partial(inner_kernel, chans // 8), in_specs=[VME...  5 us
    pallas_call x2, Pallas kernels, prepare(): pl.pallas_call(functools.partial(prepare_kernel, layer), in_specs=[pl.Blo...  3.68 us
    ppermute x12, waiting for transfers between devices, exchange(): return lax.ppermute(block, axis, pairs + [(b, a) for a, b in pairs])  2.6 us
    pallas_call x2, Pallas kernels, outer_rows(): pl.pallas_call(functools.partial(outer_kernel, wh.shape[2] // 8), in_spec...  2.48 us
    slice x1, local copies, waits for them, and re-layouts, local(): lax.slice_in_dim(field, 0, LANES, axis=2)  1.16 us
  transfers between devices with their start and end apart: 12, of which 4 were waited for; matrix products, arithmetic and copies ran while one was open for 0% of the time, Pallas kernels for 18%

profile of v5, /device:TPU:27, one launch (start us, length us, event | category | flops | bytes accessed | tf_op | source)
XLA Modules:
  0.0 50.9 jit_solution(625930111612113826)
XLA Ops:
  0.0 0.0 copy-start
  0.0 1.2 %slice.4.x_ref = f32[4,256,128]{2,1,0:T(8,128)S(1)} slice(f32[4,256,256]{2,1,0:T(8,128)} %bitcast.2), slice={[0:4], [0:256], [0:128]} | slice | bytes 1048576 | tf_op jit(solution)/shard_map/slice | solution.py:342
  1.2 0.3 frames_to_send.2
  1.5 0.8 %collective-permute-start.2 = (f32[4,64,128]{2,1,0:T(8,128)S(1)}, f32[4,64,128]{2,1,0:T(8,128)S(1)}, u32[]{:S(2)}, u32[]{:S(2)}) collective-permute-start(f32[4,64,128]{2,1,0:T(8,128)S(1)} %get-tuple-element.31), channel_id=1, source_target_pairs={{0,16},{32,48},{64,80},{96,112},{128,144},{160,176},{192,208},{224... | collective-permute-start | bytes 393224 | tf_op jit(solution)/shard_map/ppermute | solution.py:20
  2.2 8.4 %collective-permute-start.3 = (f32[4,64,128]{2,1,0:T(8,128)S(1)}, f32[4,64,128]{2,1,0:T(8,128)S(1)}, u32[]{:S(2)}, u32[]{:S(2)}) collective-permute-start(f32[4,64,128]{2,1,0:T(8,128)S(1)} %get-tuple-element.32), channel_id=1, source_target_pairs={{16,32},{48,64},{80,96},{112,128},{144,160},{176,192},{208,224},{3... | collective-permute-start | bytes 393224 | tf_op jit(solution)/shard_map/ppermute | solution.py:20
  10.6 0.0 copy-done
  10.6 0.1 rows_to_send.2
  10.7 0.8 %collective-permute-start = (f32[384,128]{1,0:T(8,128)S(1)}, f32[384,128]{1,0:T(8,128)S(1)}, u32[]{:S(2)}, u32[]{:S(2)}) collective-permute-start(f32[384,128]{1,0:T(8,128)S(1)} %get-tuple-element.29), channel_id=1, source_target_pairs={{0,1},{2,3},{4,5},{6,7},{8,9},{10,11},{12,13},{14,15},{1,0},{3,2},... | collective-permute-start | bytes 589832 | tf_op jit(solution)/shard_map/ppermute | solution.py:20
  11.6 3.5 %collective-permute-start.1 = (f32[384,128]{1,0:T(8,128)S(1)}, f32[384,128]{1,0:T(8,128)S(1)}, u32[]{:S(2)}, u32[]{:S(2)}) collective-permute-start(f32[384,128]{1,0:T(8,128)S(1)} %get-tuple-element.30), channel_id=1, source_target_pairs={{1,2},{3,4},{5,6},{7,8},{9,10},{11,12},{13,14},{2,1},{4,3},{6,5},{... | collective-permute-start | bytes 589832 | tf_op jit(solution)/shard_map/ppermute | solution.py:20
  15.1 0.0 collective-permute-done.2.after_ref.feven_ref
  15.1 1.8 %prepare.2 = (bf16[4,3,256,256]{3,2,1,0:T(8,128)(2,1)S(1)}, bf16[4,3,256,256]{3,2,1,0:T(8,128)(2,1)S(1)}, f32[8,128]{1,0:T(8,128)S(1)}) custom-call(f32[2,3,3,256,256]{4,3,2,1,0:T(8,128)} %w_ref.3, f32[4,64,128]{2,1,0:T(8,128)S(1)} %collective-permute-done.2.after_ref.feven_ref), custom_call_target="tpu_custom_call" | custom-call | tf_op jit(solution)/shard_map/prepare/pallas_call | solution.py:192
  16.9 0.0 collective-permute-done.3.fodd_ref
  17.0 0.1 forward.2
  17.1 4.5 %collective-permute-start.4 = (f32[128,128]{1,0:T(8,128)S(1)}, f32[128,128]{1,0:T(8,128)S(1)}, u32[]{:S(2)}, u32[]{:S(2)}) collective-permute-start(f32[128,128]{1,0:T(8,128)S(1)} %get-tuple-element.34), channel_id=1, source_target_pairs={{1,2},{3,4},{5,6},{7,8},{9,10},{11,12},{13,14},{2,1},{4,3},{6,5},{... | collective-permute-start | bytes 196616 | tf_op jit(solution)/shard_map/ppermute | solution.py:20
  21.6 0.4 collective-permute-start.5
  22.0 2.4 %inner_rows.2 = (f32[2,256,256]{2,1,0:T(8,128)S(1)}, f32[2,256,256]{2,1,0:T(8,128)S(1)}, f32[2,256,256]{2,1,0:T(8,128)S(1)}) custom-call(f32[4,256,256]{2,1,0:T(8,128)S(1)} %bitcast.4, f32[4,64,128]{2,1,0:T(8,128)S(1)} %collective-permute-done.2.after_ref.feven_ref, f32[4,64,128]{2,1,0:T(8,128)S(1)} %collective-permute-done.3.fodd_ref, ...), custom_call_target="tpu_custom_call" | custom-call | tf_op jit(solution)/shard_map/inner_rows/pallas_call | solution.py:258
  24.4 0.5 %collective-permute-done.4.sodd_ref = f32[128,128]{1,0:T(8,128)S(1)} collective-permute-done((f32[128,128]{1,0:T(8,128)S(1)}, f32[128,128]{1,0:T(8,128)S(1)}, u32[]{:S(2)}, u32[]{:S(2)}) %collective-permute-start.4) | collective-permute-done | bytes 65568 | tf_op jit(solution)/shard_map/ppermute | solution.py:20
  24.9 0.6 %collective-permute-done.5.seven_ref = f32[128,128]{1,0:T(8,128)S(1)} collective-permute-done((f32[128,128]{1,0:T(8,128)S(1)}, f32[128,128]{1,0:T(8,128)S(1)}, u32[]{:S(2)}, u32[]{:S(2)}) %collective-permute-start.5) | collective-permute-done | bytes 65568 | tf_op jit(solution)/shard_map/ppermute | solution.py:20
  25.5 0.0 collective-permute-done.reven_ref
  25.5 0.0 collective-permute-done.1.rodd_ref
  25.5 0.9 %outer_rows.2.x_ref = f32[4,256,256]{2,1,0:T(8,128)S(1)} custom-call(f32[384,128]{1,0:T(8,128)S(1)} %collective-permute-done.reven_ref, f32[384,128]{1,0:T(8,128)S(1)} %collective-permute-done.1.rodd_ref, f32[128,128]{1,0:T(8,128)S(1)} %collective-permute-done.4.sodd_ref, f32[128,128]{1,0:T(8,128)S(1)} %collective-permute-done.5.seven_ref, ...), custom_call_target="tpu_custom_call" | custom-call | tf_op jit(solution)/shard_map/outer_rows/pallas_call | solution.py:326
  26.4 0.3 frames_to_send.3
  26.7 0.1 collective-permute-start.8
  26.8 7.4 %collective-permute-start.9 = (f32[4,64,128]{2,1,0:T(8,128)S(1)}, f32[4,64,128]{2,1,0:T(8,128)S(1)}, u32[]{:S(2)}, u32[]{:S(2)}) collective-permute-start(f32[4,64,128]{2,1,0:T(8,128)S(1)} %get-tuple-element.44), channel_id=1, source_target_pairs={{16,32},{48,64},{80,96},{112,128},{144,160},{176,192},{208,224},{3... | collective-permute-start | bytes 393224 | tf_op jit(solution)/shard_map/ppermute | solution.py:20
  34.2 0.1 rows_to_send.3
  34.3 1.4 %collective-permute-start.6 = (f32[384,128]{1,0:T(8,128)S(1)}, f32[384,128]{1,0:T(8,128)S(1)}, u32[]{:S(2)}, u32[]{:S(2)}) collective-permute-start(f32[384,128]{1,0:T(8,128)S(1)} %get-tuple-element.41), channel_id=1, source_target_pairs={{0,1},{2,3},{4,5},{6,7},{8,9},{10,11},{12,13},{14,15},{1,0},{3,2},... | collective-permute-start | bytes 589832 | tf_op jit(solution)/shard_map/ppermute | solution.py:20
  35.7 2.2 %collective-permute-start.7 = (f32[384,128]{1,0:T(8,128)S(1)}, f32[384,128]{1,0:T(8,128)S(1)}, u32[]{:S(2)}, u32[]{:S(2)}) collective-permute-start(f32[384,128]{1,0:T(8,128)S(1)} %get-tuple-element.42), channel_id=1, source_target_pairs={{1,2},{3,4},{5,6},{7,8},{9,10},{11,12},{13,14},{2,1},{4,3},{6,5},{... | collective-permute-start | bytes 589832 | tf_op jit(solution)/shard_map/ppermute | solution.py:20
  37.9 0.0 collective-permute-done.8.after_ref.feven_ref
  37.9 1.8 %prepare.3 = (bf16[4,3,256,256]{3,2,1,0:T(8,128)(2,1)S(1)}, bf16[4,3,256,256]{3,2,1,0:T(8,128)(2,1)S(1)}, f32[8,128]{1,0:T(8,128)S(1)}) custom-call(f32[2,3,3,256,256]{4,3,2,1,0:T(8,128)} %w_ref.3, f32[4,64,128]{2,1,0:T(8,128)S(1)} %collective-permute-done.8.after_ref.feven_ref), custom_call_target="tpu_custom_call" | custom-call | tf_op jit(solution)/shard_map/prepare/pallas_call | solution.py:192
  39.8 0.8 %collective-permute-done.9.fodd_ref = f32[4,64,128]{2,1,0:T(8,128)S(1)} collective-permute-done((f32[4,64,128]{2,1,0:T(8,128)S(1)}, f32[4,64,128]{2,1,0:T(8,128)S(1)}, u32[]{:S(2)}, u32[]{:S(2)}) %collective-permute-start.9) | collective-permute-done | bytes 131104 | tf_op jit(solution)/shard_map/ppermute | solution.py:20
  40.6 0.1 forward.3
  40.7 5.0 %collective-permute-start.10 = (f32[128,128]{1,0:T(8,128)S(1)}, f32[128,128]{1,0:T(8,128)S(1)}, u32[]{:S(2)}, u32[]{:S(2)}) collective-permute-start(f32[128,128]{1,0:T(8,128)S(1)} %get-tuple-element.46), channel_id=1, source_target_pairs={{1,2},{3,4},{5,6},{7,8},{9,10},{11,12},{13,14},{2,1},{4,3},{6,5},{... | collective-permute-start | bytes 196616 | tf_op jit(solution)/shard_map/ppermute | solution.py:20
  45.7 0.1 collective-permute-start.11
  45.8 2.6 %inner_rows.3 = (f32[2,256,256]{2,1,0:T(8,128)S(1)}, f32[2,256,256]{2,1,0:T(8,128)S(1)}, f32[2,256,256]{2,1,0:T(8,128)S(1)}) custom-call(f32[4,256,256]{2,1,0:T(8,128)S(1)} %outer_rows.2.x_ref, f32[4,64,128]{2,1,0:T(8,128)S(1)} %collective-permute-done.8.after_ref.feven_ref, f32[4,64,128]{2,1,0:T(8,128)S(1)} %collective-permute-done.9.fodd_ref, ...), custom_call_target="tpu_custom_call" | custom-call | tf_op jit(solution)/shard_map/inner_rows/pallas_call | solution.py:258
  48.4 0.0 collective-permute-done.10.sodd_ref
  48.4 0.7 %collective-permute-done.11.seven_ref = f32[128,128]{1,0:T(8,128)S(1)} collective-permute-done((f32[128,128]{1,0:T(8,128)S(1)}, f32[128,128]{1,0:T(8,128)S(1)}, u32[]{:S(2)}, u32[]{:S(2)}) %collective-permute-start.11) | collective-permute-done | bytes 65568 | tf_op jit(solution)/shard_map/ppermute | solution.py:20
  49.1 0.0 collective-permute-done.6.reven_ref
  49.1 0.0 collective-permute-done.7.rodd_ref
  49.1 1.6 %outer_rows.3 = f32[4,256,256]{2,1,0:T(8,128)} custom-call(f32[384,128]{1,0:T(8,128)S(1)} %collective-permute-done.6.reven_ref, f32[384,128]{1,0:T(8,128)S(1)} %collective-permute-done.7.rodd_ref, f32[128,128]{1,0:T(8,128)S(1)} %collective-permute-done.10.sodd_ref, f32[128,128]{1,0:T(8,128)S(1)} %collective-permute-done.11.seven_ref, ...), custom_call_target="tpu_custom_call" | custom-call | tf_op jit(solution)/shard_map/outer_rows/pallas_call | solution.py:326
Async XLA Ops:
  0.0 10.6 %copy-start = (f32[1,4,256,256]{3,2,1,0:T(8,128)S(1)}, f32[1,4,256,256]{3,2,1,0:T(8,128)}, u32[]{:S(2)}) copy-start(f32[1,4,256,256]{3,2,1,0:T(8,128)} %param.2) | copy-start | bytes 3145732
  1.5 13.6 %collective-permute-start.2 = (f32[4,64,128]{2,1,0:T(8,128)S(1)}, f32[4,64,128]{2,1,0:T(8,128)S(1)}, u32[]{:S(2)}, u32[]{:S(2)}) collective-permute-start(f32[4,64,128]{2,1,0:T(8,128)S(1)} %get-tuple-element.31), channel_id=1, source_target_pairs={{0,16},{32,48},{64,80},{96,112},{128,144},{160,176},{192,208},{224... | collective-permute-start | bytes 393224 | tf_op jit(solution)/shard_map/ppermute | solution.py:20
  2.2 14.7 %collective-permute-start.3 = (f32[4,64,128]{2,1,0:T(8,128)S(1)}, f32[4,64,128]{2,1,0:T(8,128)S(1)}, u32[]{:S(2)}, u32[]{:S(2)}) collective-permute-start(f32[4,64,128]{2,1,0:T(8,128)S(1)} %get-tuple-element.32), channel_id=1, source_target_pairs={{16,32},{48,64},{80,96},{112,128},{144,160},{176,192},{208,224},{3... | collective-permute-start | bytes 393224 | tf_op jit(solution)/shard_map/ppermute | solution.py:20
  10.7 14.7 %collective-permute-start = (f32[384,128]{1,0:T(8,128)S(1)}, f32[384,128]{1,0:T(8,128)S(1)}, u32[]{:S(2)}, u32[]{:S(2)}) collective-permute-start(f32[384,128]{1,0:T(8,128)S(1)} %get-tuple-element.29), channel_id=1, source_target_pairs={{0,1},{2,3},{4,5},{6,7},{8,9},{10,11},{12,13},{14,15},{1,0},{3,2},... | collective-permute-start | bytes 589832 | tf_op jit(solution)/shard_map/ppermute | solution.py:20
  11.6 13.9 %collective-permute-start.1 = (f32[384,128]{1,0:T(8,128)S(1)}, f32[384,128]{1,0:T(8,128)S(1)}, u32[]{:S(2)}, u32[]{:S(2)}) collective-permute-start(f32[384,128]{1,0:T(8,128)S(1)} %get-tuple-element.30), channel_id=1, source_target_pairs={{1,2},{3,4},{5,6},{7,8},{9,10},{11,12},{13,14},{2,1},{4,3},{6,5},{... | collective-permute-start | bytes 589832 | tf_op jit(solution)/shard_map/ppermute | solution.py:20
  17.1 7.8 %collective-permute-start.4 = (f32[128,128]{1,0:T(8,128)S(1)}, f32[128,128]{1,0:T(8,128)S(1)}, u32[]{:S(2)}, u32[]{:S(2)}) collective-permute-start(f32[128,128]{1,0:T(8,128)S(1)} %get-tuple-element.34), channel_id=1, source_target_pairs={{1,2},{3,4},{5,6},{7,8},{9,10},{11,12},{13,14},{2,1},{4,3},{6,5},{... | collective-permute-start | bytes 196616 | tf_op jit(solution)/shard_map/ppermute | solution.py:20
  21.6 3.9 %collective-permute-start.5 = (f32[128,128]{1,0:T(8,128)S(1)}, f32[128,128]{1,0:T(8,128)S(1)}, u32[]{:S(2)}, u32[]{:S(2)}) collective-permute-start(f32[128,128]{1,0:T(8,128)S(1)} %get-tuple-element.35), channel_id=1, source_target_pairs={{0,1},{2,3},{4,5},{6,7},{8,9},{10,11},{12,13},{14,15},{1,0},{3,2},... | collective-permute-start | bytes 196616 | tf_op jit(solution)/shard_map/ppermute | solution.py:20
  26.7 11.3 %collective-permute-start.8 = (f32[4,64,128]{2,1,0:T(8,128)S(1)}, f32[4,64,128]{2,1,0:T(8,128)S(1)}, u32[]{:S(2)}, u32[]{:S(2)}) collective-permute-start(f32[4,64,128]{2,1,0:T(8,128)S(1)} %get-tuple-element.43), channel_id=1, source_target_pairs={{0,16},{32,48},{64,80},{96,112},{128,144},{160,176},{192,208},{224... | collective-permute-start | bytes 393224 | tf_op jit(solution)/shard_map/ppermute | solution.py:20
  26.8 13.8 %collective-permute-start.9 = (f32[4,64,128]{2,1,0:T(8,128)S(1)}, f32[4,64,128]{2,1,0:T(8,128)S(1)}, u32[]{:S(2)}, u32[]{:S(2)}) collective-permute-start(f32[4,64,128]{2,1,0:T(8,128)S(1)} %get-tuple-element.44), channel_id=1, source_target_pairs={{16,32},{48,64},{80,96},{112,128},{144,160},{176,192},{208,224},{3... | collective-permute-start | bytes 393224 | tf_op jit(solution)/shard_map/ppermute | solution.py:20
  34.3 14.8 %collective-permute-start.6 = (f32[384,128]{1,0:T(8,128)S(1)}, f32[384,128]{1,0:T(8,128)S(1)}, u32[]{:S(2)}, u32[]{:S(2)}) collective-permute-start(f32[384,128]{1,0:T(8,128)S(1)} %get-tuple-element.41), channel_id=1, source_target_pairs={{0,1},{2,3},{4,5},{6,7},{8,9},{10,11},{12,13},{14,15},{1,0},{3,2},... | collective-permute-start | bytes 589832 | tf_op jit(solution)/shard_map/ppermute | solution.py:20
  35.7 13.4 %collective-permute-start.7 = (f32[384,128]{1,0:T(8,128)S(1)}, f32[384,128]{1,0:T(8,128)S(1)}, u32[]{:S(2)}, u32[]{:S(2)}) collective-permute-start(f32[384,128]{1,0:T(8,128)S(1)} %get-tuple-element.42), channel_id=1, source_target_pairs={{1,2},{3,4},{5,6},{7,8},{9,10},{11,12},{13,14},{2,1},{4,3},{6,5},{... | collective-permute-start | bytes 589832 | tf_op jit(solution)/shard_map/ppermute | solution.py:20
  40.7 7.7 %collective-permute-start.10 = (f32[128,128]{1,0:T(8,128)S(1)}, f32[128,128]{1,0:T(8,128)S(1)}, u32[]{:S(2)}, u32[]{:S(2)}) collective-permute-start(f32[128,128]{1,0:T(8,128)S(1)} %get-tuple-element.46), channel_id=1, source_target_pairs={{1,2},{3,4},{5,6},{7,8},{9,10},{11,12},{13,14},{2,1},{4,3},{6,5},{... | collective-permute-start | bytes 196616 | tf_op jit(solution)/shard_map/ppermute | solution.py:20
  45.7 3.4 %collective-permute-start.11 = (f32[128,128]{1,0:T(8,128)S(1)}, f32[128,128]{1,0:T(8,128)S(1)}, u32[]{:S(2)}, u32[]{:S(2)}) collective-permute-start(f32[128,128]{1,0:T(8,128)S(1)} %get-tuple-element.47), channel_id=1, source_target_pairs={{0,1},{2,3},{4,5},{6,7},{8,9},{10,11},{12,13},{14,15},{1,0},{3,2},... | collective-permute-start | bytes 196616 | tf_op jit(solution)/shard_map/ppermute | solution.py:20

commit v6 on v5

--- a/solution.py
+++ b/solution.py
@@ -275,18 +275,27 @@
 
 
 def outer_kernel(
-    fold, reven_ref, rodd_ref, sodd_ref, seven_ref, wh_ref, wl_ref, partial_ref, beside_ref, inner_ref, out_ref, *scratch
+    fold, final, reven_ref, rodd_ref, sodd_ref, seven_ref, wh_ref, wl_ref, partial_ref, beside_ref, inner_ref, out_ref, *rest
 ):
     rows, cols, outs = out_ref.shape
     width = 2 * fold
     edges = (0, rows - 1)
-    if scratch:
-        stage, sems = scratch
+    frame_odd = lax.axis_index("frame") % 2 == 1
+
+    def pack_frames(r, row):
+        to_before, to_following = pack(row[:, :LANES], 0, fold), pack(row[:, :LANES], fold, fold)
+        rest[0][r] = jnp.where(frame_odd, to_before, to_following)
+        rest[1][r] = jnp.where(frame_odd, to_following, to_before)
+
+    if final:
+        stage, sems = rest
         copies = [pltpu.make_async_copy(stage.at[i], out_ref.at[r], sems.at[i]) for i, r in enumerate(edges)]
         copies.append(pltpu.make_async_copy(inner_ref, out_ref.at[1 : rows - 1], sems.at[2]))
         copies[2].start()
     else:
         out_ref[1 : rows - 1] = inner_ref[...]
+        for r in range(1, rows - 1):
+            pack_frames(r, inner_ref[r - 1])
 
     def finish(i, kept_ref, moved_ref):
         halves = LANES // width
@@ -303,11 +312,12 @@
         for dx in range(3):
             total = total + shift_columns(dot3(hi, lo, wh_ref[3 * i, dx], wl_ref[3 * i, dx]), dx)
         total = jnp.maximum(total, 0.0)
-        if scratch:
+        if final:
             stage[i] = total
             copies[i].start()
         else:
             out_ref[edges[i]] = total
+            pack_frames(edges[i], total)
 
     def both(above, below):
         finish(0, *above)
@@ -315,20 +325,23 @@
 
     odd, even = (rodd_ref, sodd_ref), (reven_ref, seven_ref)
     by_parity("row", lambda: both(odd, even), lambda: both(even, odd))
-    if scratch:
+    if final:
         for copy in copies:
             copy.wait()
 
 
-def outer_rows(reven, rodd, sodd, seven, wh, wl, partial, beside, inner, resident):
+def outer_rows(reven, rodd, sodd, seven, wh, wl, partial, beside, inner, final):
     rows, cols, outs = inner.shape
+    fold = outs // 8
+    field = jax.ShapeDtypeStruct((rows + 2, cols, outs), F32)
+    frames = jax.ShapeDtypeStruct((rows + 2, cols * fold // LANES, LANES), F32)
     stage = [pltpu.VMEM((2, cols, outs), F32), pltpu.SemaphoreType.DMA((3,))]
     return pl.pallas_call(
-        functools.partial(outer_kernel, wh.shape[2] // 8),
+        functools.partial(outer_kernel, fold, final),
         in_specs=[VMEM] * 9,
-        out_specs=VMEM if resident else pl.BlockSpec(memory_space=pltpu.HBM),
-        out_shape=jax.ShapeDtypeStruct((rows + 2, cols, outs), F32),
-        scratch_shapes=[] if resident else stage,
+        out_specs=[pl.BlockSpec(memory_space=pltpu.HBM)] if final else [VMEM] * 3,
+        out_shape=[field] if final else [field, frames, frames],
+        scratch_shapes=stage if final else [],
         name="outer_rows",
         compiler_params=PARAMS,
     )(reven, rodd, sodd, seven, wh, wl, partial, beside, inner)
@@ -338,16 +351,19 @@
     frames, rows, cols, chans = features.shape
     layers = conv_weight.shape[0]
     field = features.reshape(rows, cols, chans)
+    to_even, to_odd = frames_to_send(lax.slice_in_dim(field, 0, LANES, axis=2), chans // 8)
     for layer in range(layers):
-        feven, fodd = frames_to_send(field if layer else lax.slice_in_dim(field, 0, LANES, axis=2), chans // 8)
-        feven, fodd = exchange(feven, "frame", 0), exchange(fodd, "frame", 1)
+        feven, fodd = exchange(to_even, "frame", 0), exchange(to_odd, "frame", 1)
         wh, wl, ready = prepare(conv_weight, layer, feven)
         reven, rodd = rows_to_send(field)
         reven, rodd = exchange(reven, "row", 0), exchange(rodd, "row", 1)
         sodd, seven = forward(fodd, feven, ready, cols, chans // 8)
         sodd, seven = exchange(sodd, "row", 1), exchange(seven, "row", 0)
         inner, partial, beside = inner_rows(field, fodd, feven, wh, wl)
-        field = outer_rows(reven, rodd, sodd, seven, wh, wl, partial, beside, inner, layer < layers - 1)
+        last = layer == layers - 1
+        field, *frames_out = outer_rows(reven, rodd, sodd, seven, wh, wl, partial, beside, inner, last)
+        if not last:
+            to_even, to_odd = frames_out
     return field.reshape(features.shape)
 
 

time: 51.2 us -> 51.1 us (level)
  no operation moved by 1% of the time
where the time goes in v6:
time: 51.1 us; the launch traced here: 50.8 us
  starting transfers between devices  34.6 us (68%)
  Pallas kernels  12.1 us (24%)
  waiting for transfers between devices  2.56 us (5%)
  local copies, waits for them, and re-layouts  1.17 us (2%)
    ppermute x12, starting transfers between devices, exchange(): return lax.ppermute(block, axis, pairs + [(b, a) for a, b in pairs])  34.6 us
    pallas_call x2, Pallas kernels, inner_rows(): pl.pallas_call(functools.partial(inner_kernel, chans // 8), in_specs=[VME...  5 us
    pallas_call x2, Pallas kernels, prepare(): pl.pallas_call(functools.partial(prepare_kernel, layer), in_specs=[pl.Blo...  3.68 us
    pallas_call x2, Pallas kernels, outer_rows(): pl.pallas_call(functools.partial(outer_kernel, fold, final), in_specs=[VM...  2.69 us
    ppermute x12, waiting for transfers between devices, exchange(): return lax.ppermute(block, axis, pairs + [(b, a) for a, b in pairs])  2.56 us
    slice x1, local copies, waits for them, and re-layouts, local(): lax.slice_in_dim(field, 0, LANES, axis=2)  1.16 us
  transfers between devices with their start and end apart: 12, of which 4 were waited for; matrix products, arithmetic and copies ran while one was open for 0% of the time, Pallas kernels for 18%

profile of v6, /device:TPU:27, one launch (start us, length us, event | category | flops | bytes accessed | tf_op | source)
XLA Modules:
  0.0 50.8 jit_solution(1123451832458912656)
XLA Ops:
  0.0 0.0 copy-start
  0.0 1.2 %slice.4.x_ref = f32[4,256,128]{2,1,0:T(8,128)S(1)} slice(f32[4,256,256]{2,1,0:T(8,128)} %bitcast.2), slice={[0:4], [0:256], [0:128]} | slice | bytes 1048576 | tf_op jit(solution)/shard_map/slice | solution.py:354
  1.2 0.3 frames_to_send.1
  1.5 0.8 %collective-permute-start.2 = (f32[4,64,128]{2,1,0:T(8,128)S(1)}, f32[4,64,128]{2,1,0:T(8,128)S(1)}, u32[]{:S(2)}, u32[]{:S(2)}) collective-permute-start(f32[4,64,128]{2,1,0:T(8,128)S(1)} %get-tuple-element.32), channel_id=1, source_target_pairs={{0,16},{32,48},{64,80},{96,112},{128,144},{160,176},{192,208},{224... | collective-permute-start | bytes 393224 | tf_op jit(solution)/shard_map/ppermute | solution.py:20
  2.2 8.4 %collective-permute-start.3 = (f32[4,64,128]{2,1,0:T(8,128)S(1)}, f32[4,64,128]{2,1,0:T(8,128)S(1)}, u32[]{:S(2)}, u32[]{:S(2)}) collective-permute-start(f32[4,64,128]{2,1,0:T(8,128)S(1)} %get-tuple-element.33), channel_id=1, source_target_pairs={{16,32},{48,64},{80,96},{112,128},{144,160},{176,192},{208,224},{3... | collective-permute-start | bytes 393224 | tf_op jit(solution)/shard_map/ppermute | solution.py:20
  10.6 0.0 copy-done
  10.6 0.1 rows_to_send.2
  10.7 0.8 %collective-permute-start = (f32[384,128]{1,0:T(8,128)S(1)}, f32[384,128]{1,0:T(8,128)S(1)}, u32[]{:S(2)}, u32[]{:S(2)}) collective-permute-start(f32[384,128]{1,0:T(8,128)S(1)} %get-tuple-element.30), channel_id=1, source_target_pairs={{0,1},{2,3},{4,5},{6,7},{8,9},{10,11},{12,13},{14,15},{1,0},{3,2},... | collective-permute-start | bytes 589832 | tf_op jit(solution)/shard_map/ppermute | solution.py:20
  11.6 3.5 %collective-permute-start.1 = (f32[384,128]{1,0:T(8,128)S(1)}, f32[384,128]{1,0:T(8,128)S(1)}, u32[]{:S(2)}, u32[]{:S(2)}) collective-permute-start(f32[384,128]{1,0:T(8,128)S(1)} %get-tuple-element.31), channel_id=1, source_target_pairs={{1,2},{3,4},{5,6},{7,8},{9,10},{11,12},{13,14},{2,1},{4,3},{6,5},{... | collective-permute-start | bytes 589832 | tf_op jit(solution)/shard_map/ppermute | solution.py:20
  15.1 0.0 collective-permute-done.2.after_ref.feven_ref
  15.1 1.8 %prepare.2 = (bf16[4,3,256,256]{3,2,1,0:T(8,128)(2,1)S(1)}, bf16[4,3,256,256]{3,2,1,0:T(8,128)(2,1)S(1)}, f32[8,128]{1,0:T(8,128)S(1)}) custom-call(f32[2,3,3,256,256]{4,3,2,1,0:T(8,128)} %w_ref.3, f32[4,64,128]{2,1,0:T(8,128)S(1)} %collective-permute-done.2.after_ref.feven_ref), custom_call_target="tpu_custom_call" | custom-call | tf_op jit(solution)/shard_map/prepare/pallas_call | solution.py:192
  16.9 0.0 collective-permute-done.3.fodd_ref
  17.0 0.1 forward.2
  17.1 4.5 %collective-permute-start.4 = (f32[128,128]{1,0:T(8,128)S(1)}, f32[128,128]{1,0:T(8,128)S(1)}, u32[]{:S(2)}, u32[]{:S(2)}) collective-permute-start(f32[128,128]{1,0:T(8,128)S(1)} %get-tuple-element.35), channel_id=1, source_target_pairs={{1,2},{3,4},{5,6},{7,8},{9,10},{11,12},{13,14},{2,1},{4,3},{6,5},{... | collective-permute-start | bytes 196616 | tf_op jit(solution)/shard_map/ppermute | solution.py:20
  21.6 0.4 collective-permute-start.5
  22.0 2.4 %inner_rows.2 = (f32[2,256,256]{2,1,0:T(8,128)S(1)}, f32[2,256,256]{2,1,0:T(8,128)S(1)}, f32[2,256,256]{2,1,0:T(8,128)S(1)}) custom-call(f32[4,256,256]{2,1,0:T(8,128)S(1)} %bitcast.4, f32[4,64,128]{2,1,0:T(8,128)S(1)} %collective-permute-done.2.after_ref.feven_ref, f32[4,64,128]{2,1,0:T(8,128)S(1)} %collective-permute-done.3.fodd_ref, ...), custom_call_target="tpu_custom_call" | custom-call | tf_op jit(solution)/shard_map/inner_rows/pallas_call | solution.py:258
  24.4 0.5 %collective-permute-done.4.sodd_ref = f32[128,128]{1,0:T(8,128)S(1)} collective-permute-done((f32[128,128]{1,0:T(8,128)S(1)}, f32[128,128]{1,0:T(8,128)S(1)}, u32[]{:S(2)}, u32[]{:S(2)}) %collective-permute-start.4) | collective-permute-done | bytes 65568 | tf_op jit(solution)/shard_map/ppermute | solution.py:20
  24.9 0.6 %collective-permute-done.5.seven_ref = f32[128,128]{1,0:T(8,128)S(1)} collective-permute-done((f32[128,128]{1,0:T(8,128)S(1)}, f32[128,128]{1,0:T(8,128)S(1)}, u32[]{:S(2)}, u32[]{:S(2)}) %collective-permute-start.5) | collective-permute-done | bytes 65568 | tf_op jit(solution)/shard_map/ppermute | solution.py:20
  25.5 0.0 collective-permute-done.reven_ref
  25.5 0.0 collective-permute-done.1.rodd_ref
  25.5 1.1 %outer_rows.2 = (f32[4,256,256]{2,1,0:T(8,128)S(1)}, f32[4,64,128]{2,1,0:T(8,128)S(1)}, f32[4,64,128]{2,1,0:T(8,128)S(1)}) custom-call(f32[384,128]{1,0:T(8,128)S(1)} %collective-permute-done.reven_ref, f32[384,128]{1,0:T(8,128)S(1)} %collective-permute-done.1.rodd_ref, f32[128,128]{1,0:T(8,128)S(1)} %collective-permute-done.4.sodd_ref, ...), custom_call_target="tpu_custom_call" | custom-call | tf_op jit(solution)/shard_map/outer_rows/pallas_call | solution.py:339
  26.6 0.1 collective-permute-start.8
  26.7 7.4 %collective-permute-start.9 = (f32[4,64,128]{2,1,0:T(8,128)S(1)}, f32[4,64,128]{2,1,0:T(8,128)S(1)}, u32[]{:S(2)}, u32[]{:S(2)}) collective-permute-start(f32[4,64,128]{2,1,0:T(8,128)S(1)} %get-tuple-element.46), channel_id=1, source_target_pairs={{16,32},{48,64},{80,96},{112,128},{144,160},{176,192},{208,224},{3... | collective-permute-start | bytes 393224 | tf_op jit(solution)/shard_map/ppermute | solution.py:20
  34.1 0.1 rows_to_send.3
  34.2 1.4 %collective-permute-start.6 = (f32[384,128]{1,0:T(8,128)S(1)}, f32[384,128]{1,0:T(8,128)S(1)}, u32[]{:S(2)}, u32[]{:S(2)}) collective-permute-start(f32[384,128]{1,0:T(8,128)S(1)} %get-tuple-element.43), channel_id=1, source_target_pairs={{0,1},{2,3},{4,5},{6,7},{8,9},{10,11},{12,13},{14,15},{1,0},{3,2},... | collective-permute-start | bytes 589832 | tf_op jit(solution)/shard_map/ppermute | solution.py:20
  35.6 2.2 %collective-permute-start.7 = (f32[384,128]{1,0:T(8,128)S(1)}, f32[384,128]{1,0:T(8,128)S(1)}, u32[]{:S(2)}, u32[]{:S(2)}) collective-permute-start(f32[384,128]{1,0:T(8,128)S(1)} %get-tuple-element.44), channel_id=1, source_target_pairs={{1,2},{3,4},{5,6},{7,8},{9,10},{11,12},{13,14},{2,1},{4,3},{6,5},{... | collective-permute-start | bytes 589832 | tf_op jit(solution)/shard_map/ppermute | solution.py:20
  37.9 0.0 collective-permute-done.8.after_ref.feven_ref
  37.9 1.8 %prepare.3 = (bf16[4,3,256,256]{3,2,1,0:T(8,128)(2,1)S(1)}, bf16[4,3,256,256]{3,2,1,0:T(8,128)(2,1)S(1)}, f32[8,128]{1,0:T(8,128)S(1)}) custom-call(f32[2,3,3,256,256]{4,3,2,1,0:T(8,128)} %w_ref.3, f32[4,64,128]{2,1,0:T(8,128)S(1)} %collective-permute-done.8.after_ref.feven_ref), custom_call_target="tpu_custom_call" | custom-call | tf_op jit(solution)/shard_map/prepare/pallas_call | solution.py:192
  39.7 0.8 %collective-permute-done.9.fodd_ref = f32[4,64,128]{2,1,0:T(8,128)S(1)} collective-permute-done((f32[4,64,128]{2,1,0:T(8,128)S(1)}, f32[4,64,128]{2,1,0:T(8,128)S(1)}, u32[]{:S(2)}, u32[]{:S(2)}) %collective-permute-start.9) | collective-permute-done | bytes 131104 | tf_op jit(solution)/shard_map/ppermute | solution.py:20
  40.5 0.1 forward.3
  40.6 5.0 %collective-permute-start.10 = (f32[128,128]{1,0:T(8,128)S(1)}, f32[128,128]{1,0:T(8,128)S(1)}, u32[]{:S(2)}, u32[]{:S(2)}) collective-permute-start(f32[128,128]{1,0:T(8,128)S(1)} %get-tuple-element.48), channel_id=1, source_target_pairs={{1,2},{3,4},{5,6},{7,8},{9,10},{11,12},{13,14},{2,1},{4,3},{6,5},{... | collective-permute-start | bytes 196616 | tf_op jit(solution)/shard_map/ppermute | solution.py:20
  45.6 0.1 collective-permute-start.11
  45.7 2.6 %inner_rows.3 = (f32[2,256,256]{2,1,0:T(8,128)S(1)}, f32[2,256,256]{2,1,0:T(8,128)S(1)}, f32[2,256,256]{2,1,0:T(8,128)S(1)}) custom-call(f32[4,256,256]{2,1,0:T(8,128)S(1)} %get-tuple-element.42.x_ref, f32[4,64,128]{2,1,0:T(8,128)S(1)} %collective-permute-done.8.after_ref.feven_ref, f32[4,64,128]{2,1,0:T(8,128)S(1)} %collective-permute-done.9.fodd_ref, ...), custom_call_target="tpu_custom_call" | custom-call | tf_op jit(solution)/shard_map/inner_rows/pallas_call | solution.py:258
  48.3 0.0 collective-permute-done.6.reven_ref
  48.4 0.0 collective-permute-done.7.rodd_ref
  48.4 0.0 collective-permute-done.10.sodd_ref
  48.4 0.7 %collective-permute-done.11.seven_ref = f32[128,128]{1,0:T(8,128)S(1)} collective-permute-done((f32[128,128]{1,0:T(8,128)S(1)}, f32[128,128]{1,0:T(8,128)S(1)}, u32[]{:S(2)}, u32[]{:S(2)}) %collective-permute-start.11) | collective-permute-done | bytes 65568 | tf_op jit(solution)/shard_map/ppermute | solution.py:20
  49.1 1.6 %outer_rows.3 = f32[4,256,256]{2,1,0:T(8,128)} custom-call(f32[384,128]{1,0:T(8,128)S(1)} %collective-permute-done.6.reven_ref, f32[384,128]{1,0:T(8,128)S(1)} %collective-permute-done.7.rodd_ref, f32[128,128]{1,0:T(8,128)S(1)} %collective-permute-done.10.sodd_ref, f32[128,128]{1,0:T(8,128)S(1)} %collective-permute-done.11.seven_ref, ...), custom_call_target="tpu_custom_call" | custom-call | tf_op jit(solution)/shard_map/outer_rows/pallas_call | solution.py:339
Async XLA Ops:
  0.0 10.6 %copy-start = (f32[1,4,256,256]{3,2,1,0:T(8,128)S(1)}, f32[1,4,256,256]{3,2,1,0:T(8,128)}, u32[]{:S(2)}) copy-start(f32[1,4,256,256]{3,2,1,0:T(8,128)} %param.2) | copy-start | bytes 3145732
  1.5 13.6 %collective-permute-start.2 = (f32[4,64,128]{2,1,0:T(8,128)S(1)}, f32[4,64,128]{2,1,0:T(8,128)S(1)}, u32[]{:S(2)}, u32[]{:S(2)}) collective-permute-start(f32[4,64,128]{2,1,0:T(8,128)S(1)} %get-tuple-element.32), channel_id=1, source_target_pairs={{0,16},{32,48},{64,80},{96,112},{128,144},{160,176},{192,208},{224... | collective-permute-start | bytes 393224 | tf_op jit(solution)/shard_map/ppermute | solution.py:20
  2.2 14.7 %collective-permute-start.3 = (f32[4,64,128]{2,1,0:T(8,128)S(1)}, f32[4,64,128]{2,1,0:T(8,128)S(1)}, u32[]{:S(2)}, u32[]{:S(2)}) collective-permute-start(f32[4,64,128]{2,1,0:T(8,128)S(1)} %get-tuple-element.33), channel_id=1, source_target_pairs={{16,32},{48,64},{80,96},{112,128},{144,160},{176,192},{208,224},{3... | collective-permute-start | bytes 393224 | tf_op jit(solution)/shard_map/ppermute | solution.py:20
  10.7 14.7 %collective-permute-start = (f32[384,128]{1,0:T(8,128)S(1)}, f32[384,128]{1,0:T(8,128)S(1)}, u32[]{:S(2)}, u32[]{:S(2)}) collective-permute-start(f32[384,128]{1,0:T(8,128)S(1)} %get-tuple-element.30), channel_id=1, source_target_pairs={{0,1},{2,3},{4,5},{6,7},{8,9},{10,11},{12,13},{14,15},{1,0},{3,2},... | collective-permute-start | bytes 589832 | tf_op jit(solution)/shard_map/ppermute | solution.py:20
  11.6 13.9 %collective-permute-start.1 = (f32[384,128]{1,0:T(8,128)S(1)}, f32[384,128]{1,0:T(8,128)S(1)}, u32[]{:S(2)}, u32[]{:S(2)}) collective-permute-start(f32[384,128]{1,0:T(8,128)S(1)} %get-tuple-element.31), channel_id=1, source_target_pairs={{1,2},{3,4},{5,6},{7,8},{9,10},{11,12},{13,14},{2,1},{4,3},{6,5},{... | collective-permute-start | bytes 589832 | tf_op jit(solution)/shard_map/ppermute | solution.py:20
  17.1 7.8 %collective-permute-start.4 = (f32[128,128]{1,0:T(8,128)S(1)}, f32[128,128]{1,0:T(8,128)S(1)}, u32[]{:S(2)}, u32[]{:S(2)}) collective-permute-start(f32[128,128]{1,0:T(8,128)S(1)} %get-tuple-element.35), channel_id=1, source_target_pairs={{1,2},{3,4},{5,6},{7,8},{9,10},{11,12},{13,14},{2,1},{4,3},{6,5},{... | collective-permute-start | bytes 196616 | tf_op jit(solution)/shard_map/ppermute | solution.py:20
  21.6 3.9 %collective-permute-start.5 = (f32[128,128]{1,0:T(8,128)S(1)}, f32[128,128]{1,0:T(8,128)S(1)}, u32[]{:S(2)}, u32[]{:S(2)}) collective-permute-start(f32[128,128]{1,0:T(8,128)S(1)} %get-tuple-element.36), channel_id=1, source_target_pairs={{0,1},{2,3},{4,5},{6,7},{8,9},{10,11},{12,13},{14,15},{1,0},{3,2},... | collective-permute-start | bytes 196616 | tf_op jit(solution)/shard_map/ppermute | solution.py:20
  26.6 11.3 %collective-permute-start.8 = (f32[4,64,128]{2,1,0:T(8,128)S(1)}, f32[4,64,128]{2,1,0:T(8,128)S(1)}, u32[]{:S(2)}, u32[]{:S(2)}) collective-permute-start(f32[4,64,128]{2,1,0:T(8,128)S(1)} %get-tuple-element.45), channel_id=1, source_target_pairs={{0,16},{32,48},{64,80},{96,112},{128,144},{160,176},{192,208},{224... | collective-permute-start | bytes 393224 | tf_op jit(solution)/shard_map/ppermute | solution.py:20
  26.7 13.8 %collective-permute-start.9 = (f32[4,64,128]{2,1,0:T(8,128)S(1)}, f32[4,64,128]{2,1,0:T(8,128)S(1)}, u32[]{:S(2)}, u32[]{:S(2)}) collective-permute-start(f32[4,64,128]{2,1,0:T(8,128)S(1)} %get-tuple-element.46), channel_id=1, source_target_pairs={{16,32},{48,64},{80,96},{112,128},{144,160},{176,192},{208,224},{3... | collective-permute-start | bytes 393224 | tf_op jit(solution)/shard_map/ppermute | solution.py:20
  34.2 14.1 %collective-permute-start.6 = (f32[384,128]{1,0:T(8,128)S(1)}, f32[384,128]{1,0:T(8,128)S(1)}, u32[]{:S(2)}, u32[]{:S(2)}) collective-permute-start(f32[384,128]{1,0:T(8,128)S(1)} %get-tuple-element.43), channel_id=1, source_target_pairs={{0,1},{2,3},{4,5},{6,7},{8,9},{10,11},{12,13},{14,15},{1,0},{3,2},... | collective-permute-start | bytes 589832 | tf_op jit(solution)/shard_map/ppermute | solution.py:20
  35.6 12.7 %collective-permute-start.7 = (f32[384,128]{1,0:T(8,128)S(1)}, f32[384,128]{1,0:T(8,128)S(1)}, u32[]{:S(2)}, u32[]{:S(2)}) collective-permute-start(f32[384,128]{1,0:T(8,128)S(1)} %get-tuple-element.44), channel_id=1, source_target_pairs={{1,2},{3,4},{5,6},{7,8},{9,10},{11,12},{13,14},{2,1},{4,3},{6,5},{... | collective-permute-start | bytes 589832 | tf_op jit(solution)/shard_map/ppermute | solution.py:20
  40.6 7.7 %collective-permute-start.10 = (f32[128,128]{1,0:T(8,128)S(1)}, f32[128,128]{1,0:T(8,128)S(1)}, u32[]{:S(2)}, u32[]{:S(2)}) collective-permute-start(f32[128,128]{1,0:T(8,128)S(1)} %get-tuple-element.48), channel_id=1, source_target_pairs={{1,2},{3,4},{5,6},{7,8},{9,10},{11,12},{13,14},{2,1},{4,3},{6,5},{... | collective-permute-start | bytes 196616 | tf_op jit(solution)/shard_map/ppermute | solution.py:20
  45.6 3.4 %collective-permute-start.11 = (f32[128,128]{1,0:T(8,128)S(1)}, f32[128,128]{1,0:T(8,128)S(1)}, u32[]{:S(2)}, u32[]{:S(2)}) collective-permute-start(f32[128,128]{1,0:T(8,128)S(1)} %get-tuple-element.49), channel_id=1, source_target_pairs={{0,1},{2,3},{4,5},{6,7},{8,9},{10,11},{12,13},{14,15},{1,0},{3,2},... | collective-permute-start | bytes 196616 | tf_op jit(solution)/shard_map/ppermute | solution.py:20
